TPU v7x, 32 devices: a whole 2x2x4 slice. The times are simulated.
32 devices in a mesh: expert: 8 (over z, y), tensor: 4 (over x, core).
Axes of the slice: x: 2, y: 2, z: 4, core: 2. Of those that a mesh axis runs over, the one named last changes fastest.
Arguments:
- inputs: bfloat16 [4096, 2048], P('expert'), may hold values from -6 to 6
- cotangent: bfloat16 [4096, 2048], P('expert'), may hold values from -6 to 6
- positions: int32 [4096], P('expert'), may hold values from 0 to 255, as said below
- routes: int32 [4096, 6], P('expert'), may hold values from 0 to 15, as said below
- slot_index: int32 [4096, 6], P('expert'), may hold values from 0 to 256, as said below
- attention_gain: float32 [2048], replicated, may hold values from 0.5 to 1.5
- feedforward_gain: float32 [2048], replicated, may hold values from 0.5 to 1.5
- latent_gain: float32 [512], replicated, may hold values from 0.5 to 1.5
- query_weight: bfloat16 [2048, 3072], P(None, 'tensor'), may hold values from -0.125 to 0.125
- latent_down: bfloat16 [2048, 576], replicated, may hold values from -0.125 to 0.125
- latent_up: bfloat16 [512, 4096], P(None, 'tensor'), may hold values from -0.25 to 0.25
- out_weight: bfloat16 [2048, 2048], P('tensor'), may hold values from -1 to 1
- router_weight: bfloat16 [2048, 16], replicated, may hold values from -0.0625 to 0.0625
- shared_gate: bfloat16 [2048, 2816], P(None, 'tensor'), may hold values from -0.125 to 0.125
- shared_up: bfloat16 [2048, 2816], P(None, 'tensor'), may hold values from -0.125 to 0.125
- shared_down: bfloat16 [2816, 2048], P('tensor'), may hold values from -0.21875 to 0.21875
- expert_gate: bfloat16 [16, 2048, 1408], P('expert', None, 'tensor'), may hold values from -0.125 to 0.125
- expert_up: bfloat16 [16, 2048, 1408], P('expert', None, 'tensor'), may hold values from -0.125 to 0.125
- expert_down: bfloat16 [16, 1408, 2048], P('expert', 'tensor'), may hold values from -0.4375 to 0.4375
Outputs:
- layer_output: bfloat16 [4096, 2048], P('expert')
- grad_input: float32 [4096, 2048], P('expert')
- grad_attention_gain: float32 [2048], P('expert')
- grad_feedforward_gain: float32 [2048], P('expert')
- grad_latent_gain: float32 [512], P('expert')
- grad_query: float32 [2048, 3072], P('expert', 'tensor')
- grad_latent_down: float32 [2048, 576], P('expert')
- grad_latent_up: float32 [512, 4096], P('expert', 'tensor')
- grad_out_weight: float32 [2048, 2048], P('tensor', 'expert')
- grad_router: float32 [2048, 16], P('expert')
- grad_shared_gate: float32 [2048, 2816], P('expert', 'tensor')
- grad_shared_up: float32 [2048, 2816], P('expert', 'tensor')
- grad_shared_down: float32 [2816, 2048], P('tensor', 'expert')
- grad_expert_gate: float32 [16, 2048, 1408], P('expert', None, 'tensor')
- grad_expert_up: float32 [16, 2048, 1408], P('expert', None, 'tensor')
- grad_expert_down: float32 [16, 1408, 2048], P('expert', 'tensor')
Inputs may be any that keep to these rules, and one draw needn't show every extreme that they name: `positions`: each sequence of 512 consecutive rows holds three documents end to end, one of exactly 256 rows; a row's value is its place in its document, counted from 0. `routes`: each row names 6 different experts. `slot_index`: within a sequence, the pairs (row, choice) that name one expert are numbered 0, 1, 2, ... in order of row and then of choice; the value is that number, or 256 where it is 256 or more (the pair is dropped). One expert, the same in every sequence, is named by the first 257 rows of every sequence.
All inputs are finite; a program needn't handle non-finite values.
Results may differ from a plain program's by a relative error of at most 0.023.
Values may be sent and summed in bfloat16 or wider, within the bound.
A program may use at most 320 MiB of HBM per device.

v0:
```python
import math

import jax
import jax.numpy as jnp
from jax import lax
from jax.sharding import PartitionSpec as P

NOPE = 128
ROPE = 64
VD = 128
KVR = 512
TOP = 6


EPSILON = 1e-06


def plain_dot(left_side, right_side):
    return jnp.dot(left_side, right_side, preferred_element_type=jnp.float32)


def lead_dot(left_side, right_side):
    return lax.dot_general(
        left_side, right_side, (((0,), (0,)), ((), ())), preferred_element_type=jnp.float32
    )


def tail_dot(left_side, right_side):
    return lax.dot_general(
        left_side, right_side, (((1,), (1,)), ((), ())), preferred_element_type=jnp.float32
    )


def normalize(values, gain_vector):
    factor = lax.rsqrt(jnp.mean(values * values, axis=-1, keepdims=True) + EPSILON)
    unit_rows = values * factor
    return (unit_rows * gain_vector, unit_rows, factor)


def norm_back(upstream, unit_rows, factor, gain_vector):
    scaled = upstream * gain_vector
    inner_mean = jnp.mean(scaled * unit_rows, axis=-1, keepdims=True)
    return (factor * (scaled - unit_rows * inner_mean), jnp.sum(upstream * unit_rows, axis=0))


def rope_tables(positions):
    half_width = ROPE // 2
    frequency = 10000.0 ** (-2.0 * jnp.arange(half_width, dtype=jnp.float32) / ROPE)
    angles = positions.astype(jnp.float32)[:, None] * frequency[None, :]
    return (jnp.cos(angles), jnp.sin(angles))


def rotate(values, cosine, sine_table):
    half_width = values.shape[-1] // 2
    front_half = values[..., :half_width]
    back_half = values[..., half_width:]
    return jnp.concatenate(
        [
            front_half * cosine - back_half * sine_table,
            back_half * cosine + front_half * sine_table,
        ],
        axis=-1,
    )


def rotate_back(values, cosine, sine_table):
    half_width = values.shape[-1] // 2
    front_half = values[..., :half_width]
    back_half = values[..., half_width:]
    return jnp.concatenate(
        [
            front_half * cosine + back_half * sine_table,
            back_half * cosine - front_half * sine_table,
        ],
        axis=-1,
    )


def visible_mask(first_row, row_starts, row_count, key_count):
    query_index = first_row + jnp.arange(row_count, dtype=jnp.int32)
    key_index = jnp.arange(key_count, dtype=jnp.int32)
    return (key_index[None, :] <= query_index[:, None]) & (
        key_index[None, :] >= row_starts[:, None]
    )


def on_device(
    inputs,
    cotangent,
    positions,
    routes,
    slot_index,
    attention_gain,
    feedforward_gain,
    latent_gain,
    query_weight,
    latent_down,
    latent_up,
    out_weight,
    router_weight,
    shared_gate,
    shared_up,
    shared_down,
    expert_gate,
    expert_up,
    expert_down,
):
    length = inputs.shape[0]
    model_width = inputs.shape[1]
    tensor_count = lax.axis_size("tensor")
    group_count = lax.axis_size("expert")
    head_width = NOPE + ROPE
    local_heads = query_weight.shape[1] // head_width
    local_experts = expert_gate.shape[0]
    experts_all = local_experts * group_count
    capacity = max(
        tensor_count, length * TOP * 4 // (3 * experts_all) // tensor_count * tensor_count
    )
    score_scale = 1.0 / math.sqrt(NOPE + ROPE)
    block_rows = min(512, length)
    block_count = length // block_rows
    rows_in = inputs.astype(jnp.float32)
    normed_one, unit_one, factor_one = normalize(rows_in, attention_gain)
    first_norm = normed_one.astype(jnp.bfloat16)
    cosine, sine_table = rope_tables(positions)
    query_raw = plain_dot(first_norm, query_weight).reshape(length, local_heads, head_width)
    queries = jnp.concatenate(
        [
            query_raw[..., :NOPE],
            rotate(query_raw[..., NOPE:], cosine[:, None], sine_table[:, None]),
        ],
        axis=-1,
    ).astype(jnp.bfloat16)
    latent_raw = plain_dot(first_norm, latent_down)
    latent_normed, unit_latent, factor_latent = normalize(latent_raw[:, :KVR], latent_gain)
    latent = latent_normed.astype(jnp.bfloat16)
    key_rope = rotate(latent_raw[:, KVR:], cosine, sine_table).astype(jnp.bfloat16)
    key_value = (
        plain_dot(latent, latent_up).astype(jnp.bfloat16).reshape(length, local_heads, NOPE + VD)
    )
    key_rows = jnp.concatenate(
        [
            key_value[..., :NOPE],
            jnp.broadcast_to(key_rope[:, None, :], (length, local_heads, ROPE)),
        ],
        axis=-1,
    )
    values = key_value[..., NOPE:]
    row_starts = (jnp.arange(length, dtype=jnp.int32) - positions).reshape(block_count, block_rows)
    first_rows = jnp.arange(block_count, dtype=jnp.int32) * block_rows
    query_blocks = queries.reshape(block_count, block_rows, local_heads, head_width)

    def block_scores(query_block, first_row, starts):
        dispatcher_logit_values = (
            jnp.einsum("qhd,khd->hqk", query_block, key_rows, preferred_element_type=jnp.float32)
            * score_scale
        )
        visible = visible_mask(first_row, starts, block_rows, length)
        return jnp.where(visible[None], dispatcher_logit_values, -jnp.inf)

    def attend(operands):
        query_block, first_row, starts = operands
        dispatcher_logit_values = block_scores(query_block, first_row, starts)
        highest = jnp.max(dispatcher_logit_values, axis=-1, keepdims=True)
        log_total = (
            jnp.log(jnp.sum(jnp.exp(dispatcher_logit_values - highest), axis=-1, keepdims=True))
            + highest
        )
        weights = jnp.exp(dispatcher_logit_values - log_total).astype(jnp.bfloat16)
        outputs = jnp.einsum("hqk,khd->qhd", weights, values, preferred_element_type=jnp.float32)
        return (outputs.astype(jnp.bfloat16), log_total[..., 0])

    head_out, log_totals = lax.map(attend, (query_blocks, first_rows, row_starts))
    head_out = head_out.reshape(length, local_heads * VD)
    attention = lax.psum(plain_dot(head_out, out_weight), "tensor")
    residual = rows_in + attention
    normed_two, unit_two, factor_two = normalize(residual, feedforward_gain)
    second_norm = normed_two.astype(jnp.bfloat16)
    logits = plain_dot(second_norm, router_weight)
    gate_weights = jax.nn.softmax(jnp.take_along_axis(logits, routes, axis=1), axis=-1)
    shared_pre = plain_dot(second_norm, shared_gate)
    shared_lin = plain_dot(second_norm, shared_up)
    shared_hidden = (jax.nn.silu(shared_pre) * shared_lin).astype(jnp.bfloat16)
    branch_part = plain_dot(shared_hidden, shared_down)
    kept_pairs = slot_index < capacity
    places = jnp.where(kept_pairs, routes * capacity + slot_index, experts_all * capacity)
    row_ids = jnp.broadcast_to(jnp.arange(length, dtype=jnp.int32)[:, None], routes.shape)
    sources = (
        jnp.full((experts_all * capacity,), length, jnp.int32)
        .at[places.reshape(-1)]
        .set(row_ids.reshape(-1), mode="drop")
    )
    place_gates = (
        jnp.zeros((experts_all * capacity,), jnp.float32)
        .at[places.reshape(-1)]
        .set(gate_weights.reshape(-1), mode="drop")
    )
    sent_rows = jnp.take(second_norm, sources, axis=0, mode="fill", fill_value=0).reshape(
        group_count, local_experts * capacity, model_width
    )
    arrived = lax.all_to_all(sent_rows, "expert", split_axis=0, concat_axis=0, tiled=True).reshape(
        group_count, local_experts, capacity, model_width
    )
    gate_keep = []
    up_keep = []
    partials = []
    for member in range(local_experts):
        expert_rows = arrived[:, member]
        gate_pre = jnp.einsum(
            "scd,df->scf", expert_rows, expert_gate[member], preferred_element_type=jnp.float32
        )
        up_pre = jnp.einsum(
            "scd,df->scf", expert_rows, expert_up[member], preferred_element_type=jnp.float32
        )
        expert_hidden = (jax.nn.silu(gate_pre) * up_pre).astype(jnp.bfloat16)
        partials.append(
            jnp.einsum(
                "scf,fd->scd",
                expert_hidden,
                expert_down[member],
                preferred_element_type=jnp.float32,
            ).astype(jnp.bfloat16)
        )
        gate_keep.append(gate_pre)
        up_keep.append(up_pre)
    outgoing = jnp.stack(partials, axis=1).reshape(
        group_count, local_experts * capacity, model_width
    )
    returned = lax.all_to_all(outgoing, "expert", split_axis=0, concat_axis=0, tiled=True).reshape(
        experts_all * capacity, model_width
    )
    gate_grads = []
    for member in range(TOP):
        piece_rows = jnp.take(
            returned, places[:, member], axis=0, mode="fill", fill_value=0
        ).astype(jnp.float32)
        branch_part = branch_part + gate_weights[:, member : member + 1] * piece_rows
        gate_grads.append(jnp.sum(cotangent.astype(jnp.float32) * piece_rows, axis=1))
    feedforward = lax.psum(branch_part.astype(jnp.bfloat16), "tensor").astype(jnp.float32)
    result = (residual + feedforward).astype(jnp.bfloat16)
    grad_rows = cotangent.astype(jnp.float32)
    shared_dhidden = tail_dot(cotangent, shared_down)
    grad_shared_down = lead_dot(shared_hidden, cotangent)
    shared_sigmoid = jax.nn.sigmoid(shared_pre)
    shared_dpre = (
        shared_dhidden * shared_lin * shared_sigmoid * (1.0 + shared_pre * (1.0 - shared_sigmoid))
    ).astype(jnp.bfloat16)
    shared_dlin = (shared_dhidden * jax.nn.silu(shared_pre)).astype(jnp.bfloat16)
    grad_shared_gate = lead_dot(second_norm, shared_dpre)
    grad_shared_up = lead_dot(second_norm, shared_dlin)
    grad_second = tail_dot(shared_dpre, shared_gate) + tail_dot(shared_dlin, shared_up)
    grad_sent = (
        (place_gates[:, None] * jnp.take(cotangent, sources, axis=0, mode="fill", fill_value=0))
        .astype(jnp.bfloat16)
        .reshape(group_count, local_experts * capacity, model_width)
    )
    grad_arrived = lax.all_to_all(
        grad_sent, "expert", split_axis=0, concat_axis=0, tiled=True
    ).reshape(group_count, local_experts, capacity, model_width)
    grad_gate_list = []
    grad_up_list = []
    grad_down_list = []
    input_grads = []
    for member in range(local_experts):
        expert_rows = arrived[:, member]
        grad_out_rows = grad_arrived[:, member]
        gate_pre = gate_keep[member]
        up_pre = up_keep[member]
        gate_sigmoid = jax.nn.sigmoid(gate_pre)
        gate_active = jax.nn.silu(gate_pre)
        expert_hidden = (gate_active * up_pre).astype(jnp.bfloat16)
        grad_hidden = jnp.einsum(
            "scd,fd->scf", grad_out_rows, expert_down[member], preferred_element_type=jnp.float32
        )
        grad_down_list.append(
            jnp.einsum(
                "scf,scd->fd", expert_hidden, grad_out_rows, preferred_element_type=jnp.float32
            )
        )
        grad_pre = (
            grad_hidden * up_pre * gate_sigmoid * (1.0 + gate_pre * (1.0 - gate_sigmoid))
        ).astype(jnp.bfloat16)
        grad_lin = (grad_hidden * gate_active).astype(jnp.bfloat16)
        grad_gate_list.append(
            jnp.einsum("scd,scf->df", expert_rows, grad_pre, preferred_element_type=jnp.float32)
        )
        grad_up_list.append(
            jnp.einsum("scd,scf->df", expert_rows, grad_lin, preferred_element_type=jnp.float32)
        )
        input_sum = jnp.einsum(
            "scf,df->scd", grad_pre, expert_gate[member], preferred_element_type=jnp.float32
        ) + jnp.einsum(
            "scf,df->scd", grad_lin, expert_up[member], preferred_element_type=jnp.float32
        )
        input_grads.append(input_sum.astype(jnp.bfloat16))
    grad_outgoing = jnp.stack(input_grads, axis=1).reshape(
        group_count, local_experts * capacity, model_width
    )
    grad_returned = lax.all_to_all(
        grad_outgoing, "expert", split_axis=0, concat_axis=0, tiled=True
    ).reshape(experts_all * capacity, model_width)
    for member in range(TOP):
        grad_second = grad_second + jnp.take(
            grad_returned, places[:, member], axis=0, mode="fill", fill_value=0
        ).astype(jnp.float32)
    grad_second, gate_grad = lax.psum((grad_second, jnp.stack(gate_grads, axis=1)), "tensor")
    selected_grad = gate_weights * (
        gate_grad - jnp.sum(gate_weights * gate_grad, axis=1, keepdims=True)
    )
    expert_ids = jnp.arange(experts_all, dtype=jnp.int32)
    logit_grad = jnp.zeros((length, experts_all), jnp.float32)
    for member in range(TOP):
        logit_grad = logit_grad + jnp.where(
            routes[:, member : member + 1] == expert_ids[None, :],
            selected_grad[:, member : member + 1],
            0.0,
        )
    logit_low = logit_grad.astype(jnp.bfloat16)
    grad_router = lead_dot(second_norm, logit_low)
    grad_second = grad_second + tail_dot(logit_low, router_weight)
    residual_back, grad_feedforward_gain = norm_back(
        grad_second, unit_two, factor_two, feedforward_gain
    )
    grad_residual = grad_rows + residual_back
    attention_grad = grad_residual.astype(jnp.bfloat16)
    grad_out_weight = lead_dot(head_out, attention_grad)
    head_grad = (
        tail_dot(attention_grad, out_weight)
        .astype(jnp.bfloat16)
        .reshape(block_count, block_rows, local_heads, VD)
    )

    def attend_back(running, operands):
        key_grad, value_grad = running
        query_block, head_block, log_block, first_row, starts = operands
        dispatcher_logit_values = block_scores(query_block, first_row, starts)
        weights = jnp.exp(dispatcher_logit_values - log_block[..., None])
        weight_grad = jnp.einsum(
            "qhd,khd->hqk", head_block, values, preferred_element_type=jnp.float32
        )
        score_grad = (
            weights * (weight_grad - jnp.sum(weights * weight_grad, axis=-1, keepdims=True))
        ).astype(jnp.bfloat16)
        query_grad = (
            jnp.einsum("hqk,khd->qhd", score_grad, key_rows, preferred_element_type=jnp.float32)
            * score_scale
        )
        key_grad = (
            key_grad
            + jnp.einsum(
                "hqk,qhd->khd", score_grad, query_block, preferred_element_type=jnp.float32
            )
            * score_scale
        )
        value_grad = value_grad + jnp.einsum(
            "hqk,qhd->khd",
            weights.astype(jnp.bfloat16),
            head_block,
            preferred_element_type=jnp.float32,
        )
        return ((key_grad, value_grad), query_grad)

    start_carry = (
        jnp.zeros((length, local_heads, head_width), jnp.float32),
        jnp.zeros((length, local_heads, VD), jnp.float32),
    )
    (key_grad, value_grad), query_grad = lax.scan(
        attend_back, start_carry, (query_blocks, head_grad, log_totals, first_rows, row_starts)
    )
    query_grad = query_grad.reshape(length, local_heads, head_width)
    query_low = (
        jnp.concatenate(
            [
                query_grad[..., :NOPE],
                rotate_back(query_grad[..., NOPE:], cosine[:, None], sine_table[:, None]),
            ],
            axis=-1,
        )
        .astype(jnp.bfloat16)
        .reshape(length, local_heads * head_width)
    )
    grad_query = lead_dot(first_norm, query_low)
    grad_first = tail_dot(query_low, query_weight)
    keyvalue_low = (
        jnp.concatenate([key_grad[..., :NOPE], value_grad], axis=-1)
        .astype(jnp.bfloat16)
        .reshape(length, local_heads * (NOPE + VD))
    )
    grad_latent_up = lead_dot(latent, keyvalue_low)
    latent_grad = tail_dot(keyvalue_low, latent_up)
    latent_back, grad_latent_gain = norm_back(latent_grad, unit_latent, factor_latent, latent_gain)
    rope_back = rotate_back(jnp.sum(key_grad[..., NOPE:], axis=1), cosine, sine_table)
    down_grad = jnp.concatenate([latent_back, rope_back], axis=1)
    grad_first, down_grad, grad_latent_gain = (
        lax.psum(grad_first.astype(jnp.bfloat16), "tensor").astype(jnp.float32),
        lax.psum(down_grad.astype(jnp.bfloat16), "tensor").astype(jnp.float32),
        lax.psum(grad_latent_gain.astype(jnp.bfloat16), "tensor").astype(jnp.float32),
    )
    down_low = down_grad.astype(jnp.bfloat16)
    grad_latent_down = lead_dot(first_norm, down_low)
    grad_first = grad_first + tail_dot(down_low, latent_down)
    input_back, grad_attention_gain = norm_back(grad_first, unit_one, factor_one, attention_gain)
    grad_input = grad_residual + input_back
    summed = (
        lax.psum_scatter(
            grad_attention_gain.astype(jnp.bfloat16), "expert", scatter_dimension=0, tiled=True
        ).astype(jnp.float32),
        lax.psum_scatter(
            grad_feedforward_gain.astype(jnp.bfloat16), "expert", scatter_dimension=0, tiled=True
        ).astype(jnp.float32),
        lax.psum_scatter(
            grad_latent_gain.astype(jnp.bfloat16), "expert", scatter_dimension=0, tiled=True
        ).astype(jnp.float32),
        lax.psum_scatter(
            grad_query.astype(jnp.bfloat16), "expert", scatter_dimension=0, tiled=True
        ).astype(jnp.float32),
        lax.psum_scatter(
            grad_latent_down.astype(jnp.bfloat16), "expert", scatter_dimension=0, tiled=True
        ).astype(jnp.float32),
        lax.psum_scatter(
            grad_latent_up.astype(jnp.bfloat16), "expert", scatter_dimension=0, tiled=True
        ).astype(jnp.float32),
        lax.psum_scatter(
            grad_out_weight.astype(jnp.bfloat16), "expert", scatter_dimension=1, tiled=True
        ).astype(jnp.float32),
        lax.psum_scatter(
            grad_router.astype(jnp.bfloat16), "expert", scatter_dimension=0, tiled=True
        ).astype(jnp.float32),
        lax.psum_scatter(
            grad_shared_gate.astype(jnp.bfloat16), "expert", scatter_dimension=0, tiled=True
        ).astype(jnp.float32),
        lax.psum_scatter(
            grad_shared_up.astype(jnp.bfloat16), "expert", scatter_dimension=0, tiled=True
        ).astype(jnp.float32),
        lax.psum_scatter(
            grad_shared_down.astype(jnp.bfloat16), "expert", scatter_dimension=1, tiled=True
        ).astype(jnp.float32),
    )
    return (
        result,
        grad_input,
        summed[0],
        summed[1],
        summed[2],
        summed[3],
        summed[4],
        summed[5],
        summed[6],
        summed[7],
        summed[8],
        summed[9],
        summed[10],
        jnp.stack(grad_gate_list),
        jnp.stack(grad_up_list),
        jnp.stack(grad_down_list),
    )


def solution(mesh):
    placed = (
        P("expert", None),
        P("expert", None),
        P("expert"),
        P("expert", None),
        P("expert", None),
        P(),
        P(),
        P(),
        P(None, "tensor"),
        P(),
        P(None, "tensor"),
        P("tensor", None),
        P(),
        P(None, "tensor"),
        P(None, "tensor"),
        P("tensor", None),
        P("expert", None, "tensor"),
        P("expert", None, "tensor"),
        P("expert", "tensor", None),
    )
    return jax.shard_map(
        on_device,
        mesh=mesh,
        in_specs=placed,
        out_specs=(
            P("expert", None),
            P("expert", None),
            P("expert"),
            P("expert"),
            P("expert"),
            P("expert", "tensor"),
            P("expert", None),
            P("expert", "tensor"),
            P("tensor", "expert"),
            P("expert", None),
            P("expert", "tensor"),
            P("expert", "tensor"),
            P("tensor", "expert"),
            P("expert", None, "tensor"),
            P("expert", None, "tensor"),
            P("expert", "tensor", None),
        ),
        check_vma=False,
    )
```

profile of v0, /device:TPU:0, one launch (start us, length us, event | category | flops | bytes accessed | tf_op | source)
XLA Modules:
  0.0 2734.5 jit_solution(1815496612394614610)
XLA Ops:
  37.4 12.0 scatter_custom_fusion
  49.5 74.4 %all-reduce.9.cloned.1.call-done = f32[512,2048]{1,0:T(8,128)} async-done(((f32[512,2048]{1,0:T(8,128)}), f32[512,2048]{1,0:T(8,128)}) %all-reduce.9.cloned.1.call-update) | async-done | bytes 4194320 | tf_op jit(solution)/shard_map/psum | solution.py:175
  131.1 33.2 %gather_fusion.1 = bf16[4096,2048]{1,0:T(8,128)(2,1)} fusion(bf16[512,2048]{1,0:T(8,128)(2,1)} %multiply_convert_fusion.2, s32[4096]{0:T(1024)S(1)} %fusion.101), kind=kCustom, calls=%fused_computation.clone | custom fusion | bytes 33570816 | tf_op jit(solution)/shard_map/jit(_take)/gather | solution.py:198
  164.3 9.0 broadcast_select_fusion
  173.3 368.8 %all_to_all.20 = bf16[8,512,2048]{2,1,0:T(8,128)(2,1)S(1)} all-to-all(bf16[8,512,2048]{2,1,0:T(8,128)(2,1)S(1)} %bitcast.235), channel_id=1, replica_groups=mesh['expert'=8,'tensor'=4] {'expert'}, dimensions={0} | all-to-all | bytes 33554432 | tf_op jit(solution)/shard_map/all_to_all | solution.py:201
  542.2 5.5 fusion.13
  552.4 6.3 multiply_convert_fusion.7
  558.8 6.5 multiply_convert_fusion.8
  565.2 6.3 convert_bitcast_fusion.1
  571.5 5.2 convert_bitcast_fusion
  578.4 6.7 copy.125
  585.1 5.9 all-to-all-start.1
  591.4 33.2 %gather_fusion.8 = bf16[4096,2048]{1,0:T(8,128)(2,1)} fusion(bf16[512,2048]{1,0:T(8,128)(2,1)} %param.24, s32[4096]{0:T(1024)S(1)} %fusion.101), kind=kCustom, calls=%fused_computation.2.clone | custom fusion | bytes 33570816 | tf_op jit(solution)/shard_map/jit(_take)/gather | solution.py:253
  627.0 24.9 gather_fusion
  652.4 300.6 %all-to-all-done.1 = bf16[8,512,2048]{2,1,0:T(8,128)(2,1)} async-done(((bf16[8,512,2048]{2,1,0:T(8,128)(2,1)}), bf16[8,512,2048]{2,1,0:T(8,128)(2,1)}, u32[]{:S(2)}, u32[]{:S(2)}) %all-to-all-start.1) | async-done | bytes 16777248 | tf_op jit(solution)/shard_map/all_to_all | solution.py:229
  952.9 13.2 gather_fusion.7
  966.1 13.3 gather_fusion.6
  979.4 13.2 gather_fusion.5
  992.6 13.1 gather_fusion.4
  1005.7 13.4 gather_fusion.3
  1019.2 13.2 gather_fusion.2
  1032.3 7.3 fusion.37
  1039.6 10.1 psum.52
  1050.7 11.9 scatter_custom_fusion.1
  1062.6 10.0 multiply_convert_fusion
  1072.7 367.2 %all_to_all.21 = bf16[8,512,2048]{2,1,0:T(8,128)(2,1)S(1)} all-to-all(bf16[8,512,2048]{2,1,0:T(8,128)(2,1)S(1)} %bitcast.234), channel_id=1, replica_groups=mesh['expert'=8,'tensor'=4] {'expert'}, dimensions={0} | all-to-all | bytes 33554432 | tf_op jit(solution)/shard_map/all_to_all | solution.py:257
  1439.8 10.2 multiply_convert_fusion.5
  1450.0 8.0 multiply_convert_fusion.3
  1458.1 9.7 fusion.52
  1467.7 8.4 fusion.59
  1476.2 14.7 fusion.1
  1490.8 10.2 fusion
  1501.1 8.0 pad_maximum_fusion.1
  1509.1 6.7 copy.129
  1515.8 5.7 all-to-all-start.3
  1536.6 346.8 %all-to-all-done.3 = bf16[8,512,2048]{2,1,0:T(8,128)(2,1)} async-done(((bf16[8,512,2048]{2,1,0:T(8,128)(2,1)}), bf16[8,512,2048]{2,1,0:T(8,128)(2,1)}, u32[]{:S(2)}, u32[]{:S(2)}) %all-to-all-start.3) | async-done | bytes 16777248 | tf_op jit(solution)/shard_map/all_to_all | solution.py:299
  1883.4 13.6 gather_fusion.14
  1897.0 13.1 gather_fusion.13
  1910.1 13.3 gather_fusion.12
  1923.4 13.2 gather_fusion.11
  1936.6 13.2 gather_fusion.10
  1949.8 13.4 gather_fusion.9
  1963.2 11.5 convert_add_fusion.3
  1995.4 11.4 fusion.24
  2006.9 51.6 %all-reduce.11.cloned.1.call-done = f32[512,2048]{1,0:T(8,128)} async-done(((f32[512,2048]{1,0:T(8,128)}), f32[512,2048]{1,0:T(8,128)}) %all-reduce.11.cloned.1.call-update) | async-done | bytes 4194320 | tf_op jit(solution)/shard_map/psum | solution.py:306
  2058.5 6.6 multiply_reduce_fusion
  2092.9 5.5 convolution_convert_fusion
  2100.9 33.5 %reduce-scatter.21.cloned.1.call-done = bf16[256,704]{0,1:T(8,128)(2,1)} async-done(((bf16[2048,704]{0,1:T(8,128)(2,1)}), bf16[256,704]{0,1:T(8,128)(2,1)}) %reduce-scatter.21.cloned.1.call-update) | async-done | bytes 360464 | tf_op jit(solution)/shard_map/reduce_scatter | solution.py:432
  2136.2 73.6 %reduce-scatter.19.cloned.1.call-done = bf16[256,704]{0,1:T(8,128)(2,1)} async-done(((bf16[2048,704]{0,1:T(8,128)(2,1)}), bf16[256,704]{0,1:T(8,128)(2,1)}) %reduce-scatter.19.cloned.1.call-update) | async-done | bytes 360464 | tf_op jit(solution)/shard_map/reduce_scatter | solution.py:429
  2211.7 73.0 %reduce-scatter.23.cloned.1.call-done = bf16[704,256]{1,0:T(8,128)(2,1)} async-done(((bf16[704,2048]{1,0:T(8,128)(2,1)}), bf16[704,256]{1,0:T(8,128)(2,1)}) %reduce-scatter.23.cloned.1.call-update) | async-done | bytes 360464 | tf_op jit(solution)/shard_map/reduce_scatter | solution.py:435
  2286.6 53.9 %reduce-scatter.17.cloned.1.call-done = bf16[256,16]{0,1:T(8,128)(2,1)} async-done(((bf16[2048,16]{0,1:T(8,128)(2,1)}), bf16[256,16]{0,1:T(8,128)(2,1)}) %reduce-scatter.17.cloned.1.call-update) | async-done | bytes 8208 | tf_op jit(solution)/shard_map/reduce_scatter | solution.py:426
  2341.8 6.1 fusion.43
  2348.0 6.4 fusion.44
  2369.0 69.7 %all-reduce.13.cloned.1.call-done = (bf16[512,2048]{1,0:T(8,128)(2,1)}, bf16[512,2048]{1,0:T(8,128)(2,1)}, bf16[512,576]{0,1:T(8,128)(2,1)}) async-done(((bf16[512,2048]{1,0:T(8,128)(2,1)}, bf16[512,2048]{1,0:T(8,128)(2,1)}, bf16[512,576]{0,1:T(8,128)(2,1)}), (bf16[512,2048]{1,0:T(8,128)(2,1)}, bf16[512,2048]{1,0:T(8,128)(2,1)}, bf16[512,576]{0,1:T(8,128)(2,1)})) %all-reduce.13.cloned.1.call-update) | async-done | bytes 4784144 | tf_op jit(solution)/shard_map/psum | solution.py:239
  2443.5 6.1 fusion.41
  2449.6 5.9 fusion.39
  2458.4 47.7 %reduce-scatter.13.cloned.1.call-done = bf16[64,1024]{1,0:T(8,128)(2,1)} async-done(((bf16[512,1024]{1,0:T(8,128)(2,1)}), bf16[64,1024]{1,0:T(8,128)(2,1)}) %reduce-scatter.13.cloned.1.call-update) | async-done | bytes 131088 | tf_op jit(solution)/shard_map/reduce_scatter | solution.py:420
  2507.7 7.7 fusion.30
  2515.4 20.4 all-reduce.3
  2535.9 6.0 psum.56
  2548.8 5.3 fusion.29
  2554.1 23.0 reduce-scatter.15.cloned.1.call-done
  2579.0 74.9 %reduce-scatter.9.cloned.1.call-done = bf16[256,768]{1,0:T(8,128)(2,1)} async-done(((bf16[2048,768]{1,0:T(8,128)(2,1)}), bf16[256,768]{1,0:T(8,128)(2,1)}) %reduce-scatter.9.cloned.1.call-update) | async-done | bytes 393232 | tf_op jit(solution)/shard_map/reduce_scatter | solution.py:414
  2655.7 70.2 %reduce-scatter.11.cloned.1.call-done = bf16[256,576]{0,1:T(8,128)(2,1)} async-done(((bf16[2048,576]{0,1:T(8,128)(2,1)}), bf16[256,576]{0,1:T(8,128)(2,1)}) %reduce-scatter.11.cloned.1.call-update) | async-done | bytes 294928 | tf_op jit(solution)/shard_map/reduce_scatter | solution.py:417
  (331 shorter events, 155.2 us)
Async XLA Ops:
  7.2 13.9 copy-start
  7.2 116.7 %all-reduce.9.cloned.1.call-start = ((), (), s32[]{:S(2)}) async-start(), calls=%async_computation.12 | async-start | bytes 8388608 | tf_op jit(solution)/shard_map/psum | solution.py:175
  7.3 17.7 copy-start.81
  9.5 11.6 copy-start.79
  10.3 14.7 copy-start.68
  10.4 18.6 copy-start.18
  10.4 5.5 copy-start.77
  10.4 5.5 copy-start.86
  15.9 5.2 copy-start.74
  21.1 5.9 copy-start.28
  36.3 13.1 copy-start.58
  49.4 114.9 %copy-start.64 = (pred[4096]{0:T(1024)(128)(4,1)}, pred[4096]{0:T(1024)(128)(4,1)S(1)}, u32[]{:S(2)}) copy-start(pred[4096]{0:T(1024)(128)(4,1)S(1)} %compare_and_fusion) | copy-start | bytes 12292
  49.5 79.9 %copy-start.60 = (f32[2048]{0:T(1024)S(1)}, f32[2048]{0:T(1024)}, u32[]{:S(2)}) copy-start(f32[2048]{0:T(1024)} %param.29) | copy-start | bytes 24580
  127.4 3.7 copy-start.66
  173.3 368.9 %copy-start.20 = (bf16[2,2048,352]{1,2,0:T(8,128)(2,1)S(1)}, bf16[2,2048,352]{1,2,0:T(8,128)(2,1)}, u32[]{:S(2)}) copy-start(bf16[2,2048,352]{1,2,0:T(8,128)(2,1)} %param.39) | copy-start | bytes 8650756
  542.2 16.6 copy-start.9
  547.6 4.8 copy-start.23
  558.7 6.5 copy-start.83
  565.2 6.3 copy-start.89
  585.1 5.9 copy-start.43
  585.1 367.8 %all-to-all-start.1 = ((bf16[8,512,2048]{2,1,0:T(8,128)(2,1)}), bf16[8,512,2048]{2,1,0:T(8,128)(2,1)}, u32[]{:S(2)}, u32[]{:S(2)}) async-start(bf16[8,512,2048]{2,1,0:T(8,128)(2,1)} %bitcast.232), calls=%async_computation.1 | async-start | bytes 33554432 | tf_op jit(solution)/shard_map/all_to_all | solution.py:229
  591.4 33.2 %copy-start.59 = (s32[512,6]{0,1:T(8,128)S(1)}, s32[512,6]{0,1:T(8,128)}, u32[]{:S(2)}) copy-start(s32[512,6]{0,1:T(8,128)} %copy-done.58) | copy-start | bytes 36868
  591.4 33.4 %copy-start.48 = (bf16[2048,16]{0,1:T(8,128)(2,1)S(1)}, bf16[2048,16]{0,1:T(8,128)(2,1)}, u32[]{:S(2)}) copy-start(bf16[2048,16]{0,1:T(8,128)(2,1)} %param.35) | copy-start | bytes 196612
  1032.3 30.3 %copy-start.65 = (pred[4096]{0:T(1024)(128)(4,1)S(1)}, pred[4096]{0:T(1024)(128)(4,1)}, u32[]{:S(2)}) copy-start(pred[4096]{0:T(1024)(128)(4,1)} %copy-done.64) | copy-start | bytes 12292
  1049.8 22.9 copy-start.52
  1050.4 22.3 copy-start.50
  1072.7 367.2 %copy-start.84 = (bf16[2,352,2048]{2,1,0:T(8,128)(2,1)S(1)}, bf16[2,352,2048]{2,1,0:T(8,128)(2,1)}, u32[]{:S(2)}) copy-start(bf16[2,352,2048]{2,1,0:T(8,128)(2,1)} %param.41) | copy-start | bytes 8650756
  1439.8 10.2 copy-start.10
  1450.0 8.0 copy-start.21
  1458.0 9.7 copy-start.25
  1476.1 14.7 copy-start.24
  1476.1 14.7 copy-start.32
  1515.8 367.7 %all-to-all-start.3 = ((bf16[8,512,2048]{2,1,0:T(8,128)(2,1)}), bf16[8,512,2048]{2,1,0:T(8,128)(2,1)}, u32[]{:S(2)}, u32[]{:S(2)}) async-start(bf16[8,512,2048]{2,1,0:T(8,128)(2,1)} %bitcast.233), calls=%async_computation.3 | async-start | bytes 33554432 | tf_op jit(solution)/shard_map/all_to_all | solution.py:299
  1521.5 537.0 %all-reduce.11.cloned.1.call-start = ((), (), s32[]{:S(2)}) async-start(), calls=%async_computation.13 | async-start | bytes 8388608 | tf_op jit(solution)/shard_map/psum | solution.py:306
  1521.8 4.3 copy-start.3
  1521.8 4.3 copy-start.22
  1974.7 159.6 %reduce-scatter.21.cloned.1.call-start = ((), (), s32[]{:S(2)}) async-start(), calls=%async_computation.20 | async-start | bytes 3244032 | tf_op jit(solution)/shard_map/reduce_scatter | solution.py:432
  1979.9 229.9 %reduce-scatter.19.cloned.1.call-start = ((), (), s32[]{:S(2)}) async-start(), calls=%async_computation.19 | async-start | bytes 3244032 | tf_op jit(solution)/shard_map/reduce_scatter | solution.py:429
  1985.0 299.7 %reduce-scatter.23.cloned.1.call-start = ((), (), s32[]{:S(2)}) async-start(), calls=%async_computation.21 | async-start | bytes 3244032 | tf_op jit(solution)/shard_map/reduce_scatter | solution.py:435
  1990.3 350.2 %reduce-scatter.17.cloned.1.call-start = ((), (), s32[]{:S(2)}) async-start(), calls=%async_computation.18 | async-start | bytes 73728 | tf_op jit(solution)/shard_map/reduce_scatter | solution.py:426
  1995.4 443.4 %all-reduce.13.cloned.1.call-start = ((), (), s32[]{:S(2)}) async-start(), calls=%async_computation.22 | async-start | bytes 9568256 | tf_op jit(solution)/shard_map/psum | solution.py:239
  1995.4 63.1 %copy-start.49 = (bf16[2048,16]{0,1:T(8,128)(2,1)S(1)}, bf16[2048,16]{0,1:T(8,128)(2,1)}, u32[]{:S(2)}) copy-start(bf16[2048,16]{0,1:T(8,128)(2,1)} %param.35) | copy-start | bytes 196612
  1995.4 63.1 %copy-start.61 = (f32[2048]{0:T(1024)S(1)}, f32[2048]{0:T(1024)}, u32[]{:S(2)}) copy-start(f32[2048]{0:T(1024)} %param.29) | copy-start | bytes 24580
  1995.4 63.1 %copy-start.67 = (f32[512]{0:T(512)S(1)}, f32[512]{0:T(512)}, u32[]{:S(2)}) copy-start(f32[512]{0:T(512)} %copy-done.66) | copy-start | bytes 6148
  2058.5 6.6 copy-start.2
  2058.5 6.6 copy-start.5
  2066.7 3.8 copy-start.7
  2066.7 3.8 copy-start.19
  2066.7 3.8 copy-start.63
  2084.1 422.0 %reduce-scatter.13.cloned.1.call-start = ((), (), s32[]{:S(2)}) async-start(), calls=%async_computation.16 | async-start | bytes 1179648 | tf_op jit(solution)/shard_map/reduce_scatter | solution.py:420
  2087.6 5.3 copy-start.75
  2087.6 5.3 copy-start.80
  2087.6 489.6 %reduce-scatter.15.cloned.1.call-start = ((), (), s32[]{:S(2)}) async-start(), calls=%async_computation.17 | async-start | bytes 2359296 | tf_op jit(solution)/shard_map/reduce_scatter | solution.py:423
  2092.8 561.0 %reduce-scatter.9.cloned.1.call-start = ((), (), s32[]{:S(2)}) async-start(), calls=%async_computation.14 | async-start | bytes 3538944 | tf_op jit(solution)/shard_map/reduce_scatter | solution.py:414
  2098.4 627.6 %reduce-scatter.11.cloned.1.call-start = ((), (), s32[]{:S(2)}) async-start(), calls=%async_computation.15 | async-start | bytes 2654208 | tf_op jit(solution)/shard_map/reduce_scatter | solution.py:417
  2341.8 6.1 copy-start.90
  2347.9 9.8 slice-start
  2347.9 9.8 slice-start.1
  2347.9 9.8 slice-start.2
  2354.4 5.0 slice-start.3
  2354.4 5.4 copy-start.26
  2443.5 6.1 copy-start.33
  2543.7 5.1 copy-start.8
  2543.8 5.1 copy-start.12
  (44 other events, 67.4 us)
Sparse Core Ops, SparseCore 0:
  35.7 88.1 all-reduce.8
  1974.8 83.5 all-reduce.10
  2062.1 72.2 reduce-scatter.20
  2138.3 71.4 reduce-scatter.18
  2213.2 71.4 reduce-scatter.22
  2287.7 52.7 reduce-scatter.16
  2344.2 94.4 all-reduce.12
  2442.5 63.5 reduce-scatter.12
  2509.6 67.5 reduce-scatter.14
  2580.6 73.1 reduce-scatter.8
  2657.3 68.5 reduce-scatter.10
where the time goes:
time: 2740 us; the launch traced here: 2730 us
  waiting for transfers between devices  1290 us (47%)
  blocking collectives  773 us (28%)
  local copies, waits for them, and re-layouts  311 us (11%)
  matrix products  242 us (9%)
  other arithmetic  87 us (3%)
    all_to_all x1, blocking collectives, on_device(): lax.all_to_all(sent_rows, 'expert', split_axis=0, concat_axis=0, tiled=True)  369 us
    all_to_all x1, blocking collectives, on_device(): lax.all_to_all(grad_sent, 'expert', split_axis=0, concat_axis=0, tiled=True)  367 us
    all_to_all x1, waiting for transfers between devices, on_device(): lax.all_to_all(grad_outgoing, 'expert', split_axis=0, concat_axis=0, tile...  347 us
    all_to_all x1, waiting for transfers between devices, on_device(): lax.all_to_all(outgoing, 'expert', split_axis=0, concat_axis=0, tiled=True)  301 us
    gather x6, local copies, waits for them, and re-layouts, on_device(): jnp.take(grad_returned, places[:, member], axis=0, mode='fill', fill_valu...  79.7 us
    gather x6, local copies, waits for them, and re-layouts, on_device(): jnp.take(returned, places[:, member], axis=0, mode='fill', fill_value=0)  79.4 us
    reduce_scatter x1, waiting for transfers between devices, on_device(): lax.psum_scatter(grad_query.astype(jnp.bfloat16), 'expert', scatter_dimen...  74.9 us
    psum x1, waiting for transfers between devices, on_device(): attention = lax.psum(plain_dot(head_out, out_weight), 'tensor')  74.4 us
  transfers between devices with their start and end apart: 13, of which 13 were waited for; matrix products, arithmetic and copies ran while one was open for 8% of the time, Pallas kernels for 0%

commit v1 on v0

v1 whole, which is shorter than its diff:
```python
import math

import jax
import jax.numpy as jnp
from jax import lax
from jax.sharding import PartitionSpec as P

NOPE = 128
ROPE = 64
VD = 128
KVR = 512
TOP = 6


EPSILON = 1e-06


def plain_dot(left_side, right_side):
    return jnp.dot(left_side, right_side, preferred_element_type=jnp.float32)


def lead_dot(left_side, right_side):
    return lax.dot_general(
        left_side, right_side, (((0,), (0,)), ((), ())), preferred_element_type=jnp.float32
    )


def tail_dot(left_side, right_side):
    return lax.dot_general(
        left_side, right_side, (((1,), (1,)), ((), ())), preferred_element_type=jnp.float32
    )


def normalize(values, gain_vector):
    factor = lax.rsqrt(jnp.mean(values * values, axis=-1, keepdims=True) + EPSILON)
    unit_rows = values * factor
    return (unit_rows * gain_vector, unit_rows, factor)


def norm_back(upstream, unit_rows, factor, gain_vector):
    scaled = upstream * gain_vector
    inner_mean = jnp.mean(scaled * unit_rows, axis=-1, keepdims=True)
    return (factor * (scaled - unit_rows * inner_mean), jnp.sum(upstream * unit_rows, axis=0))


def rope_tables(positions):
    half_width = ROPE // 2
    frequency = 10000.0 ** (-2.0 * jnp.arange(half_width, dtype=jnp.float32) / ROPE)
    angles = positions.astype(jnp.float32)[:, None] * frequency[None, :]
    return (jnp.cos(angles), jnp.sin(angles))


def rotate(values, cosine, sine_table):
    half_width = values.shape[-1] // 2
    front_half = values[..., :half_width]
    back_half = values[..., half_width:]
    return jnp.concatenate(
        [
            front_half * cosine - back_half * sine_table,
            back_half * cosine + front_half * sine_table,
        ],
        axis=-1,
    )


def rotate_back(values, cosine, sine_table):
    half_width = values.shape[-1] // 2
    front_half = values[..., :half_width]
    back_half = values[..., half_width:]
    return jnp.concatenate(
        [
            front_half * cosine + back_half * sine_table,
            back_half * cosine - front_half * sine_table,
        ],
        axis=-1,
    )


BOTH = ("expert", "tensor")


def visible_mask(positions, length):
    rows = jnp.arange(length, dtype=jnp.int32)
    starts = rows - positions
    return (rows[None, :] <= rows[:, None]) & (rows[None, :] >= starts[:, None])


def gather_rows(rows):
    return lax.all_gather(rows, BOTH, axis=0, tiled=True)


def scatter_rows(rows):
    return lax.psum_scatter(rows, BOTH, scatter_dimension=0, tiled=True)


def expert_table(routes, values, expert_total):
    ids = jnp.arange(expert_total, dtype=jnp.int32)
    table = jnp.zeros((routes.shape[0], expert_total), jnp.float32)
    for member in range(TOP):
        table = table + jnp.where(
            routes[:, member : member + 1] == ids[None, :], values[:, member : member + 1], 0.0
        )
    return table


def on_device(
    inputs,
    cotangent,
    positions,
    routes,
    slot_index,
    attention_gain,
    feedforward_gain,
    latent_gain,
    query_weight,
    latent_down,
    latent_up,
    out_weight,
    router_weight,
    shared_gate,
    shared_up,
    shared_down,
    expert_gate,
    expert_up,
    expert_down,
):
    length, model_width = inputs.shape
    tensor_count = lax.axis_size("tensor")
    group_count = lax.axis_size("expert")
    tensor_index = lax.axis_index("tensor")
    group_index = lax.axis_index("expert")
    head_width = NOPE + ROPE
    local_heads = query_weight.shape[1] // head_width
    local_experts, _, expert_hidden_width = expert_gate.shape
    shared_width = shared_gate.shape[1]
    experts_all = local_experts * group_count
    capacity = max(
        tensor_count, length * TOP * 4 // (3 * experts_all) // tensor_count * tensor_count
    )
    score_scale = 1.0 / math.sqrt(head_width)
    part_rows = length // tensor_count
    part_start = tensor_index * part_rows
    shard_columns = model_width // group_count

    def own_part(rows):
        return lax.dynamic_slice_in_dim(rows, part_start, part_rows, 0)

    def own_sequence(rows):
        return lax.dynamic_slice_in_dim(rows, group_index * length, length, 0)

    def own_columns(rows):
        return lax.dynamic_slice_in_dim(rows, group_index * shard_columns, shard_columns, 1)

    cotangent_all = gather_rows(own_part(cotangent))
    marked = jnp.where(slot_index < capacity, routes, routes + experts_all)
    marked_all = lax.all_gather(marked, "expert", axis=0, tiled=True)

    rows_in = inputs.astype(jnp.float32)
    normed_one, unit_one, factor_one = normalize(rows_in, attention_gain)
    first_norm = normed_one.astype(jnp.bfloat16)
    cosine, sine_table = rope_tables(positions)
    query_raw = plain_dot(first_norm, query_weight).reshape(length, local_heads, head_width)
    queries = jnp.concatenate(
        [
            query_raw[..., :NOPE],
            rotate(query_raw[..., NOPE:], cosine[:, None], sine_table[:, None]),
        ],
        axis=-1,
    ).astype(jnp.bfloat16)
    latent_raw = plain_dot(first_norm, latent_down)
    latent_normed, unit_latent, factor_latent = normalize(latent_raw[:, :KVR], latent_gain)
    latent = latent_normed.astype(jnp.bfloat16)
    key_rope = rotate(latent_raw[:, KVR:], cosine, sine_table).astype(jnp.bfloat16)
    key_value = (
        plain_dot(latent, latent_up).astype(jnp.bfloat16).reshape(length, local_heads, NOPE + VD)
    )
    key_rows = jnp.concatenate(
        [
            key_value[..., :NOPE],
            jnp.broadcast_to(key_rope[:, None, :], (length, local_heads, ROPE)),
        ],
        axis=-1,
    )
    values = key_value[..., NOPE:]
    visible = visible_mask(positions, length)
    scores = jnp.where(
        visible[None],
        jnp.einsum("qhd,khd->hqk", queries, key_rows, preferred_element_type=jnp.float32)
        * score_scale,
        -jnp.inf,
    )
    weights = jax.nn.softmax(scores, axis=-1)
    weights_low = weights.astype(jnp.bfloat16)
    head_out = (
        jnp.einsum("hqk,khd->qhd", weights_low, values, preferred_element_type=jnp.float32)
        .astype(jnp.bfloat16)
        .reshape(length, local_heads * VD)
    )
    attention = lax.psum_scatter(
        plain_dot(head_out, out_weight).astype(jnp.bfloat16),
        "tensor",
        scatter_dimension=0,
        tiled=True,
    ).astype(jnp.float32)
    residual = own_part(rows_in) + attention
    normed_two, unit_two, factor_two = normalize(residual, feedforward_gain)
    second_part = normed_two.astype(jnp.bfloat16)
    second_all = gather_rows(second_part)

    logits_all = plain_dot(second_all, router_weight)
    ones = jnp.ones(marked_all.shape, jnp.float32)
    kept_all = expert_table(marked_all, ones, experts_all)
    named_all = kept_all + expert_table(marked_all - experts_all, ones, experts_all)
    highest = jnp.max(jnp.where(named_all > 0, logits_all, -jnp.inf), axis=1, keepdims=True)
    raised = jnp.where(named_all > 0, jnp.exp(logits_all - highest), 0.0)
    gates_all = raised / jnp.sum(raised, axis=1, keepdims=True)
    kept_gates = gates_all * kept_all
    local_gates = lax.dynamic_slice_in_dim(
        kept_gates, group_index * local_experts, local_experts, 1
    )
    local_kept = lax.dynamic_slice_in_dim(kept_all, group_index * local_experts, local_experts, 1)

    shared_pre = plain_dot(second_all, shared_gate)
    shared_lin = plain_dot(second_all, shared_up)
    shared_sigmoid = jax.nn.sigmoid(shared_pre)
    shared_hidden = (shared_pre * shared_sigmoid * shared_lin).astype(jnp.bfloat16)
    shared_dhidden = tail_dot(cotangent_all, shared_down)
    shared_dpre = (
        shared_dhidden * shared_lin * shared_sigmoid * (1.0 + shared_pre * (1.0 - shared_sigmoid))
    ).astype(jnp.bfloat16)
    shared_dlin = (shared_dhidden * shared_pre * shared_sigmoid).astype(jnp.bfloat16)
    second_columns = own_columns(second_all)
    grad_shared_gate = lead_dot(second_columns, shared_dpre)
    grad_shared_up = lead_dot(second_columns, shared_dlin)
    grad_shared_down = lead_dot(shared_hidden, own_columns(cotangent_all))

    hidden_list = []
    gate_grad_list = []
    grad_gate_list = []
    grad_up_list = []
    grad_down_list = []
    input_grad_list = []
    weight_list = []
    down_rows = expert_down.reshape(local_experts * expert_hidden_width, model_width)
    raw_dhidden = tail_dot(cotangent_all, down_rows)
    for member in range(local_experts):
        gate = local_gates[:, member : member + 1]
        gate_pre = plain_dot(second_all, expert_gate[member])
        up_pre = plain_dot(second_all, expert_up[member])
        sigmoid = jax.nn.sigmoid(gate_pre)
        active = gate_pre * sigmoid
        hidden = active * up_pre
        hidden_low = (gate * hidden).astype(jnp.bfloat16)
        hidden_list.append(hidden_low)
        dhidden = raw_dhidden[
            :, member * expert_hidden_width : (member + 1) * expert_hidden_width
        ]
        gate_grad_list.append(
            local_kept[:, member] * jnp.sum(hidden * dhidden, axis=1)
        )
        dhidden = gate * dhidden
        dpre = (dhidden * up_pre * sigmoid * (1.0 + gate_pre * (1.0 - sigmoid))).astype(
            jnp.bfloat16
        )
        dlin = (dhidden * active).astype(jnp.bfloat16)
        grad_gate_list.append(lead_dot(second_all, dpre))
        grad_up_list.append(lead_dot(second_all, dlin))
        grad_down_list.append(lead_dot(hidden_low, cotangent_all))
        input_grad_list += [dpre, dlin]
        weight_list += [expert_gate[member], expert_up[member]]

    branch = plain_dot(jnp.concatenate(hidden_list, axis=1), down_rows).astype(jnp.bfloat16)
    own_branch = own_sequence(branch) + plain_dot(
        own_sequence(shared_hidden), shared_down
    ).astype(jnp.bfloat16)
    branch = lax.dynamic_update_slice_in_dim(branch, own_branch, group_index * length, 0)
    feedforward = scatter_rows(branch).astype(jnp.float32)
    result_part = (residual + feedforward).astype(jnp.bfloat16)
    result = lax.all_gather(result_part, "tensor", axis=0, tiled=True)

    second_grad = tail_dot(
        jnp.concatenate(input_grad_list, axis=1), jnp.concatenate(weight_list, axis=1)
    ).astype(jnp.bfloat16)
    own_grad = own_sequence(second_grad) + tail_dot(
        jnp.concatenate([own_sequence(shared_dpre), own_sequence(shared_dlin)], axis=1),
        jnp.concatenate([shared_gate, shared_up], axis=1),
    ).astype(jnp.bfloat16)
    second_grad = lax.dynamic_update_slice_in_dim(second_grad, own_grad, group_index * length, 0)
    grad_second = scatter_rows(second_grad).astype(jnp.float32)

    gate_grad_local = jnp.stack(gate_grad_list, axis=1)
    gate_grad = scatter_rows(
        lax.dynamic_update_slice_in_dim(
            jnp.zeros((group_count * length, experts_all), jnp.float32),
            gate_grad_local,
            group_index * local_experts,
            1,
        )
    )
    part_gates = lax.dynamic_slice_in_dim(
        gates_all, group_index * length + part_start, part_rows, 0
    )
    logit_low = (
        part_gates * (gate_grad - jnp.sum(part_gates * gate_grad, axis=1, keepdims=True))
    ).astype(jnp.bfloat16)
    grad_router = lead_dot(second_part, logit_low)
    grad_second = grad_second + tail_dot(logit_low, router_weight)
    residual_back, grad_feedforward_gain = norm_back(
        grad_second, unit_two, factor_two, feedforward_gain
    )
    grad_residual = own_part(cotangent).astype(jnp.float32) + residual_back
    attention_grad = lax.all_gather(
        grad_residual.astype(jnp.bfloat16), "tensor", axis=0, tiled=True
    )
    grad_out_weight = lead_dot(head_out, attention_grad)
    head_grad = (
        tail_dot(attention_grad, out_weight).astype(jnp.bfloat16).reshape(length, local_heads, VD)
    )
    weight_grad = jnp.einsum("qhd,khd->hqk", head_grad, values, preferred_element_type=jnp.float32)
    score_grad = (
        weights * (weight_grad - jnp.sum(weights * weight_grad, axis=-1, keepdims=True))
    ).astype(jnp.bfloat16)
    query_grad = (
        jnp.einsum("hqk,khd->qhd", score_grad, key_rows, preferred_element_type=jnp.float32)
        * score_scale
    )
    key_grad = (
        jnp.einsum("hqk,qhd->khd", score_grad, queries, preferred_element_type=jnp.float32)
        * score_scale
    )
    value_grad = jnp.einsum(
        "hqk,qhd->khd", weights_low, head_grad, preferred_element_type=jnp.float32
    )
    query_low = (
        jnp.concatenate(
            [
                query_grad[..., :NOPE],
                rotate_back(query_grad[..., NOPE:], cosine[:, None], sine_table[:, None]),
            ],
            axis=-1,
        )
        .astype(jnp.bfloat16)
        .reshape(length, local_heads * head_width)
    )
    grad_query = lead_dot(first_norm, query_low)
    keyvalue_low = (
        jnp.concatenate([key_grad[..., :NOPE], value_grad], axis=-1)
        .astype(jnp.bfloat16)
        .reshape(length, local_heads * (NOPE + VD))
    )
    grad_latent_up = lead_dot(latent, keyvalue_low)
    latent_grad = tail_dot(keyvalue_low, latent_up)
    latent_back, grad_latent_gain = norm_back(latent_grad, unit_latent, factor_latent, latent_gain)
    rope_back = rotate_back(jnp.sum(key_grad[..., NOPE:], axis=1), cosine, sine_table)
    down_low = jnp.concatenate([latent_back, rope_back], axis=1).astype(jnp.bfloat16)
    grad_latent_down = lead_dot(first_norm, down_low)
    grad_first = lax.psum_scatter(
        (tail_dot(query_low, query_weight) + tail_dot(down_low, latent_down)).astype(jnp.bfloat16),
        "tensor",
        scatter_dimension=0,
        tiled=True,
    ).astype(jnp.float32)
    input_back, grad_attention_gain = norm_back(
        grad_first, own_part(unit_one), own_part(factor_one), attention_gain
    )
    grad_input = lax.all_gather(
        (grad_residual + input_back).astype(jnp.bfloat16), "tensor", axis=0, tiled=True
    ).astype(jnp.float32)

    pack_columns = latent_down.shape[1] + experts_all
    gains = jnp.concatenate(
        [
            grad_attention_gain.reshape(group_count, -1),
            grad_feedforward_gain.reshape(group_count, -1),
            grad_latent_gain.reshape(group_count, -1),
        ],
        axis=1,
    )
    gain_rows = 16 * tensor_count
    packed = jnp.concatenate(
        [
            jnp.concatenate([grad_latent_down, grad_router], axis=1).reshape(
                group_count, shard_columns, pack_columns
            ),
            jnp.pad(
                gains[:, None, :],
                ((0, 0), (0, gain_rows - 1), (0, pack_columns - gains.shape[1])),
            ),
        ],
        axis=1,
    ).astype(jnp.bfloat16)
    packed = scatter_rows(packed.reshape(-1, pack_columns))
    packed = lax.all_gather(packed, "tensor", axis=0, tiled=True).astype(jnp.float32)
    gain_row = packed[shard_columns]
    gain_cut = model_width // group_count

    def expert_sum(array, dimension):
        return lax.psum_scatter(
            array.astype(jnp.bfloat16), "expert", scatter_dimension=dimension, tiled=True
        ).astype(jnp.float32)

    return (
        result,
        grad_input,
        gain_row[:gain_cut],
        gain_row[gain_cut : 2 * gain_cut],
        gain_row[2 * gain_cut : 2 * gain_cut + KVR // group_count],
        expert_sum(grad_query, 0),
        packed[:shard_columns, : latent_down.shape[1]],
        expert_sum(grad_latent_up, 0),
        expert_sum(grad_out_weight, 1),
        packed[:shard_columns, latent_down.shape[1] :],
        grad_shared_gate,
        grad_shared_up,
        grad_shared_down,
        jnp.stack(grad_gate_list),
        jnp.stack(grad_up_list),
        jnp.stack(grad_down_list),
    )


def solution(mesh):
    placed = (
        P("expert", None),
        P("expert", None),
        P("expert"),
        P("expert", None),
        P("expert", None),
        P(),
        P(),
        P(),
        P(None, "tensor"),
        P(),
        P(None, "tensor"),
        P("tensor", None),
        P(),
        P(None, "tensor"),
        P(None, "tensor"),
        P("tensor", None),
        P("expert", None, "tensor"),
        P("expert", None, "tensor"),
        P("expert", "tensor", None),
    )
    return jax.shard_map(
        on_device,
        mesh=mesh,
        in_specs=placed,
        out_specs=(
            P("expert", None),
            P("expert", None),
            P("expert"),
            P("expert"),
            P("expert"),
            P("expert", "tensor"),
            P("expert", None),
            P("expert", "tensor"),
            P("tensor", "expert"),
            P("expert", None),
            P("expert", "tensor"),
            P("expert", "tensor"),
            P("tensor", "expert"),
            P("expert", None, "tensor"),
            P("expert", None, "tensor"),
            P("expert", "tensor", None),
        ),
        check_vma=False,
    )
```

time: 2740 us -> 1350 us (0.49)
  blocking collectives: 773 us -> 37.7 us
  waiting for transfers between devices: 1290 us -> 860 us
  local copies, waits for them, and re-layouts: 311 us -> 39.6 us
  matrix products: 242 us -> 337 us
  other arithmetic: 87 us -> 52.7 us
    all_to_all x2 -> x0, blocking collectives: 736 us -> none  [the longest x1 369 us: on_device(): lax.all_to_all(sent_rows, 'expert', split_axis=0, concat_axis=0, tiled=True)]
    all_to_all x2 -> x0, waiting for transfers between devices: 647 us -> none  [the longest x1 347 us: on_device(): lax.all_to_all(grad_outgoing, 'expert', split_axis=0, concat_axis=0, tile...]
    gather x19 -> x0, local copies, waits for them, and re-layouts: 251 us -> none  [the longest x6 79.7 us: on_device(): jnp.take(grad_returned, places[:, member], axis=0, mode='fill', fill_valu...]
    reduce_scatter x8 -> x9, waiting for transfers between devices: 450 us -> 665 us  [the longest x4 529 us: scatter_rows(): return lax.psum_scatter(rows, BOTH, scatter_dimension=0, tiled=True)]
    psum x3 -> x0, waiting for transfers between devices: 196 us -> none  [the longest x1 74.4 us: on_device(): attention = lax.psum(plain_dot(head_out, out_weight), 'tensor')]
    all_gather x0 -> x5, waiting for transfers between devices: none -> 195 us  [the longest x2 125 us: gather_rows(): return lax.all_gather(rows, BOTH, axis=0, tiled=True)]
    dot_general x24 -> x6, matrix products: 133 us -> 4.29 us  [the longest x1 0.84 us: on_device(): jnp.einsum('hqk,qhd->khd', score_grad, queries, preferred_element_type=jn...]
    dot_general x8 -> x13, matrix products: 32.4 us -> 146 us  [plain_dot(): return jnp.dot(left_side, right_side, preferred_element_type=jnp.float32)]
  transfers between devices with their start and end apart: 13 -> 14, of which waited for: 13 -> 12; matrix products, arithmetic and copies ran while one was open for 8% -> 23% of each run, Pallas kernels for 0% -> 0%
where the time goes in v1:
time: 1350 us
  waiting for transfers between devices  860 us (64%)
  matrix products  337 us (25%)
  other arithmetic  52.7 us (4%)
  local copies, waits for them, and re-layouts  39.6 us (3%)
  blocking collectives  37.7 us (3%)
  between operations  17.1 us (1%)
    reduce_scatter x4, waiting for transfers between devices, scatter_rows(): return lax.psum_scatter(rows, BOTH, scatter_dimension=0, tiled=True)  529 us
    dot_general x13, matrix products, plain_dot(): return jnp.dot(left_side, right_side, preferred_element_type=jnp.float32)  146 us
    all_gather x2, waiting for transfers between devices, gather_rows(): return lax.all_gather(rows, BOTH, axis=0, tiled=True)  125 us
    reduce_scatter x3, waiting for transfers between devices, expert_sum(): lax.psum_scatter(array.astype(jnp.bfloat16), 'expert', scatter_dimension=...  107 us
    dot_general x14, matrix products, lead_dot(): lax.dot_general(left_side, right_side, (((0,), (0,)), ((), ())), preferre...  97 us
    dot_general x9, matrix products, tail_dot(): lax.dot_general(left_side, right_side, (((1,), (1,)), ((), ())), preferre...  90.4 us
    all_gather x1, blocking collectives, on_device(): marked_all = lax.all_gather(marked, 'expert', axis=0, tiled=True)  31.3 us
    reduce_scatter x1, waiting for transfers between devices, on_device(): lax.psum_scatter(plain_dot(head_out, out_weight).astype(jnp.bfloat16), 't...  28.2 us
  transfers between devices with their start and end apart: 14, of which 12 were waited for; matrix products, arithmetic and copies ran while one was open for 23% of the time, Pallas kernels for 0%

profile of v1, /device:TPU:0, one launch (start us, length us, event | category | flops | bytes accessed | tf_op | source)
XLA Modules:
  0.0 1345.7 jit_solution(11684194114760397046)
XLA Ops:
  8.1 2.2 multiply_reduce_fusion.3
  11.3 3.9 fusion.104
  18.7 2.3 copy.67
  22.1 3.7 fusion.103
  29.6 2.1 fusion.109
  34.9 2.6 convolution_convert_fusion.6
  37.6 1.9 constant_dynamic-slice_fusion.2
  39.6 4.1 convert_element_type.153
  43.7 28.2 %reduce-scatter.10.cloned.1.call-done = bf16[128,2048]{1,0:T(8,128)(2,1)} async-done(((bf16[512,2048]{1,0:T(8,128)(2,1)}), bf16[128,2048]{1,0:T(8,128)(2,1)}) %reduce-scatter.10.cloned.1.call-update) | async-done | bytes 524304 | tf_op jit(solution)/shard_map/reduce_scatter | solution.py:199
  75.6 31.3 %all_gather.21 = s32[4096,6]{0,1:T(8,128)S(1)} all-gather(s32[512,6]{0,1:T(8,128)S(1)} %add_select_fusion), channel_id=1, replica_groups=mesh['expert'=8,'tensor'=4] {'expert'}, dimensions={0}, use_global_device_ids=true | all-gather | bytes 110592 | tf_op jit(solution)/shard_map/all_gather | solution.py:156
  106.9 6.7 slice_bitcast_fusion.2
  113.7 46.0 %all-gather.10.cloned.1.call-done = bf16[4096,2048]{1,0:T(8,128)(2,1)} async-done(((bf16[128,2048]{1,0:T(8,128)(2,1)}), bf16[4096,2048]{1,0:T(8,128)(2,1)}) %all-gather.10.cloned.1.call-update) | async-done | bytes 16777232 | tf_op jit(solution)/shard_map/all_gather | solution.py:89
  159.7 20.5 %fusion.112 = f32[4096,704]{0,1:T(8,128)} fusion(bf16[4096,2048]{1,0:T(8,128)(2,1)} %all-gather.10.cloned.1.call-done, bf16[704,2048]{1,0:T(8,128)(2,1)} %param.34), kind=kOutput, calls=%fused_computation.232 | convolution fusion | flops 11811160064 | bytes 31195136 | tf_op jit(solution)/shard_map/dot_general | solution.py:29
  180.2 16.8 %fusion.111 = f32[4096,704]{0,1:T(8,128)} fusion(bf16[4096,2048]{1,0:T(8,128)(2,1)S(1)} %copy-done.59, bf16[704,2048]{1,0:T(8,128)(2,1)} %bitcast.151), kind=kOutput, calls=%fused_computation.231 | convolution fusion | flops 11811160064 | bytes 31195136 | tf_op jit(solution)/shard_map/dot_general | solution.py:29
  197.0 79.4 %all-gather.6.cloned.1.call-done = bf16[4096,2048]{1,0:T(8,128)(2,1)} async-done(((bf16[128,2048]{1,0:T(8,128)(2,1)}), bf16[4096,2048]{1,0:T(8,128)(2,1)}) %all-gather.6.cloned.1.call-update) | async-done | bytes 16777232 | tf_op jit(solution)/shard_map/all_gather | solution.py:89
  276.4 10.4 select_reduce_fusion
  287.8 8.0 fusion.101
  295.8 7.9 fusion.100
  303.7 7.9 fusion.98
  311.6 26.5 %multiply_reduce_fusion.1 = (f32[4096]{0:T(1024)S(1)}, f32[4096]{0:T(1024)S(1)}, bf16[4096,352]{0,1:T(8,128)(2,1)}, bf16[4096,352]{0,1:T(8,128)(2,1)}, bf16[4096...) fusion(f32[4096,704]{0,1:T(8,128)} %fusion.111, ...), kind=kOutput, calls=%fused_computation.34 | convolution fusion | flops 5960359936 | bytes 64421888 | tf_op jit(solution)/shard_map/dot_general | solution.py:19
  339.1 19.0 %fusion.110 = f32[4096,704]{0,1:T(8,128)} fusion(bf16[4096,2048]{1,0:T(8,128)(2,1)} %all-gather.6.cloned.1.call-done, bf16[2048,704]{0,1:T(8,128)(2,1)} %param.33), kind=kOutput, calls=%fused_computation.230 | convolution fusion | flops 11811160064 | bytes 31195136 | tf_op jit(solution)/shard_map/dot_general | solution.py:19
  358.1 29.2 %multiply_convert_fusion.1 = (bf16[4096,704]{0,1:T(8,128)(2,1)}, bf16[4096,704]{0,1:T(8,128)(2,1)}, bf16[4096,704]{0,1:T(8,128)(2,1)}) fusion(f32[4096,704]{0,1:T(8,128)} %fusion.112, f32[4096,704]{0,1:T(8,128)} %fusion.110, bf16[4096,2048]{1,0:T(8,128)(2,1)} %all-gather.6.cloned.1.call-done, bf16[2048,704]{0,1:T(8,128)(2,1)} %param.32), kind=kOutput, calls=%fused_computation.11 | convolution fusion | flops 11857297408 | bytes 60030976 | tf_op jit(solution)/shard_map/dot_general | solution.py:19
  387.3 2.5 constant_dynamic-slice_fusion
  389.9 33.0 %convolution_convert_fusion = bf16[4096,2048]{1,0:T(8,128)(2,1)} fusion(bf16[4096,352]{0,1:T(8,128)(2,1)} %get-tuple-element.50, bf16[4096,352]{0,1:T(8,128)(2,1)} %get-tuple-element.48, bf16[4096,352]{0,1:T(8,128)(2,1)} %get-tuple-element.49, bf16[4096,352]{0,1:T(8,128)(2,1)} %get-tuple-element.47, bf16[2048,352]{0,1:T(8,128)(2,1)} %get-tuple-element.56, ...), kind=kOutput, calls=%fused_computation.1 | convolution fusion | flops 23699914752 | bytes 34078720 | tf_op jit(solution)/shard_map/dot_general | solution.py:29
  422.8 8.5 fusion.35
  431.5 39.6 %reduce-scatter.16.cloned.1.call-done = f32[128,16]{0,1:T(8,128)} async-done(((f32[4096,16]{0,1:T(8,128)}), f32[128,16]{0,1:T(8,128)}) %reduce-scatter.16.cloned.1.call-update) | async-done | bytes 8208 | tf_op jit(solution)/shard_map/reduce_scatter | solution.py:93
  471.8 180.9 %reduce-scatter.14.cloned.1.call-done = bf16[128,2048]{1,0:T(8,128)(2,1)} async-done(((bf16[4096,2048]{1,0:T(8,128)(2,1)}), bf16[128,2048]{1,0:T(8,128)(2,1)}) %reduce-scatter.14.cloned.1.call-update) | async-done | bytes 524304 | tf_op jit(solution)/shard_map/reduce_scatter | solution.py:93
  652.7 1.9 multiply_reduce_fusion.5
  655.6 2.5 fusion.102
  658.6 23.3 %all-gather.12.cloned.1.call-done = bf16[512,2048]{1,0:T(8,128)(2,1)} async-done(((bf16[128,2048]{1,0:T(8,128)(2,1)}), bf16[512,2048]{1,0:T(8,128)(2,1)}) %all-gather.12.cloned.1.call-update) | async-done | bytes 2097168 | tf_op jit(solution)/shard_map/all_gather | solution.py:312
  681.9 3.6 convolution_convert_fusion.10
  696.2 3.3 add_convert_fusion
  699.8 19.7 %convolution_convert_fusion.1 = bf16[4096,2048]{1,0:T(8,128)(2,1)} fusion(bf16[704,2048]{1,0:T(8,128)(2,1)} %bitcast.152, bf16[4096,352]{0,1:T(8,128)(2,1)} %get-tuple-element.51, bf16[4096,352]{0,1:T(8,128)(2,1)} %get-tuple-element.52), kind=kOutput, calls=%fused_computation.2 | convolution fusion | flops 11831083008 | bytes 25427968 | tf_op jit(solution)/shard_map/dot_general | solution.py:19
  719.5 5.0 fusion.31
  724.6 3.3 convolution_convert_fusion.8
  728.0 4.4 convolution_convert_fusion.4
  732.5 5.5 convolution_convert_fusion.2
  738.6 4.2 broadcast_multiply_fusion
  744.5 171.7 %reduce-scatter.12.cloned.1.call-done = bf16[128,2048]{1,0:T(8,128)(2,1)} async-done(((bf16[4096,2048]{1,0:T(8,128)(2,1)}), bf16[128,2048]{1,0:T(8,128)(2,1)}) %reduce-scatter.12.cloned.1.call-update) | async-done | bytes 524304 | tf_op jit(solution)/shard_map/reduce_scatter | solution.py:93
  916.2 3.7 fusion.56
  920.0 11.6 convolution_bitcast_fusion.3
  931.7 11.8 convolution_bitcast_fusion.2
  943.5 11.4 convolution_bitcast_fusion.4
  955.9 3.3 convolution_convert_fusion.3
  960.8 4.3 copy.66
  965.2 3.9 fusion.25
  969.1 10.8 convolution_bitcast_fusion.5
  979.9 3.3 pad_maximum_fusion.2
  983.2 10.8 convolution_bitcast_fusion.1
  994.1 8.3 convolution_bitcast_fusion
  1002.4 4.8 pad_maximum_fusion
  1007.2 5.5 fusion.43
  1012.7 5.4 fusion.45
  1018.0 4.2 fusion.38
  1023.8 31.7 %reduce-scatter.26.cloned.1.call-done = bf16[512,256]{1,0:T(8,128)(2,1)} async-done(((bf16[512,2048]{1,0:T(8,128)(2,1)}), bf16[512,256]{1,0:T(8,128)(2,1)}) %reduce-scatter.26.cloned.1.call-update) | async-done | bytes 262160 | tf_op jit(solution)/shard_map/reduce_scatter | solution.py:398
  1057.3 75.4 %reduce-scatter.22.cloned.1.call-done = bf16[256,768]{1,0:T(8,128)(2,1)} async-done(((bf16[2048,768]{1,0:T(8,128)(2,1)}), bf16[256,768]{1,0:T(8,128)(2,1)}) %reduce-scatter.22.cloned.1.call-update) | async-done | bytes 393232 | tf_op jit(solution)/shard_map/reduce_scatter | solution.py:398
  1132.7 1.9 convert_element_type.194
  1134.6 21.4 %all-gather.8.cloned.1.call-done = bf16[512,2048]{1,0:T(8,128)(2,1)} async-done(((bf16[128,2048]{1,0:T(8,128)(2,1)}), bf16[512,2048]{1,0:T(8,128)(2,1)}) %all-gather.8.cloned.1.call-update) | async-done | bytes 2097168 | tf_op jit(solution)/shard_map/all_gather | solution.py:279
  1155.9 24.8 %all-gather.14.cloned.1.call-done = bf16[512,2048]{1,0:T(8,128)(2,1)} async-done(((bf16[128,2048]{1,0:T(8,128)(2,1)}), bf16[512,2048]{1,0:T(8,128)(2,1)}) %all-gather.14.cloned.1.call-update) | async-done | bytes 2097168 | tf_op jit(solution)/shard_map/all_gather | solution.py:366
  1180.7 4.1 convert_element_type.190
  1184.8 137.1 %reduce-scatter.20.cloned.1.call-done = bf16[80,592]{1,0:T(8,128)(2,1)} async-done(((bf16[2560,592]{1,0:T(8,128)(2,1)}), bf16[80,592]{1,0:T(8,128)(2,1)}) %reduce-scatter.20.cloned.1.call-update) | async-done | bytes 94736 | tf_op jit(solution)/shard_map/reduce_scatter | solution.py:93
  1321.9 6.4 all_gather.27
  1331.5 2.1 copy.57
  1334.8 3.2 copy.73
  (243 shorter events, 43.9 us)
Async XLA Ops:
  8.0 14.0 %copy-start = (bf16[2048,768]{1,0:T(8,128)(2,1)S(1)}, bf16[2048,768]{1,0:T(8,128)(2,1)}, u32[]{:S(2)}) copy-start(bf16[2048,768]{1,0:T(8,128)(2,1)} %param.27) | copy-start | bytes 9437188
  8.0 63.9 %reduce-scatter.10.cloned.1.call-start = ((), (), s32[]{:S(2)}) async-start(), calls=%async_computation.9 | async-start | bytes 2621440 | tf_op jit(solution)/shard_map/reduce_scatter | solution.py:199
  8.1 17.8 %copy-start.57 = (f32[32]{0:T(128)}, f32[32]{0:T(128)S(1)}, u32[]{:S(2)}) copy-start(f32[32]{0:T(128)S(1)} %multiply_power_fusion) | copy-start | bytes 388
  10.3 11.7 copy-start.53
  11.1 14.8 %copy-start.43 = (f32[512]{0:T(512)}, f32[512]{0:T(512)S(1)}, u32[]{:S(2)}) copy-start(f32[512]{0:T(512)S(1)} %get-tuple-element.91) | copy-start | bytes 6148
  11.2 5.6 copy-start.55
  11.3 5.6 copy-start.62
  15.2 6.9 copy-start.41
  22.1 6.0 copy-start.7
  25.9 2.2 copy-start.22
  29.6 2.2 copy-start.20
  31.8 2.1 copy-start.9
  31.8 2.1 copy-start.49
  31.8 3.1 copy-start.61
  37.6 122.2 %all-gather.10.cloned.1.call-start = ((), (), s32[]{:S(2)}) async-start(), calls=%async_computation.13 | async-start | bytes 17301504 | tf_op jit(solution)/shard_map/all_gather | solution.py:89
  39.5 35.0 %copy-start.38 = (f32[2048]{0:T(1024)S(1)}, f32[2048]{0:T(1024)}, u32[]{:S(2)}) copy-start(f32[2048]{0:T(1024)} %param.25) | copy-start | bytes 24580
  39.5 36.0 %copy-start.47 = (s32[512,6]{0,1:T(8,128)S(1)}, s32[512,6]{0,1:T(8,128)}, u32[]{:S(2)}) copy-start(s32[512,6]{0,1:T(8,128)} %param.22) | copy-start | bytes 36868
  39.5 36.0 %copy-start.48 = (s32[512,6]{0,1:T(8,128)S(1)}, s32[512,6]{0,1:T(8,128)}, u32[]{:S(2)}) copy-start(s32[512,6]{0,1:T(8,128)} %param.23) | copy-start | bytes 36868
  39.6 236.9 %all-gather.6.cloned.1.call-start = ((), (), s32[]{:S(2)}) async-start(), calls=%async_computation.10 | async-start | bytes 17301504 | tf_op jit(solution)/shard_map/all_gather | solution.py:89
  75.5 395.6 %reduce-scatter.16.cloned.1.call-start = ((), (), s32[]{:S(2)}) async-start(), calls=%async_computation.15 | async-start | bytes 270336 | tf_op jit(solution)/shard_map/reduce_scatter | solution.py:93
  159.7 20.5 %copy-start.59 = (bf16[4096,2048]{1,0:T(8,128)(2,1)S(1)}, bf16[4096,2048]{1,0:T(8,128)(2,1)}, u32[]{:S(2)}) copy-start(bf16[4096,2048]{1,0:T(8,128)(2,1)} %all-gather.10.cloned.1.call-done) | copy-start | bytes 50331652
  180.2 96.2 %copy-start.36 = (bf16[2048,16]{0,1:T(8,128)(2,1)S(1)}, bf16[2048,16]{0,1:T(8,128)(2,1)}, u32[]{:S(2)}) copy-start(bf16[2048,16]{0,1:T(8,128)(2,1)} %param.31) | copy-start | bytes 196612
  276.4 11.4 copy-start.2
  276.4 11.4 copy-start.14
  287.8 8.0 copy-start.13
  339.1 313.6 %reduce-scatter.14.cloned.1.call-start = ((), (), s32[]{:S(2)}) async-start(), calls=%async_computation.14 | async-start | bytes 17301504 | tf_op jit(solution)/shard_map/reduce_scatter | solution.py:93
  431.4 221.3 %copy-start.37 = (bf16[2048,16]{0,1:T(8,128)(2,1)S(1)}, bf16[2048,16]{0,1:T(8,128)(2,1)}, u32[]{:S(2)}) copy-start(bf16[2048,16]{0,1:T(8,128)(2,1)} %param.31) | copy-start | bytes 196612
  431.4 221.3 %copy-start.39 = (f32[2048]{0:T(1024)S(1)}, f32[2048]{0:T(1024)}, u32[]{:S(2)}) copy-start(f32[2048]{0:T(1024)} %param.25) | copy-start | bytes 24580
  431.4 221.3 %copy-start.52 = (f32[128]{0:T(128)S(1)}, f32[128]{0:T(128)}, u32[]{:S(2)}) copy-start(f32[128]{0:T(128)} %copy-done.51) | copy-start | bytes 1540
  431.4 250.5 %all-gather.12.cloned.1.call-start = ((), (), s32[]{:S(2)}) async-start(), calls=%async_computation.16 | async-start | bytes 2621440 | tf_op jit(solution)/shard_map/all_gather | solution.py:312
  658.1 27.4 %copy-start.50 = (f32[4,512]{1,0:T(4,128)S(1)}, f32[4,512]{1,0:T(4,128)}, u32[]{:S(2)}) copy-start(f32[4,512]{1,0:T(4,128)} %copy-done.49) | copy-start | bytes 24580
  658.1 84.7 %reduce-scatter.18.cloned.1.call-start = ((), (), s32[]{:S(2)}) async-start(), calls=%async_computation.17 | async-start | bytes 2621440 | tf_op jit(solution)/shard_map/reduce_scatter | solution.py:357
  681.9 3.7 copy-start.10
  685.6 1.2 copy-start.21
  687.6 1.2 copy-start.23
  689.9 2.4 copy-start.5
  689.9 2.4 copy-start.46
  690.0 2.4 copy-start.56
  690.0 2.4 copy-start.63
  693.3 1.9 copy-start.25
  693.3 2.9 copy-start.60
  699.6 216.7 %reduce-scatter.12.cloned.1.call-start = ((), (), s32[]{:S(2)}) async-start(), calls=%async_computation.11 | async-start | bytes 17301504 | tf_op jit(solution)/shard_map/reduce_scatter | solution.py:93
  699.8 19.7 %copy-start.12 = (bf16[704,2048]{1,0:T(8,128)(2,1)S(1)}, bf16[704,2048]{1,0:T(8,128)(2,1)}, u32[]{:S(2)}) copy-start(bf16[704,2048]{1,0:T(8,128)(2,1)} %param.34) | copy-start | bytes 8650756
  724.5 297.7 %reduce-scatter.24.cloned.1.call-start = ((), (), s32[]{:S(2)}) async-start(), calls=%async_computation.21 | async-start | bytes 1179648 | tf_op jit(solution)/shard_map/reduce_scatter | solution.py:398
  727.9 4.6 copy-start.42
  727.9 4.6 copy-start.54
  727.9 327.6 %reduce-scatter.26.cloned.1.call-start = ((), (), s32[]{:S(2)}) async-start(), calls=%async_computation.22 | async-start | bytes 2359296 | tf_op jit(solution)/shard_map/reduce_scatter | solution.py:398
  732.4 400.3 %reduce-scatter.22.cloned.1.call-start = ((), (), s32[]{:S(2)}) async-start(), calls=%async_computation.20 | async-start | bytes 3538944 | tf_op jit(solution)/shard_map/reduce_scatter | solution.py:398
  738.0 417.9 %all-gather.8.cloned.1.call-start = ((), (), s32[]{:S(2)}) async-start(), calls=%async_computation.12 | async-start | bytes 2621440 | tf_op jit(solution)/shard_map/all_gather | solution.py:279
  920.0 260.7 %all-gather.14.cloned.1.call-start = ((), (), s32[]{:S(2)}) async-start(), calls=%async_computation.18 | async-start | bytes 2621440 | tf_op jit(solution)/shard_map/all_gather | solution.py:366
  931.7 390.2 %reduce-scatter.20.cloned.1.call-start = ((), (), s32[]{:S(2)}) async-start(), calls=%async_computation.19 | async-start | bytes 3379200 | tf_op jit(solution)/shard_map/reduce_scatter | solution.py:93
  931.7 11.8 copy-start.66
  943.5 11.4 copy-start.6
  943.5 11.4 copy-start.40
  969.0 10.8 copy-start.17
  979.8 3.4 copy-start.65
  979.9 14.1 %slice-start = ((s8[16777216]{0:T(1024)(128)(4,1)}), s8[4194304]{0:T(1024)(128)(4,1)S(1)}, s32[]{:S(2)}) async-start(s8[16777216]{0:T(1024)(128)(4,1)} %bitcast.118), calls=%async_computation.23 | async-start | bytes 8388608
  983.2 10.8 slice-start.1
  983.2 10.8 slice-start.2
  983.2 10.8 slice-start.3
  994.0 8.3 copy-start.15
  994.0 8.3 copy-start.16
  1007.2 10.9 slice-start.4
  1012.7 5.4 slice-start.5
  (23 other events, 20.3 us)
Sparse Core Ops, SparseCore 0:
  37.7 34.2 reduce-scatter.9
  658.3 23.5 all-gather.11
  699.7 31.4 reduce-scatter.17
  733.4 182.8 reduce-scatter.11
  919.9 65.1 reduce-scatter.23
  988.5 66.9 reduce-scatter.25
  1059.1 73.5 reduce-scatter.21
  1134.2 21.6 all-gather.7
  1158.1 22.5 all-gather.13
  1182.8 139.0 reduce-scatter.19
Sparse Core Ops, SparseCore 1:
  41.9 117.8 all-gather.9
  163.4 112.9 all-gather.5
  339.1 131.9 reduce-scatter.15
  473.4 179.2 reduce-scatter.13

commit v2 on v1

--- a/solution.py
+++ b/solution.py
@@ -1,8 +1,11 @@
+import functools
 import math
 
 import jax
 import jax.numpy as jnp
 from jax import lax
+from jax.experimental import pallas as pl
+from jax.experimental.pallas import tpu as pltpu
 from jax.sharding import PartitionSpec as P
 
 NOPE = 128
@@ -101,6 +104,597 @@
             routes[:, member : member + 1] == ids[None, :], values[:, member : member + 1], 0.0
         )
     return table
+
+
+MESH = pl.DeviceIdType.MESH
+LANES = 128
+
+
+def expert_kernel(
+    part_ref,
+    cotangent_ref,
+    code_ref,
+    gate_ref,
+    up_ref,
+    down_ref,
+    shared_gate_ref,
+    shared_up_ref,
+    shared_down_ref,
+    router_ref,
+    rows_ref,
+    branch_ref,
+    hidden_ref,
+    dhidden_ref,
+    shared_hidden_ref,
+    shared_dhidden_ref,
+    grad_ref,
+    gate_w,
+    up_w,
+    down_w,
+    shared_gate_w,
+    shared_up_w,
+    shared_down_w,
+    router_w,
+    rows_buf,
+    cotangent_buf,
+    code_buf,
+    gates_buf,
+    kept_buf,
+    gate_grad_buf,
+    hidden_buf,
+    dhidden_buf,
+    shared_hidden_buf,
+    shared_dhidden_buf,
+    branch_buf,
+    grad_buf,
+    core_land,
+    side_send,
+    side_keep,
+    side_land,
+    owner_send,
+    owner_land,
+    weight_sem,
+    own_sem,
+    load_sem,
+    store_sem,
+    spread_send_sem,
+    side_spread_sem,
+    core_spread_sem,
+    arrive_sem,
+    core_sem,
+    core_land_sem,
+    side_sem,
+    side_land_sem,
+    owner_sem,
+    owner_land_sem,
+    *,
+    groups,
+    tensors,
+):
+    sides = tensors // 2
+    length = rows_buf.shape[1]
+    part_rows = length // tensors
+    width = rows_buf.shape[2]
+    local_experts = gate_w.shape[0]
+    me = lax.axis_index("expert")
+    mine = lax.axis_index("tensor")
+    side = mine // 2
+    core = mine % 2
+    sibling = side * 2 + (1 - core)
+
+    def tensor_of(shift):
+        return ((side + shift) % sides) * 2 + core
+
+    weight_pairs = (
+        (gate_ref, gate_w),
+        (up_ref, up_w),
+        (down_ref, down_w),
+        (shared_gate_ref, shared_gate_w),
+        (shared_up_ref, shared_up_w),
+        (shared_down_ref, shared_down_w),
+        (router_ref, router_w),
+    )
+
+    def weight_copy(index):
+        return pltpu.make_async_copy(
+            weight_pairs[index][0], weight_pairs[index][1], weight_sem.at[index]
+        )
+
+    def sequence_of(step):
+        return (me + step) % groups
+
+    def load_copies(step):
+        slot = step % 2
+        sequence = sequence_of(step)
+        return (
+            pltpu.make_async_copy(
+                rows_ref.at[sequence], rows_buf.at[slot], load_sem.at[slot, 0]
+            ),
+            pltpu.make_async_copy(
+                cotangent_ref.at[sequence], cotangent_buf.at[slot], load_sem.at[slot, 1]
+            ),
+            pltpu.make_async_copy(
+                code_ref.at[sequence], code_buf.at[slot], load_sem.at[slot, 2]
+            ),
+        )
+
+    def store_copies(step):
+        sequence = sequence_of(step)
+        return (
+            pltpu.make_async_copy(hidden_buf, hidden_ref.at[:, sequence], store_sem.at[0]),
+            pltpu.make_async_copy(dhidden_buf, dhidden_ref.at[:, sequence], store_sem.at[1]),
+            pltpu.make_async_copy(
+                shared_hidden_buf, shared_hidden_ref.at[sequence], store_sem.at[2]
+            ),
+            pltpu.make_async_copy(
+                shared_dhidden_buf, shared_dhidden_ref.at[:, sequence], store_sem.at[3]
+            ),
+            pltpu.make_async_copy(branch_buf, branch_ref.at[sequence], store_sem.at[4]),
+        )
+
+    def piece(step, tensor):
+        return rows_ref.at[sequence_of(step), pl.ds(pl.multiple_of(tensor * part_rows, part_rows), part_rows), :]
+
+    def peer_spread(step):
+        return pltpu.make_async_remote_copy(
+            src_ref=part_ref,
+            dst_ref=rows_ref.at[me, pl.ds(pl.multiple_of(mine * part_rows, part_rows), part_rows), :],
+            send_sem=spread_send_sem.at[step],
+            recv_sem=arrive_sem.at[step, mine],
+            device_id={"expert": (me + groups - step) % groups},
+            device_id_type=MESH,
+        )
+
+    def side_spread(step, shift):
+        return pltpu.make_async_remote_copy(
+            src_ref=piece(step, mine),
+            dst_ref=piece(step, mine),
+            send_sem=side_spread_sem.at[step, shift],
+            recv_sem=arrive_sem.at[step, mine],
+            device_id={"tensor": tensor_of(shift)},
+            device_id_type=MESH,
+        )
+
+    def core_spread(step, shift):
+        tensor = tensor_of(shift)
+        return pltpu.make_async_remote_copy(
+            src_ref=piece(step, tensor),
+            dst_ref=piece(step, tensor),
+            send_sem=core_spread_sem.at[step, shift],
+            recv_sem=arrive_sem.at[step, tensor],
+            device_id={"tensor": sibling},
+            device_id_type=MESH,
+        )
+
+    def wait_piece(step, tensor):
+        view = piece(step, tensor)
+        pltpu.make_async_copy(view, view, arrive_sem.at[step, tensor]).wait()
+
+    def forward_own(step):
+        for shift in range(1, sides):
+            side_spread(step, shift).start()
+        core_spread(step, 0).start()
+
+    def forward_sides(step):
+        for shift in range(1, sides):
+            wait_piece(step, tensor_of(shift))
+            core_spread(step, shift).start()
+
+    def await_sibling(step):
+        for shift in range(sides):
+            wait_piece(step, ((side + shift) % sides) * 2 + (1 - core))
+
+    def core_send(step):
+        slot = step % 2
+        return pltpu.make_async_remote_copy(
+            src_ref=grad_buf.at[slot, :, 1 - core],
+            dst_ref=core_land.at[slot],
+            send_sem=core_sem.at[slot],
+            recv_sem=core_land_sem.at[slot],
+            device_id={"tensor": sibling},
+            device_id_type=MESH,
+        )
+
+    def side_copy(step, shift):
+        slot = step % 2
+        return pltpu.make_async_remote_copy(
+            src_ref=side_send.at[slot, shift - 1],
+            dst_ref=side_land.at[slot, shift - 1],
+            send_sem=side_sem.at[slot, shift - 1],
+            recv_sem=side_land_sem.at[slot, shift - 1],
+            device_id={"tensor": tensor_of(shift)},
+            device_id_type=MESH,
+        )
+
+    def owner_copy(step):
+        slot = step % 2
+        return pltpu.make_async_remote_copy(
+            src_ref=owner_send.at[slot],
+            dst_ref=owner_land.at[step],
+            send_sem=owner_sem.at[slot],
+            recv_sem=owner_land_sem.at[step],
+            device_id={"expert": sequence_of(step)},
+            device_id_type=MESH,
+        )
+
+    def reduce_core(step):
+        slot = step % 2
+        copy = core_send(step)
+        copy.wait_recv()
+        copy.wait_send()
+
+        @pl.when(step >= 2)
+        def _():
+            for shift in range(1, sides):
+                side_copy(step - 2, shift).wait_send()
+
+        for shift in range(sides):
+            other = (side + shift) % sides
+            total = grad_buf[slot, other, core].astype(jnp.float32) + core_land[
+                slot, other
+            ].astype(jnp.float32)
+            if shift == 0:
+                side_keep[slot] = total
+            else:
+                side_send[slot, shift - 1] = total.astype(jnp.bfloat16)
+                side_copy(step, shift).start()
+
+    def reduce_sides(step):
+        slot = step % 2
+        for shift in range(1, sides):
+            side_copy(step, shift).wait_recv()
+        total = side_keep[slot]
+        for shift in range(1, sides):
+            total = total + side_land[slot, shift - 1].astype(jnp.float32)
+
+        @pl.when(step == 0)
+        def _():
+            owner_land[0] = total.astype(jnp.bfloat16)
+
+        @pl.when(step > 0)
+        def _():
+            @pl.when(step >= 3)
+            def _():
+                owner_copy(step - 2).wait_send()
+
+            owner_send[slot] = total.astype(jnp.bfloat16)
+            owner_copy(step).start()
+
+    for index in range(len(weight_pairs)):
+        weight_copy(index).start()
+    barrier = pltpu.get_barrier_semaphore()
+    for step in range(1, groups):
+        pl.semaphore_signal(
+            barrier, inc=1, device_id={"expert": (me + step) % groups}, device_id_type=MESH
+        )
+    for shift in range(1, sides):
+        pl.semaphore_signal(
+            barrier, inc=1, device_id={"tensor": tensor_of(shift)}, device_id_type=MESH
+        )
+    pl.semaphore_signal(barrier, inc=1, device_id={"tensor": sibling}, device_id_type=MESH)
+    own_copy = pltpu.make_async_copy(part_ref, piece(0, mine), own_sem)
+    own_copy.start()
+    pl.semaphore_wait(barrier, groups + sides - 1)
+    own_copy.wait()
+    forward_own(0)
+    for step in range(1, groups):
+        peer_spread(step).start()
+    forward_sides(0)
+    await_sibling(0)
+    for copy in load_copies(0):
+        copy.start()
+    if groups > 1:
+        wait_piece(1, mine)
+        forward_own(1)
+    for index in range(len(weight_pairs)):
+        weight_copy(index).wait()
+
+    def step_body(step, carry):
+        slot = step % 2
+        for copy in load_copies(step):
+            copy.wait()
+
+        @pl.when(step > 0)
+        def _():
+            for copy in store_copies(step - 1):
+                copy.wait()
+
+        logits = jnp.dot(rows_buf[slot], router_w[...], preferred_element_type=jnp.float32)
+        code = code_buf[slot].astype(jnp.float32)
+        lane = lax.broadcasted_iota(jnp.int32, code.shape, 1)
+        named = code > 0.5
+        highest = jnp.max(jnp.where(named, logits, -jnp.inf), axis=1, keepdims=True)
+        raised = jnp.where(named, jnp.exp(logits - highest), 0.0)
+        kept = jnp.where(code > 1.5, 1.0, 0.0)
+        gates = raised / jnp.sum(raised, axis=1, keepdims=True) * kept
+        for member in range(local_experts):
+            chosen = lane == me * local_experts + member
+            gates_buf[member] = jnp.broadcast_to(
+                jnp.sum(jnp.where(chosen, gates, 0.0), axis=1, keepdims=True), code.shape
+            )
+            kept_buf[member] = jnp.where(chosen, kept, 0.0)
+
+        row_block = min(256, length)
+
+        def expert_rows(block, inner):
+            rows = pl.ds(pl.multiple_of(block * row_block, row_block), row_block)
+            here = rows_buf[slot, rows, :]
+            back = cotangent_buf[slot, rows, :]
+            gate_grad = jnp.zeros((row_block, LANES), jnp.float32)
+            for member in range(local_experts):
+                pre = jnp.dot(here, gate_w[member], preferred_element_type=jnp.float32)
+                lin = jnp.dot(here, up_w[member], preferred_element_type=jnp.float32)
+                dhid = lax.dot_general(
+                    back,
+                    down_w[member],
+                    (((1,), (1,)), ((), ())),
+                    preferred_element_type=jnp.float32,
+                )
+                gate = gates_buf[member, rows, :][:, 0:1]
+                sigmoid = jax.nn.sigmoid(pre)
+                active = pre * sigmoid
+                hid = active * lin
+                gate_grad = gate_grad + kept_buf[member, rows, :] * jnp.sum(
+                    hid * dhid, axis=1, keepdims=True
+                )
+                dhid = dhid * gate
+                hidden_buf[member, rows, :] = (hid * gate).astype(jnp.bfloat16)
+                dhidden_buf[member, rows, :] = (
+                    dhid * lin * sigmoid * (1.0 + pre * (1.0 - sigmoid))
+                ).astype(jnp.bfloat16)
+                dhidden_buf[local_experts + member, rows, :] = (dhid * active).astype(jnp.bfloat16)
+            gate_grad_buf[rows, :] = gate_grad
+            return inner
+
+        lax.fori_loop(0, length // row_block, expert_rows, 0)
+
+        @pl.when(step + 2 < groups)
+        def _():
+            wait_piece(step + 2, mine)
+            forward_own(step + 2)
+
+        @pl.when(step + 1 < groups)
+        def _():
+            forward_sides(step + 1)
+
+        def shared_rows(block, inner):
+            rows = pl.ds(pl.multiple_of(block * row_block, row_block), row_block)
+            here = rows_buf[slot, rows, :]
+            back = cotangent_buf[slot, rows, :]
+            pre = jnp.dot(here, shared_gate_w[...], preferred_element_type=jnp.float32)
+            lin = jnp.dot(here, shared_up_w[...], preferred_element_type=jnp.float32)
+            dhid = lax.dot_general(
+                back,
+                shared_down_w[...],
+                (((1,), (1,)), ((), ())),
+                preferred_element_type=jnp.float32,
+            )
+            sigmoid = jax.nn.sigmoid(pre)
+            active = pre * sigmoid
+            shared_hidden_buf[rows, :] = (active * lin).astype(jnp.bfloat16)
+            shared_dhidden_buf[0, rows, :] = (
+                dhid * lin * sigmoid * (1.0 + pre * (1.0 - sigmoid))
+            ).astype(jnp.bfloat16)
+            shared_dhidden_buf[1, rows, :] = (dhid * active).astype(jnp.bfloat16)
+            return inner
+
+        lax.fori_loop(0, length // row_block, shared_rows, 0)
+
+        @pl.when(step + 1 < groups)
+        def _():
+            await_sibling(step + 1)
+            for copy in load_copies(step + 1):
+                copy.start()
+
+        @pl.when(step >= 2)
+        def _():
+            reduce_sides(step - 2)
+
+        @pl.when(step >= 1)
+        def _():
+            reduce_core(step - 1)
+
+        column_block = 512
+
+        def mix_columns(block, inner):
+            columns = pl.ds(pl.multiple_of(block * column_block, column_block), column_block)
+            total = jnp.dot(
+                hidden_buf[0], down_w[0, :, columns], preferred_element_type=jnp.float32
+            )
+            for member in range(1, local_experts):
+                total = total + jnp.dot(
+                    hidden_buf[member],
+                    down_w[member, :, columns],
+                    preferred_element_type=jnp.float32,
+                )
+            branch_buf[:, columns] = total.astype(jnp.bfloat16)
+            total = None
+            for member in range(local_experts):
+                for half, weight in ((0, gate_w), (1, up_w)):
+                    term = lax.dot_general(
+                        dhidden_buf[half * local_experts + member],
+                        weight[member, columns, :],
+                        (((1,), (1,)), ((), ())),
+                        preferred_element_type=jnp.float32,
+                    )
+                    total = term if total is None else total + term
+            grad_buf[slot, :, :, :, columns] = total.astype(jnp.bfloat16).reshape(
+                sides, 2, part_rows, column_block
+            )
+            return inner
+
+        lax.fori_loop(0, width // column_block, mix_columns, 0)
+
+        @pl.when(step == 0)
+        def _():
+            def mix_shared(block, inner):
+                columns = pl.ds(pl.multiple_of(block * column_block, column_block), column_block)
+                branch_buf[:, columns] = (
+                    branch_buf[:, columns].astype(jnp.float32)
+                    + jnp.dot(
+                        shared_hidden_buf[...],
+                        shared_down_w[:, columns],
+                        preferred_element_type=jnp.float32,
+                    )
+                ).astype(jnp.bfloat16)
+                total = lax.dot_general(
+                    shared_dhidden_buf[0],
+                    shared_gate_w[columns, :],
+                    (((1,), (1,)), ((), ())),
+                    preferred_element_type=jnp.float32,
+                ) + lax.dot_general(
+                    shared_dhidden_buf[1],
+                    shared_up_w[columns, :],
+                    (((1,), (1,)), ((), ())),
+                    preferred_element_type=jnp.float32,
+                )
+                grad_buf[0, :, :, :, columns] = (
+                    grad_buf[0, :, :, :, columns].astype(jnp.float32)
+                    + total.reshape(sides, 2, part_rows, column_block)
+                ).astype(jnp.bfloat16)
+                return inner
+
+            lax.fori_loop(0, width // column_block, mix_shared, 0)
+
+        grad_buf[slot, :, :, :, pl.ds(width, LANES)] = (
+            gate_grad_buf[...].astype(jnp.bfloat16).reshape(sides, 2, part_rows, LANES)
+        )
+        core_send(step).start()
+        for copy in store_copies(step):
+            copy.start()
+        return carry
+
+    lax.fori_loop(0, groups, step_body, 0)
+
+    if groups > 1:
+        reduce_sides(groups - 2)
+    reduce_core(groups - 1)
+    reduce_sides(groups - 1)
+    total = owner_land[0].astype(jnp.float32)
+    for step in range(1, groups):
+        owner_copy(step).wait_recv()
+        total = total + owner_land[step].astype(jnp.float32)
+    grad_ref[...] = total
+
+    for copy in store_copies(groups - 1):
+        copy.wait()
+    for step in range(groups):
+        if step > 0:
+            peer_spread(step).wait_send()
+        for shift in range(1, sides):
+            side_spread(step, shift).wait_send()
+        for shift in range(sides):
+            core_spread(step, shift).wait_send()
+    for step in range(max(groups - 2, 0), groups):
+        for shift in range(1, sides):
+            side_copy(step, shift).wait_send()
+        if step > 0:
+            owner_copy(step).wait_send()
+
+
+def run_experts(
+    part,
+    cotangent_all,
+    code_all,
+    expert_gate,
+    expert_up,
+    expert_down,
+    shared_gate,
+    shared_up,
+    shared_down,
+    router_padded,
+    length,
+):
+    groups = lax.axis_size("expert")
+    tensors = lax.axis_size("tensor")
+    sides = tensors // 2
+    part_rows = length // tensors
+    local_experts, width, hidden = expert_gate.shape
+    shared = shared_gate.shape[1]
+    bf16 = jnp.bfloat16
+    f32 = jnp.float32
+    packed = width + LANES
+    anywhere = pl.BlockSpec(memory_space=pl.ANY)
+    dma = pltpu.SemaphoreType.DMA
+    flops = (
+        2 * groups * length * width * 6 * local_experts * hidden
+        + 2 * groups * length * width * 3 * shared
+    )
+    return pl.pallas_call(
+        functools.partial(expert_kernel, groups=groups, tensors=tensors),
+        out_shape=(
+            jax.ShapeDtypeStruct((groups, length, width), bf16),
+            jax.ShapeDtypeStruct((groups, length, width), bf16),
+            jax.ShapeDtypeStruct((local_experts, groups, length, hidden), bf16),
+            jax.ShapeDtypeStruct((2 * local_experts, groups, length, hidden), bf16),
+            jax.ShapeDtypeStruct((groups, length, shared), bf16),
+            jax.ShapeDtypeStruct((2, groups, length, shared), bf16),
+            jax.ShapeDtypeStruct((part_rows, packed), f32),
+        ),
+        in_specs=[anywhere] * 10,
+        out_specs=(anywhere,) * 6 + (pl.BlockSpec(memory_space=pltpu.VMEM),),
+        scratch_shapes=[
+            pltpu.VMEM((local_experts, width, hidden), bf16),
+            pltpu.VMEM((local_experts, width, hidden), bf16),
+            pltpu.VMEM((local_experts, hidden, width), bf16),
+            pltpu.VMEM((width, shared), bf16),
+            pltpu.VMEM((width, shared), bf16),
+            pltpu.VMEM((shared, width), bf16),
+            pltpu.VMEM((width, LANES), bf16),
+            pltpu.VMEM((2, length, width), bf16),
+            pltpu.VMEM((2, length, width), bf16),
+            pltpu.VMEM((2, length, LANES), bf16),
+            pltpu.VMEM((local_experts, length, LANES), f32),
+            pltpu.VMEM((local_experts, length, LANES), f32),
+            pltpu.VMEM((length, LANES), f32),
+            pltpu.VMEM((local_experts, length, hidden), bf16),
+            pltpu.VMEM((2 * local_experts, length, hidden), bf16),
+            pltpu.VMEM((length, shared), bf16),
+            pltpu.VMEM((2, length, shared), bf16),
+            pltpu.VMEM((length, width), bf16),
+            pltpu.VMEM((2, sides, 2, part_rows, packed), bf16),
+            pltpu.VMEM((2, sides, part_rows, packed), bf16),
+            pltpu.VMEM((2, sides - 1, part_rows, packed), bf16),
+            pltpu.VMEM((2, part_rows, packed), f32),
+            pltpu.VMEM((2, sides - 1, part_rows, packed), bf16),
+            pltpu.VMEM((2, part_rows, packed), bf16),
+            pltpu.VMEM((groups, part_rows, packed), bf16),
+            dma((7,)),
+            dma(()),
+            dma((2, 3)),
+            dma((5,)),
+            dma((groups,)),
+            dma((groups, sides)),
+            dma((groups, sides)),
+            dma((groups, tensors)),
+            dma((2,)),
+            dma((2,)),
+            dma((2, sides - 1)),
+            dma((2, sides - 1)),
+            dma((2,)),
+            dma((groups,)),
+        ],
+        compiler_params=pltpu.CompilerParams(
+            collective_id=1,
+            has_side_effects=True,
+            vmem_limit_bytes=60 * 1024 * 1024,
+        ),
+        cost_estimate=pl.CostEstimate(
+            flops=flops, bytes_accessed=100_000_000, transcendentals=0
+        ),
+        name="experts",
+    )(
+        part,
+        cotangent_all.reshape(groups, length, width),
+        code_all.reshape(groups, length, LANES),
+        expert_gate,
+        expert_up,
+        expert_down,
+        shared_gate,
+        shared_up,
+        shared_down,
+        router_padded,
+    )
 
 
 def on_device(
@@ -152,8 +746,10 @@
         return lax.dynamic_slice_in_dim(rows, group_index * shard_columns, shard_columns, 1)
 
     cotangent_all = gather_rows(own_part(cotangent))
-    marked = jnp.where(slot_index < capacity, routes, routes + experts_all)
-    marked_all = lax.all_gather(marked, "expert", axis=0, tiled=True)
+    code_part = own_part(
+        expert_table(routes, jnp.where(slot_index < capacity, 2.0, 1.0), LANES)
+    )
+    code_all = gather_rows(code_part.astype(jnp.bfloat16))
 
     rows_in = inputs.astype(jnp.float32)
     normed_one, unit_one, factor_one = normalize(rows_in, attention_gain)
@@ -205,101 +801,54 @@
     residual = own_part(rows_in) + attention
     normed_two, unit_two, factor_two = normalize(residual, feedforward_gain)
     second_part = normed_two.astype(jnp.bfloat16)
-    second_all = gather_rows(second_part)
-
-    logits_all = plain_dot(second_all, router_weight)
-    ones = jnp.ones(marked_all.shape, jnp.float32)
-    kept_all = expert_table(marked_all, ones, experts_all)
-    named_all = kept_all + expert_table(marked_all - experts_all, ones, experts_all)
-    highest = jnp.max(jnp.where(named_all > 0, logits_all, -jnp.inf), axis=1, keepdims=True)
-    raised = jnp.where(named_all > 0, jnp.exp(logits_all - highest), 0.0)
-    gates_all = raised / jnp.sum(raised, axis=1, keepdims=True)
-    kept_gates = gates_all * kept_all
-    local_gates = lax.dynamic_slice_in_dim(
-        kept_gates, group_index * local_experts, local_experts, 1
-    )
-    local_kept = lax.dynamic_slice_in_dim(kept_all, group_index * local_experts, local_experts, 1)
-
-    shared_pre = plain_dot(second_all, shared_gate)
-    shared_lin = plain_dot(second_all, shared_up)
-    shared_sigmoid = jax.nn.sigmoid(shared_pre)
-    shared_hidden = (shared_pre * shared_sigmoid * shared_lin).astype(jnp.bfloat16)
-    shared_dhidden = tail_dot(cotangent_all, shared_down)
-    shared_dpre = (
-        shared_dhidden * shared_lin * shared_sigmoid * (1.0 + shared_pre * (1.0 - shared_sigmoid))
-    ).astype(jnp.bfloat16)
-    shared_dlin = (shared_dhidden * shared_pre * shared_sigmoid).astype(jnp.bfloat16)
+    (
+        second_all,
+        branch,
+        hidden_all,
+        dhidden_all,
+        shared_hidden,
+        shared_dhidden,
+        grad_part,
+    ) = run_experts(
+        second_part,
+        cotangent_all,
+        code_all,
+        expert_gate,
+        expert_up,
+        expert_down,
+        shared_gate,
+        shared_up,
+        shared_down,
+        jnp.pad(router_weight, ((0, 0), (0, LANES - experts_all))),
+        length,
+    )
+    tokens = group_count * length
+    second_all = second_all.reshape(tokens, model_width)
+    hidden_all = hidden_all.reshape(local_experts, tokens, expert_hidden_width)
+    dhidden_all = dhidden_all.reshape(2 * local_experts, tokens, expert_hidden_width)
+    shared_hidden = shared_hidden.reshape(tokens, shared_width)
+    shared_dhidden = shared_dhidden.reshape(2, tokens, shared_width)
     second_columns = own_columns(second_all)
-    grad_shared_gate = lead_dot(second_columns, shared_dpre)
-    grad_shared_up = lead_dot(second_columns, shared_dlin)
+    grad_shared_gate = lead_dot(second_columns, shared_dhidden[0])
+    grad_shared_up = lead_dot(second_columns, shared_dhidden[1])
     grad_shared_down = lead_dot(shared_hidden, own_columns(cotangent_all))
-
-    hidden_list = []
-    gate_grad_list = []
     grad_gate_list = []
     grad_up_list = []
     grad_down_list = []
-    input_grad_list = []
-    weight_list = []
-    down_rows = expert_down.reshape(local_experts * expert_hidden_width, model_width)
-    raw_dhidden = tail_dot(cotangent_all, down_rows)
     for member in range(local_experts):
-        gate = local_gates[:, member : member + 1]
-        gate_pre = plain_dot(second_all, expert_gate[member])
-        up_pre = plain_dot(second_all, expert_up[member])
-        sigmoid = jax.nn.sigmoid(gate_pre)
-        active = gate_pre * sigmoid
-        hidden = active * up_pre
-        hidden_low = (gate * hidden).astype(jnp.bfloat16)
-        hidden_list.append(hidden_low)
-        dhidden = raw_dhidden[
-            :, member * expert_hidden_width : (member + 1) * expert_hidden_width
-        ]
-        gate_grad_list.append(
-            local_kept[:, member] * jnp.sum(hidden * dhidden, axis=1)
-        )
-        dhidden = gate * dhidden
-        dpre = (dhidden * up_pre * sigmoid * (1.0 + gate_pre * (1.0 - sigmoid))).astype(
-            jnp.bfloat16
-        )
-        dlin = (dhidden * active).astype(jnp.bfloat16)
-        grad_gate_list.append(lead_dot(second_all, dpre))
-        grad_up_list.append(lead_dot(second_all, dlin))
-        grad_down_list.append(lead_dot(hidden_low, cotangent_all))
-        input_grad_list += [dpre, dlin]
-        weight_list += [expert_gate[member], expert_up[member]]
-
-    branch = plain_dot(jnp.concatenate(hidden_list, axis=1), down_rows).astype(jnp.bfloat16)
-    own_branch = own_sequence(branch) + plain_dot(
-        own_sequence(shared_hidden), shared_down
-    ).astype(jnp.bfloat16)
-    branch = lax.dynamic_update_slice_in_dim(branch, own_branch, group_index * length, 0)
-    feedforward = scatter_rows(branch).astype(jnp.float32)
+        grad_gate_list.append(lead_dot(second_all, dhidden_all[member]))
+        grad_up_list.append(lead_dot(second_all, dhidden_all[local_experts + member]))
+        grad_down_list.append(lead_dot(hidden_all[member], cotangent_all))
+
+    feedforward = scatter_rows(branch.reshape(tokens, model_width)).astype(jnp.float32)
     result_part = (residual + feedforward).astype(jnp.bfloat16)
     result = lax.all_gather(result_part, "tensor", axis=0, tiled=True)
 
-    second_grad = tail_dot(
-        jnp.concatenate(input_grad_list, axis=1), jnp.concatenate(weight_list, axis=1)
-    ).astype(jnp.bfloat16)
-    own_grad = own_sequence(second_grad) + tail_dot(
-        jnp.concatenate([own_sequence(shared_dpre), own_sequence(shared_dlin)], axis=1),
-        jnp.concatenate([shared_gate, shared_up], axis=1),
-    ).astype(jnp.bfloat16)
-    second_grad = lax.dynamic_update_slice_in_dim(second_grad, own_grad, group_index * length, 0)
-    grad_second = scatter_rows(second_grad).astype(jnp.float32)
-
-    gate_grad_local = jnp.stack(gate_grad_list, axis=1)
-    gate_grad = scatter_rows(
-        lax.dynamic_update_slice_in_dim(
-            jnp.zeros((group_count * length, experts_all), jnp.float32),
-            gate_grad_local,
-            group_index * local_experts,
-            1,
-        )
-    )
-    part_gates = lax.dynamic_slice_in_dim(
-        gates_all, group_index * length + part_start, part_rows, 0
-    )
+    grad_second = grad_part[:, :model_width]
+    gate_grad = grad_part[:, model_width : model_width + experts_all]
+    code_own = code_part[:, :experts_all]
+    logits = jnp.where(code_own > 0, plain_dot(second_part, router_weight), -jnp.inf)
+    part_gates = jax.nn.softmax(logits, axis=1)
     logit_low = (
         part_gates * (gate_grad - jnp.sum(part_gates * gate_grad, axis=1, keepdims=True))
     ).astype(jnp.bfloat16)

time: 1350 us -> 1210 us (0.90)
  Pallas kernels: 0 us -> 302 us
  waiting for transfers between devices: 860 us -> 635 us
  matrix products: 337 us -> 121 us
  blocking collectives: 37.7 us -> 6.4 us
  local copies, waits for them, and re-layouts: 39.6 us -> 65.8 us
    pallas_call x0 -> x1, Pallas kernels: none -> 302 us  [run_experts(): pl.pallas_call(functools.partial(expert_kernel, groups=groups, tensors=te...]
    reduce_scatter x4 -> x2, waiting for transfers between devices: 529 us -> 270 us  [scatter_rows(): return lax.psum_scatter(rows, BOTH, scatter_dimension=0, tiled=True)]
    dot_general x13 -> x5, matrix products: 146 us -> 12.6 us  [plain_dot(): return jnp.dot(left_side, right_side, preferred_element_type=jnp.float32)]
    dot_general x9 -> x5, matrix products: 90.4 us -> 12.4 us  [tail_dot(): lax.dot_general(left_side, right_side, (((1,), (1,)), ((), ())), preferre...]
    reduce_scatter x3, waiting for transfers between devices: 107 us -> 158 us  [expert_sum(): lax.psum_scatter(array.astype(jnp.bfloat16), 'expert', scatter_dimension=...]
    all_gather x1 -> x0, blocking collectives: 31.3 us -> none  [on_device(): marked_all = lax.all_gather(marked, 'expert', axis=0, tiled=True)]
    reduce_scatter x1, waiting for transfers between devices: 28.2 us -> 4.53 us  [on_device(): lax.psum_scatter(plain_dot(head_out, out_weight).astype(jnp.bfloat16), 't...]
    unnamed x150 -> x177, local copies, waits for them, and re-layouts: 17.5 us -> 36.7 us
  transfers between devices with their start and end apart: 14 -> 12, of which waited for: 12 -> 11; matrix products, arithmetic and copies ran while one was open for 23% -> 15% of each run, Pallas kernels for 0% -> 0%
where the time goes in v2:
time: 1210 us
  waiting for transfers between devices  635 us (52%)
  Pallas kernels  302 us (25%)
  matrix products  121 us (10%)
  local copies, waits for them, and re-layouts  65.8 us (5%)
  other arithmetic  56.1 us (5%)
  between operations  17.2 us (1%)
    pallas_call x1, Pallas kernels, run_experts(): pl.pallas_call(functools.partial(expert_kernel, groups=groups, tensors=te...  302 us
    reduce_scatter x2, waiting for transfers between devices, scatter_rows(): return lax.psum_scatter(rows, BOTH, scatter_dimension=0, tiled=True)  270 us
    reduce_scatter x3, waiting for transfers between devices, expert_sum(): lax.psum_scatter(array.astype(jnp.bfloat16), 'expert', scatter_dimension=...  158 us
    all_gather x2, waiting for transfers between devices, gather_rows(): return lax.all_gather(rows, BOTH, axis=0, tiled=True)  137 us
    dot_general x14, matrix products, lead_dot(): lax.dot_general(left_side, right_side, (((0,), (0,)), ((), ())), preferre...  91.9 us
    unnamed x177, local copies, waits for them, and re-layouts  36.7 us
    all_gather x1, waiting for transfers between devices, on_device(): lax.all_gather(grad_residual.astype(jnp.bfloat16), 'tensor', axis=0, tile...  33.8 us
  transfers between devices with their start and end apart: 12, of which 11 were waited for; matrix products, arithmetic and copies ran while one was open for 15% of the time, Pallas kernels for 0%

profile of v2, /device:TPU:0, one launch (start us, length us, event | category | flops | bytes accessed | tf_op | source)
XLA Modules:
  0.0 1206.0 jit_solution(11951107759084518843)
XLA Ops:
  8.1 2.2 multiply_reduce_fusion.1
  11.1 4.0 fusion.58
  15.1 3.1 fusion.57
  18.9 1.8 convolution_convert_fusion.6
  20.7 2.3 copy.80
  29.7 2.1 fusion.66
  32.3 1.6 copy-done.12
  35.0 2.6 convolution_convert_fusion.3
  39.7 1.9 constant_dynamic-slice_fusion
  41.8 4.1 convert_element_type.116
  45.9 4.7 copy.57.gate_ref
  50.6 4.6 copy.58.up_ref
  55.2 4.7 copy.59.shared_gate_ref
  59.9 4.7 copy.60.shared_up_ref
  65.6 1.9 pad.9.router_ref
  67.6 4.5 reduce-scatter.8.cloned.1.call-done
  72.1 1.6 multiply_reduce_fusion.6
  78.1 19.8 %all-gather.8.cloned.1.call-done = bf16[4096,128]{1,0:T(8,128)(2,1)} async-done(((bf16[128,128]{1,0:T(8,128)(2,1)}), bf16[4096,128]{1,0:T(8,128)(2,1)}) %all-gather.8.cloned.1.call-update) | async-done | bytes 1048592 | tf_op jit(solution)/shard_map/all_gather | solution.py:92
  97.9 117.5 %all-gather.6.cloned.1.call-done = bf16[4096,2048]{1,0:T(8,128)(2,1)} async-done(((bf16[128,2048]{1,0:T(8,128)(2,1)}), bf16[4096,2048]{1,0:T(8,128)(2,1)}) %all-gather.6.cloned.1.call-update) | async-done | bytes 16777232 | tf_op jit(solution)/shard_map/all_gather | solution.py:92
  215.4 302.4 %experts.1 = (bf16[8,512,2048]{2,1,0:T(8,128)(2,1)}, bf16[8,512,2048]{2,1,0:T(8,128)(2,1)}, bf16[2,8,512,352]{3,2,1,0:T(8,128)(2,1)}, bf16[4,8,512,352]{3,2,1,0:...) custom-call(bf16[128,2048]{1,0:T(8,128)(2,1)} %copy-done.24, ...), custom_call_target="tpu_custom_call" | custom-call | flops 106300440576 | bytes 100000000 | tf_op jit(solution)/shard_map/experts/pallas_call | solution.py:623
  519.0 2.7 multiply_reduce_fusion.3
  522.7 2.2 fusion.56
  524.9 33.8 %all-gather.12.cloned.1.call-done = bf16[512,2048]{1,0:T(8,128)(2,1)} async-done(((bf16[128,2048]{1,0:T(8,128)(2,1)}), bf16[512,2048]{1,0:T(8,128)(2,1)}) %all-gather.12.cloned.1.call-update) | async-done | bytes 2097168 | tf_op jit(solution)/shard_map/all_gather | solution.py:861
  558.8 3.6 convolution_convert_fusion.7
  570.6 1.8 fusion.68
  572.7 3.3 add_convert_fusion
  577.7 1.7 convolution_convert_fusion.5
  579.6 4.5 convolution_convert_fusion.2
  584.6 3.7 convolution_convert_fusion
  588.5 2.4 broadcast_multiply_fusion
  592.1 5.7 fusion.62
  597.7 11.5 convolution_bitcast_fusion
  610.8 1.6 pad_maximum_fusion.3
  612.4 3.1 copy.79
  615.5 1.8 fusion.20
  617.4 2.1 fusion.2
  619.7 1.6 copy-done.20
  621.3 10.2 convolution_bitcast_fusion.1
  631.5 2.9 pad_maximum_fusion.2
  634.4 3.5 fusion.60
  637.9 11.6 convolution_bitcast_fusion.3
  649.5 11.9 convolution_bitcast_fusion.2
  661.3 131.4 %reduce-scatter.10.cloned.1.call-done = bf16[128,2048]{1,0:T(8,128)(2,1)} async-done(((bf16[4096,2048]{1,0:T(8,128)(2,1)}), bf16[128,2048]{1,0:T(8,128)(2,1)}) %reduce-scatter.10.cloned.1.call-update) | async-done | bytes 524304 | tf_op jit(solution)/shard_map/reduce_scatter | solution.py:96
  792.7 2.9 fusion.19
  796.0 6.1 pad_maximum_fusion.1
  802.1 11.8 convolution_bitcast_fusion.5
  813.9 7.8 convolution_bitcast_fusion.4
  821.7 6.0 pad_maximum_fusion
  827.7 5.9 fusion.61
  833.6 5.2 fusion.9
  838.8 5.2 fusion.11
  843.9 4.3 fusion.4
  848.2 12.8 %reduce-scatter.18.cloned.1.call-done = bf16[64,1024]{1,0:T(8,128)(2,1)} async-done(((bf16[512,1024]{1,0:T(8,128)(2,1)}), bf16[64,1024]{1,0:T(8,128)(2,1)}) %reduce-scatter.18.cloned.1.call-update) | async-done | bytes 131088 | tf_op jit(solution)/shard_map/reduce_scatter | solution.py:947
  861.0 1.6 convert_element_type.146
  862.7 69.6 %reduce-scatter.20.cloned.1.call-done = bf16[512,256]{1,0:T(8,128)(2,1)} async-done(((bf16[512,2048]{1,0:T(8,128)(2,1)}), bf16[512,256]{1,0:T(8,128)(2,1)}) %reduce-scatter.20.cloned.1.call-update) | async-done | bytes 262160 | tf_op jit(solution)/shard_map/reduce_scatter | solution.py:947
  932.2 1.8 convert_element_type.148
  934.0 75.5 %reduce-scatter.16.cloned.1.call-done = bf16[256,768]{1,0:T(8,128)(2,1)} async-done(((bf16[2048,768]{1,0:T(8,128)(2,1)}), bf16[256,768]{1,0:T(8,128)(2,1)}) %reduce-scatter.16.cloned.1.call-update) | async-done | bytes 393232 | tf_op jit(solution)/shard_map/reduce_scatter | solution.py:947
  1009.5 1.9 convert_element_type.144
  1011.4 138.9 %reduce-scatter.14.cloned.1.call-done = bf16[80,592]{1,0:T(8,128)(2,1)} async-done(((bf16[2560,592]{1,0:T(8,128)(2,1)}), bf16[80,592]{1,0:T(8,128)(2,1)}) %reduce-scatter.14.cloned.1.call-update) | async-done | bytes 94736 | tf_op jit(solution)/shard_map/reduce_scatter | solution.py:96
  1150.3 6.4 all_gather.23
  1159.7 11.3 all-gather.14.cloned.1.call-done
  1170.9 4.3 convert_element_type.140
  1175.2 19.7 %all-gather.10.cloned.1.call-done = bf16[512,2048]{1,0:T(8,128)(2,1)} async-done(((bf16[128,2048]{1,0:T(8,128)(2,1)}), bf16[512,2048]{1,0:T(8,128)(2,1)}) %all-gather.10.cloned.1.call-update) | async-done | bytes 2097168 | tf_op jit(solution)/shard_map/all_gather | solution.py:845
  1195.0 3.2 copy.83
  (261 shorter events, 36.1 us)
Async XLA Ops:
  8.0 7.1 copy-start
  8.0 64.1 %reduce-scatter.8.cloned.1.call-start = ((), (), s32[]{:S(2)}) async-start(), calls=%async_computation.7 | async-start | bytes 2621440 | tf_op jit(solution)/shard_map/reduce_scatter | solution.py:795
  8.1 17.6 %copy-start.62 = (f32[32]{0:T(128)}, f32[32]{0:T(128)S(1)}, u32[]{:S(2)}) copy-start(f32[32]{0:T(128)S(1)} %multiply_power_fusion) | copy-start | bytes 388
  10.3 4.7 copy-start.51
  11.1 14.6 %copy-start.45 = (f32[512]{0:T(512)}, f32[512]{0:T(512)S(1)}, u32[]{:S(2)}) copy-start(f32[512]{0:T(512)S(1)} %get-tuple-element.93) | copy-start | bytes 6148
  11.1 4.0 copy-start.2
  11.1 4.0 copy-start.43
  15.1 3.2 copy-start.7
  15.1 3.8 copy-start.53
  15.1 3.8 copy-start.72
  24.1 4.2 copy-start.10
  25.6 2.7 copy-start.26
  31.9 3.2 copy-start.71
  35.0 2.7 copy-start.49
  35.0 3.2 copy-start.50
  37.6 60.3 %all-gather.8.cloned.1.call-start = ((), (), s32[]{:S(2)}) async-start(), calls=%async_computation.9 | async-start | bytes 1081344 | tf_op jit(solution)/shard_map/all_gather | solution.py:92
  39.6 175.8 %all-gather.6.cloned.1.call-start = ((), (), s32[]{:S(2)}) async-start(), calls=%async_computation.8 | async-start | bytes 17301504 | tf_op jit(solution)/shard_map/all_gather | solution.py:92
  41.6 517.2 %all-gather.12.cloned.1.call-start = ((), (), s32[]{:S(2)}) async-start(), calls=%async_computation.12 | async-start | bytes 2621440 | tf_op jit(solution)/shard_map/all_gather | solution.py:861
  59.9 4.7 copy-start.41
  64.6 10.1 copy-start.42
  215.4 302.5 %copy-start.59 = (f32[128]{0:T(128)S(1)}, f32[128]{0:T(128)}, u32[]{:S(2)}) copy-start(f32[128]{0:T(128)} %copy-done.58) | copy-start | bytes 1540
  215.4 302.5 %copy-start.66 = (f32[128]{0:T(128)S(1)}, f32[128]{0:T(128)}, u32[]{:S(2)}) copy-start(f32[128]{0:T(128)} %fusion.45) | copy-start | bytes 1540
  215.4 303.6 %copy-start.56 = (f32[128]{0:T(128)S(1)}, f32[128]{0:T(128)}, u32[]{:S(2)}) copy-start(f32[128]{0:T(128)} %copy-done.55) | copy-start | bytes 1540
  517.8 4.9 copy-start.5
  519.0 2.7 copy-start.68
  521.7 40.7 %copy-start.64 = (f32[128]{0:T(128)}, f32[128]{0:T(128)S(1)}, u32[]{:S(2)}) copy-start(f32[128]{0:T(128)S(1)} %broadcast_multiply_fusion.3) | copy-start | bytes 1540
  524.9 90.7 %reduce-scatter.12.cloned.1.call-start = ((), (), s32[]{:S(2)}) async-start(), calls=%async_computation.13 | async-start | bytes 2621440 | tf_op jit(solution)/shard_map/reduce_scatter | solution.py:906
  558.8 3.7 copy-start.13
  567.6 2.6 copy-start.46
  567.6 2.6 copy-start.63
  567.7 2.9 copy-start.14
  572.7 3.4 copy-start.39
  576.1 216.6 %reduce-scatter.10.cloned.1.call-start = ((), (), s32[]{:S(2)}) async-start(), calls=%async_computation.10 | async-start | bytes 17301504 | tf_op jit(solution)/shard_map/reduce_scatter | solution.py:96
  576.7 284.4 %reduce-scatter.18.cloned.1.call-start = ((), (), s32[]{:S(2)}) async-start(), calls=%async_computation.17 | async-start | bytes 1179648 | tf_op jit(solution)/shard_map/reduce_scatter | solution.py:947
  579.5 5.1 copy-start.3
  579.5 5.1 copy-start.30
  579.5 5.1 copy-start.44
  579.5 5.1 copy-start.52
  579.6 352.7 %reduce-scatter.20.cloned.1.call-start = ((), (), s32[]{:S(2)}) async-start(), calls=%async_computation.18 | async-start | bytes 2359296 | tf_op jit(solution)/shard_map/reduce_scatter | solution.py:947
  584.1 425.3 %reduce-scatter.16.cloned.1.call-start = ((), (), s32[]{:S(2)}) async-start(), calls=%async_computation.16 | async-start | bytes 3538944 | tf_op jit(solution)/shard_map/reduce_scatter | solution.py:947
  588.4 561.9 %reduce-scatter.14.cloned.1.call-start = ((), (), s32[]{:S(2)}) async-start(), calls=%async_computation.15 | async-start | bytes 3379200 | tf_op jit(solution)/shard_map/reduce_scatter | solution.py:96
  588.5 2.4 copy-start.67
  588.5 2.4 copy-start.69
  597.7 11.5 copy-start.40
  619.4 551.5 %all-gather.14.cloned.1.call-start = ((), (), s32[]{:S(2)}) async-start(), calls=%async_computation.14 | async-start | bytes 2621440 | tf_op jit(solution)/shard_map/all_gather | solution.py:915
  619.7 14.7 %slice-start = ((s8[12582912]{0:T(1024)(128)(4,1)}), s8[4194304]{0:T(1024)(128)(4,1)S(1)}, s32[]{:S(2)}) async-start(s8[12582912]{0:T(1024)(128)(4,1)} %bitcast.100), calls=%async_computation.19 | async-start | bytes 8388608
  621.3 10.2 copy-start.21
  621.3 13.1 %slice-start.1 = ((s8[12582912]{0:T(1024)(128)(4,1)}), s8[4194304]{0:T(1024)(128)(4,1)S(1)}, s32[]{:S(2)}) async-start(s8[12582912]{0:T(1024)(128)(4,1)} %bitcast.100), calls=%async_computation.20 | async-start | bytes 8388608
  621.3 13.1 %slice-start.2 = ((s8[12582912]{0:T(1024)(128)(4,1)}), s8[4194304]{0:T(1024)(128)(4,1)S(1)}, s32[]{:S(2)}) async-start(s8[12582912]{0:T(1024)(128)(4,1)} %bitcast.100), calls=%async_computation.21 | async-start | bytes 8388608
  649.4 143.3 %copy-start.6 = (f32[128,2048]{1,0:T(8,128)S(1)}, f32[128,2048]{1,0:T(8,128)}, u32[]{:S(2)}) copy-start(f32[128,2048]{1,0:T(8,128)} %copy-done.4) | copy-start | bytes 3145732
  649.5 143.3 %copy-start.17 = (f32[128,2048]{1,0:T(8,128)S(1)}, f32[128,2048]{1,0:T(8,128)}, u32[]{:S(2)}) copy-start(f32[128,2048]{1,0:T(8,128)} %copy-done.16) | copy-start | bytes 3145732
  649.5 143.3 %copy-start.28 = (bf16[128,2048]{1,0:T(8,128)(2,1)S(1)}, bf16[128,2048]{1,0:T(8,128)(2,1)}, u32[]{:S(2)}) copy-start(bf16[128,2048]{1,0:T(8,128)(2,1)} %reduce-scatter.12.cloned.1.call-done) | copy-start | bytes 1572868
  649.5 143.3 %copy-start.57 = (f32[128]{0:T(128)S(1)}, f32[128]{0:T(128)}, u32[]{:S(2)}) copy-start(f32[128]{0:T(128)} %copy-done.55) | copy-start | bytes 1540
  649.5 143.3 %copy-start.65 = (f32[128]{0:T(128)S(1)}, f32[128]{0:T(128)}, u32[]{:S(2)}) copy-start(f32[128]{0:T(128)} %copy-done.64) | copy-start | bytes 1540
  795.7 399.3 %all-gather.10.cloned.1.call-start = ((), (), s32[]{:S(2)}) async-start(), calls=%async_computation.11 | async-start | bytes 2621440 | tf_op jit(solution)/shard_map/all_gather | solution.py:845
  795.9 6.1 copy-start.19
  796.0 17.9 %slice-start.3 = ((s8[16777216]{0:T(1024)(128)(4,1)}), s8[4194304]{0:T(1024)(128)(4,1)S(1)}, s32[]{:S(2)}) async-start(s8[16777216]{0:T(1024)(128)(4,1)} %bitcast.141), calls=%async_computation.22 | async-start | bytes 8388608
  802.1 11.8 copy-start.18
  802.1 11.8 slice-start.4
  802.1 11.8 slice-start.5
  802.1 11.8 slice-start.6
  833.6 10.4 slice-start.7
  838.8 5.2 slice-start.8
  1170.9 27.2 %copy-start.1 = (bf16[2048,768]{1,0:T(8,128)(2,1)S(1)}, bf16[2048,768]{1,0:T(8,128)(2,1)}, u32[]{:S(2)}) copy-start(bf16[2048,768]{1,0:T(8,128)(2,1)} %param.27) | copy-start | bytes 9437188
  (32 other events, 43.2 us)
Sparse Core Ops, SparseCore 0:
  37.8 34.2 reduce-scatter.7
  525.0 33.7 all-gather.11
  576.2 31.4 reduce-scatter.11
  609.8 182.8 reduce-scatter.9
  796.0 65.0 reduce-scatter.17
  864.8 67.3 reduce-scatter.19
  936.2 73.2 reduce-scatter.15
  1011.9 138.3 reduce-scatter.13
  1152.4 18.4 all-gather.13
  1172.3 22.5 all-gather.9
Sparse Core Ops, SparseCore 1:
  41.4 56.5 all-gather.7
  101.6 113.7 all-gather.5

commit v3 on v1

v3 whole, which is shorter than its diff:
```python
import functools
import math

import jax
import jax.numpy as jnp
from jax import lax
from jax.experimental import pallas as pl
from jax.experimental.pallas import tpu as pltpu
from jax.sharding import PartitionSpec as P

NOPE = 128
ROPE = 64
VD = 128
KVR = 512
TOP = 6


EPSILON = 1e-06


def plain_dot(left_side, right_side):
    return jnp.dot(left_side, right_side, preferred_element_type=jnp.float32)


def lead_dot(left_side, right_side):
    return lax.dot_general(
        left_side, right_side, (((0,), (0,)), ((), ())), preferred_element_type=jnp.float32
    )


def tail_dot(left_side, right_side):
    return lax.dot_general(
        left_side, right_side, (((1,), (1,)), ((), ())), preferred_element_type=jnp.float32
    )


def normalize(values, gain_vector):
    factor = lax.rsqrt(jnp.mean(values * values, axis=-1, keepdims=True) + EPSILON)
    unit_rows = values * factor
    return (unit_rows * gain_vector, unit_rows, factor)


def norm_back(upstream, unit_rows, factor, gain_vector):
    scaled = upstream * gain_vector
    inner_mean = jnp.mean(scaled * unit_rows, axis=-1, keepdims=True)
    return (factor * (scaled - unit_rows * inner_mean), jnp.sum(upstream * unit_rows, axis=0))


def rope_tables(positions):
    half_width = ROPE // 2
    frequency = 10000.0 ** (-2.0 * jnp.arange(half_width, dtype=jnp.float32) / ROPE)
    angles = positions.astype(jnp.float32)[:, None] * frequency[None, :]
    return (jnp.cos(angles), jnp.sin(angles))


def rotate(values, cosine, sine_table):
    half_width = values.shape[-1] // 2
    front_half = values[..., :half_width]
    back_half = values[..., half_width:]
    return jnp.concatenate(
        [
            front_half * cosine - back_half * sine_table,
            back_half * cosine + front_half * sine_table,
        ],
        axis=-1,
    )


def rotate_back(values, cosine, sine_table):
    half_width = values.shape[-1] // 2
    front_half = values[..., :half_width]
    back_half = values[..., half_width:]
    return jnp.concatenate(
        [
            front_half * cosine + back_half * sine_table,
            back_half * cosine - front_half * sine_table,
        ],
        axis=-1,
    )


BOTH = ("expert", "tensor")


def visible_mask(positions, length):
    rows = jnp.arange(length, dtype=jnp.int32)
    starts = rows - positions
    return (rows[None, :] <= rows[:, None]) & (rows[None, :] >= starts[:, None])


def gather_rows(rows):
    return lax.all_gather(rows, BOTH, axis=0, tiled=True)


def scatter_rows(rows):
    return lax.psum_scatter(rows, BOTH, scatter_dimension=0, tiled=True)


def expert_table(routes, values, expert_total):
    ids = jnp.arange(expert_total, dtype=jnp.int32)
    table = jnp.zeros((routes.shape[0], expert_total), jnp.float32)
    for member in range(TOP):
        table = table + jnp.where(
            routes[:, member : member + 1] == ids[None, :], values[:, member : member + 1], 0.0
        )
    return table


MESH = pl.DeviceIdType.MESH
LANES = 128
LAYERS = 4
EPS = EPSILON


def dot_rows(left_side, right_side):
    return lax.dot_general(
        left_side, right_side, (((1,), (1,)), ((), ())), preferred_element_type=jnp.float32
    )


def dot_plain(left_side, right_side):
    return jnp.dot(left_side, right_side, preferred_element_type=jnp.float32)


class Place:
    def __init__(self, groups, tensors):
        self.groups = groups
        self.tensors = tensors
        self.layers = min(LAYERS, groups)
        self.lanes = groups // self.layers
        self.sides = tensors // 2
        self.me = lax.axis_index("expert")
        self.mine = lax.axis_index("tensor")
        self.layer = self.me // self.lanes
        self.lane = self.me % self.lanes
        self.side = self.mine // 2
        self.core = self.mine % 2
        self.sibling = self.side * 2 + (1 - self.core)

    def side_of(self, shift):
        return (self.side + shift) % self.sides

    def tensor_of(self, shift):
        return self.side_of(shift) * 2 + self.core

    def expert_of(self, layer_shift, lane_shift):
        return ((self.layer + layer_shift) % self.layers) * self.lanes + (
            self.lane + lane_shift
        ) % self.lanes

    def greet(self, peers):
        barrier = pltpu.get_barrier_semaphore()
        count = self.sides
        if peers:
            count = count + self.layers + self.lanes - 2
            partners = [self.expert_of(shift, 0) for shift in range(1, self.layers)]
            partners += [self.expert_of(0, shift) for shift in range(1, self.lanes)]
            for partner in partners:
                pl.semaphore_signal(
                    barrier, inc=1, device_id={"expert": partner}, device_id_type=MESH
                )
        for shift in range(1, self.sides):
            pl.semaphore_signal(
                barrier, inc=1, device_id={"tensor": self.tensor_of(shift)}, device_id_type=MESH
            )
        pl.semaphore_signal(
            barrier, inc=1, device_id={"tensor": self.sibling}, device_id_type=MESH
        )
        return barrier, count


def remote(source, target, send_sem, recv_sem, axis, index):
    return pltpu.make_async_remote_copy(
        src_ref=source,
        dst_ref=target,
        send_sem=send_sem,
        recv_sem=recv_sem,
        device_id={axis: index},
        device_id_type=MESH,
    )


def sum_over_tensor(place, terms, core_land, side_send, side_land, sems):
    core_send_sem, core_land_sem, side_send_sem, side_land_sem = sems
    core_copy = remote(
        terms.at[:, 1 - place.core],
        core_land,
        core_send_sem,
        core_land_sem,
        "tensor",
        place.sibling,
    )
    core_copy.start()
    core_copy.wait_recv()
    copies = []
    for shift in range(1, place.sides):
        other = place.side_of(shift)
        side_send[shift - 1] = (
            terms[other, place.core].astype(jnp.float32) + core_land[other].astype(jnp.float32)
        ).astype(jnp.bfloat16)
        copy = remote(
            side_send.at[shift - 1],
            side_land.at[shift - 1],
            side_send_sem.at[shift - 1],
            side_land_sem.at[shift - 1],
            "tensor",
            place.tensor_of(shift),
        )
        copy.start()
        copies.append(copy)
    total = terms[place.side, place.core].astype(jnp.float32) + core_land[place.side].astype(
        jnp.float32
    )
    for copy in copies:
        copy.wait_recv()
    for shift in range(1, place.sides):
        total = total + side_land[shift - 1].astype(jnp.float32)
    core_copy.wait_send()
    for copy in copies:
        copy.wait_send()
    return total


def spread_over_tensor(place, part, whole, sems):
    own_sem, side_sem, core_sem, arrive_sem = sems
    own_copy = pltpu.make_async_copy(part, whole.at[place.mine], own_sem)
    own_copy.start()
    sends = []
    for shift in range(1, place.sides):
        sends.append(
            remote(
                part,
                whole.at[place.mine],
                side_sem.at[shift],
                arrive_sem.at[place.mine],
                "tensor",
                place.tensor_of(shift),
            )
        )
    sends.append(
        remote(
            part,
            whole.at[place.mine],
            core_sem.at[0],
            arrive_sem.at[place.mine],
            "tensor",
            place.sibling,
        )
    )
    for copy in sends:
        copy.start()

    def wait_piece(tensor):
        view = whole.at[tensor]
        pltpu.make_async_copy(view, view, arrive_sem.at[tensor]).wait()

    for shift in range(1, place.sides):
        tensor = place.tensor_of(shift)
        wait_piece(tensor)
        copy = remote(
            whole.at[tensor],
            whole.at[tensor],
            core_sem.at[shift],
            arrive_sem.at[tensor],
            "tensor",
            place.sibling,
        )
        copy.start()
        sends.append(copy)
    for shift in range(place.sides):
        wait_piece(place.side_of(shift) * 2 + (1 - place.core))
    own_copy.wait()
    for copy in sends:
        copy.wait_send()


def forward_kernel(
    attention_ref,
    inputs_ref,
    gain_ref,
    gate_ref,
    up_ref,
    shared_gate_ref,
    shared_up_ref,
    router_ref,
    rows_ref,
    acts_ref,
    logits_ref,
    residual_ref,
    gate_w,
    up_w,
    shared_gate_w,
    shared_up_w,
    router_w,
    terms_buf,
    core_land,
    side_send,
    side_land,
    inputs_buf,
    part_buf,
    rows_buf,
    logits_buf,
    acts_buf,
    weight_sem,
    first_sem,
    load_sem,
    store_sem,
    sum_core_sem,
    sum_core_land_sem,
    sum_side_sem,
    sum_side_land_sem,
    layer_sem,
    layer_land_sem,
    lane_sem,
    lane_land_sem,
    side_sem,
    side_land_sem,
    lane_half_sem,
    lane_half_land_sem,
    side_half_sem,
    side_half_land_sem,
    core_sem,
    core_land_sem,
    *,
    groups,
    tensors,
):
    place = Place(groups, tensors)
    sides, layers, lanes = place.sides, place.layers, place.lanes
    me, mine, core = place.me, place.mine, place.core
    length = rows_buf.shape[1]
    width = rows_buf.shape[2]
    half = width // 2
    part_rows = length // tensors
    row_block = min(256, length)

    pairs = (
        (gate_ref, gate_w),
        (up_ref, up_w),
        (shared_gate_ref, shared_gate_w),
        (shared_up_ref, shared_up_w),
        (router_ref, router_w),
    )
    first_copies = (
        pltpu.make_async_copy(attention_ref, terms_buf, first_sem.at[0]),
        pltpu.make_async_copy(
            inputs_ref.at[pl.ds(pl.multiple_of(mine * part_rows, part_rows), part_rows), :],
            inputs_buf,
            first_sem.at[1],
        ),
    )
    for copy in first_copies:
        copy.start()
    weight_copies = [
        pltpu.make_async_copy(source, target, weight_sem.at[index])
        for index, (source, target) in enumerate(pairs)
    ]
    barrier, count = place.greet(True)

    def sequence_of(step):
        return place.expert_of(step // lanes, step % lanes)

    def load_copy(step):
        slot = step % 2
        return pltpu.make_async_copy(
            rows_ref.at[sequence_of(step)], rows_buf.at[slot], load_sem.at[slot]
        )

    def store_copies(step):
        slot = step % 2
        sequence = sequence_of(step)
        return (
            pltpu.make_async_copy(
                acts_buf.at[slot], acts_ref.at[:, sequence], store_sem.at[slot, 0]
            ),
            pltpu.make_async_copy(
                logits_buf.at[slot], logits_ref.at[sequence], store_sem.at[slot, 1]
            ),
        )

    def piece(layer_shift, lane_shift, tensor, columns=None):
        rows = pl.ds(pl.multiple_of(tensor * part_rows, part_rows), part_rows)
        sequence = place.expert_of(layer_shift, lane_shift)
        if columns is None:
            return rows_ref.at[sequence, rows, :]
        return rows_ref.at[sequence, rows, pl.ds(columns * half, half)]

    def await_bytes(view, sem):
        pltpu.make_async_copy(view, view, sem).wait()

    def layer_spread(shift):
        return remote(
            part_buf,
            piece(0, 0, mine),
            layer_sem.at[shift],
            layer_land_sem.at[shift],
            "expert",
            place.expert_of(layers - shift, 0),
        )

    def lane_spread(layer_shift, shift):
        view = piece(layer_shift, 0, mine)
        return remote(
            view,
            view,
            lane_sem.at[layer_shift, shift],
            lane_land_sem.at[layer_shift, shift],
            "expert",
            place.expert_of(0, lanes - shift),
        )

    def side_spread(layer_shift, shift):
        view = piece(layer_shift, 0, mine)
        return remote(
            view,
            view,
            side_sem.at[layer_shift, shift],
            side_land_sem.at[layer_shift, shift],
            "tensor",
            place.tensor_of(sides - shift),
        )

    def side_half_spread(layer_shift, lane_shift, shift):
        view = piece(layer_shift, lane_shift, mine, 0)
        return remote(
            view,
            view,
            side_half_sem.at[layer_shift, lane_shift, shift],
            side_half_land_sem.at[layer_shift, lane_shift, shift],
            "tensor",
            place.tensor_of(sides - shift),
        )

    def lane_half_spread(layer_shift, shift, side_shift):
        view = piece(layer_shift, 0, place.tensor_of(side_shift), 1)
        return remote(
            view,
            view,
            lane_half_sem.at[layer_shift, shift, side_shift],
            lane_half_land_sem.at[layer_shift, shift, side_shift],
            "expert",
            place.expert_of(0, lanes - shift),
        )

    def core_spread(layer_shift, lane_shift, side_shift):
        view = piece(layer_shift, lane_shift, place.tensor_of(side_shift))
        return remote(
            view,
            view,
            core_sem.at[layer_shift, lane_shift, side_shift],
            core_land_sem.at[layer_shift, lane_shift, side_shift],
            "tensor",
            place.sibling,
        )

    def first_hop(layer_shift, landed):
        if landed:
            await_bytes(piece(layer_shift, 0, mine), layer_land_sem.at[layer_shift])
        for shift in range(1, sides):
            side_spread(layer_shift, shift).start()
        for shift in range(1, lanes):
            lane_spread(layer_shift, shift).start()
        core_spread(layer_shift, 0, 0).start()

    def second_hop(layer_shift):
        for shift in range(1, sides):
            await_bytes(
                piece(layer_shift, 0, place.tensor_of(shift)),
                side_land_sem.at[layer_shift, shift],
            )
            core_spread(layer_shift, 0, shift).start()
            for lane_shift in range(1, lanes):
                lane_half_spread(layer_shift, lane_shift, shift).start()
        for lane_shift in range(1, lanes):
            await_bytes(
                piece(layer_shift, lane_shift, mine), lane_land_sem.at[layer_shift, lane_shift]
            )
            for shift in range(1, sides):
                side_half_spread(layer_shift, lane_shift, shift).start()
            core_spread(layer_shift, lane_shift, 0).start()

    def third_hop(layer_shift):
        for lane_shift in range(1, lanes):
            for shift in range(1, sides):
                tensor = place.tensor_of(shift)
                await_bytes(
                    piece(layer_shift, lane_shift, tensor, 0),
                    side_half_land_sem.at[layer_shift, lane_shift, shift],
                )
                await_bytes(
                    piece(layer_shift, lane_shift, tensor, 1),
                    lane_half_land_sem.at[layer_shift, lane_shift, shift],
                )
                core_spread(layer_shift, lane_shift, shift).start()

    def await_sibling(step):
        layer_shift = step // lanes
        lane_shift = step % lanes
        for shift in range(sides):
            tensor = place.side_of(shift) * 2 + (1 - core)
            await_bytes(
                piece(layer_shift, lane_shift, tensor),
                core_land_sem.at[layer_shift, lane_shift, shift],
            )

    for copy in first_copies:
        copy.wait()
    pl.semaphore_wait(barrier, count)
    for copy in weight_copies:
        copy.start()
    attention = sum_over_tensor(
        place,
        terms_buf,
        core_land,
        side_send,
        side_land,
        (sum_core_sem, sum_core_land_sem, sum_side_sem, sum_side_land_sem),
    )
    residual = inputs_buf[...].astype(jnp.float32) + attention
    residual_ref[...] = residual
    factor = lax.rsqrt(jnp.mean(residual * residual, axis=1, keepdims=True) + EPS)
    part_buf[...] = (residual * factor * gain_ref[...]).astype(jnp.bfloat16)

    own_copy = pltpu.make_async_copy(part_buf, piece(0, 0, mine), first_sem.at[2])
    own_copy.start()
    for shift in range(1, layers):
        layer_spread(shift).start()
    own_copy.wait()
    first_hop(0, False)
    second_hop(0)
    await_sibling(0)
    load_copy(0).start()
    for copy in weight_copies:
        copy.wait()

    def step_body(step, carry):
        slot = step % 2
        layer_shift = step // lanes
        lane_shift = step % lanes
        load_copy(step).wait()

        @pl.when(step > 1)
        def _():
            for copy in store_copies(step - 2):
                copy.wait()

        logits_buf[slot] = dot_plain(rows_buf[slot], router_w[...])

        def hidden_rows(block, inner):
            rows = pl.ds(pl.multiple_of(block * row_block, row_block), row_block)
            here = rows_buf[slot, rows, :]
            for index, weight in ((0, gate_w), (1, up_w)):
                acts_buf[slot, index, rows, :] = dot_rows(here, weight[...]).astype(jnp.bfloat16)
            return inner

        lax.fori_loop(0, length // row_block, hidden_rows, 0)

        @pl.when(lane_shift == 0)
        def _():
            third_hop(layer_shift)

            @pl.when(layer_shift + 1 < layers)
            def _():
                first_hop(layer_shift + 1, True)

        @pl.when((lane_shift == lanes - 1) & (layer_shift + 1 < layers))
        def _():
            second_hop(layer_shift + 1)

        def shared_rows(block, inner):
            rows = pl.ds(pl.multiple_of(block * row_block, row_block), row_block)
            here = rows_buf[slot, rows, :]
            for index, weight in ((2, shared_gate_w), (3, shared_up_w)):
                acts_buf[slot, index, rows, :] = dot_rows(here, weight[...]).astype(jnp.bfloat16)
            return inner

        lax.fori_loop(0, length // row_block, shared_rows, 0)

        @pl.when(step + 1 < groups)
        def _():
            await_sibling(step + 1)
            load_copy(step + 1).start()

        for copy in store_copies(step):
            copy.start()
        return carry

    lax.fori_loop(0, groups, step_body, 0)

    for step in range(max(groups - 2, 0), groups):
        for copy in store_copies(step):
            copy.wait()
    for shift in range(1, layers):
        layer_spread(shift).wait_send()
    for layer_shift in range(layers):
        for shift in range(1, sides):
            side_spread(layer_shift, shift).wait_send()
        for lane_shift in range(lanes):
            if lane_shift > 0:
                lane_spread(layer_shift, lane_shift).wait_send()
                for shift in range(1, sides):
                    side_half_spread(layer_shift, lane_shift, shift).wait_send()
                    lane_half_spread(layer_shift, lane_shift, shift).wait_send()
            for shift in range(sides):
                core_spread(layer_shift, lane_shift, shift).wait_send()


def backward_kernel(
    cotangent_ref,
    acts_ref,
    logits_ref,
    gate_ref,
    up_ref,
    down_ref,
    shared_gate_ref,
    shared_up_ref,
    shared_down_ref,
    router_ref,
    residual_ref,
    gain_ref,
    expert_hidden_ref,
    expert_dpre_ref,
    expert_dlin_ref,
    shared_hidden_ref,
    shared_dpre_ref,
    shared_dlin_ref,
    spread_ref,
    result_ref,
    grad_residual_ref,
    logit_ref,
    gain_grad_ref,
    gate_w,
    up_w,
    down_w,
    shared_gate_w,
    shared_up_w,
    shared_down_w,
    router_w,
    cotangent_buf,
    acts_buf,
    logits_buf,
    codes_buf,
    units_buf,
    gate_grad_buf,
    sum_buf,
    core_land,
    side_land,
    lane_send,
    lane_land,
    block_land,
    block_send,
    block_side_land,
    layer_send,
    layer_land,
    cotangent_part,
    code_part,
    gates_part,
    part_buf,
    weight_sem,
    load_sem,
    store_sem,
    part_sem,
    core_sem,
    core_land_sem,
    side_sem,
    side_land_sem,
    lane_sem,
    lane_land_sem,
    block_sem,
    block_land_sem,
    block_side_sem,
    block_side_land_sem,
    layer_sem,
    layer_land_sem,
    own_sem,
    spread_side_sem,
    spread_core_sem,
    arrive_sem,
    *,
    groups,
    tensors,
    local_experts,
):
    place = Place(groups, tensors)
    sides, layers, lanes = place.sides, place.layers, place.lanes
    me, mine, core, side = place.me, place.mine, place.core, place.side
    length = cotangent_buf.shape[0]
    width = cotangent_buf.shape[1]
    part_rows = length // tensors
    hidden = gate_w.shape[0]
    own_width = hidden // local_experts
    row_block = min(256, length)
    column_block = min(512, width)
    first = pl.ds(0, width)
    second = pl.ds(width, width + LANES)
    marks = pl.ds(width, LANES)

    pairs = (
        (down_ref, down_w),
        (shared_down_ref, shared_down_w),
        (gate_ref, gate_w),
        (up_ref, up_w),
        (shared_gate_ref, shared_gate_w),
        (shared_up_ref, shared_up_w),
        (router_ref, router_w),
    )
    weight_copies = [
        pltpu.make_async_copy(source, target, weight_sem.at[index])
        for index, (source, target) in enumerate(pairs)
    ]

    def shifts_of(step):
        return (step // lanes + 1) % layers, lanes - 1 - step % lanes

    def sequence_of(step):
        layer_shift, lane_shift = shifts_of(step)
        return place.expert_of(layer_shift, lane_shift)

    def load_copies(step):
        sequence = sequence_of(step)
        return (
            pltpu.make_async_copy(
                cotangent_ref.at[sequence, :, first], cotangent_buf, load_sem.at[0]
            ),
            pltpu.make_async_copy(acts_ref.at[:, sequence], acts_buf, load_sem.at[1]),
            pltpu.make_async_copy(logits_ref.at[sequence], logits_buf, load_sem.at[2]),
            pltpu.make_async_copy(cotangent_ref.at[sequence, :, marks], codes_buf, load_sem.at[3]),
        )

    unit_refs = (
        expert_hidden_ref,
        expert_dpre_ref,
        expert_dlin_ref,
        shared_hidden_ref,
        shared_dpre_ref,
        shared_dlin_ref,
    )

    def store_copies(step):
        sequence = sequence_of(step)
        return [
            pltpu.make_async_copy(units_buf.at[index], ref.at[sequence], store_sem.at[index])
            for index, ref in enumerate(unit_refs)
        ]

    part_slice = pl.ds(pl.multiple_of(mine * part_rows, part_rows), part_rows)
    part_copies = (
        pltpu.make_async_copy(
            cotangent_ref.at[me, part_slice, first], cotangent_part, part_sem.at[0]
        ),
        pltpu.make_async_copy(cotangent_ref.at[me, part_slice, marks], code_part, part_sem.at[1]),
        pltpu.make_async_copy(logits_ref.at[me, part_slice, :], gates_part, part_sem.at[2]),
    )
    for copy in load_copies(0):
        copy.start()
    for copy in weight_copies:
        copy.start()
    for copy in part_copies:
        copy.start()
    barrier, count = place.greet(True)

    def core_send(step):
        slot = step % 2
        return remote(
            sum_buf.at[slot, :, 1 - core],
            core_land.at[slot],
            core_sem.at[slot],
            core_land_sem.at[slot],
            "tensor",
            place.sibling,
        )

    def side_copy(step, shift):
        slot = step % 2
        return remote(
            sum_buf.at[slot, place.side_of(shift), core, :, first],
            side_land.at[slot, shift - 1],
            side_sem.at[slot, shift - 1],
            side_land_sem.at[slot, shift - 1],
            "tensor",
            place.tensor_of(shift),
        )

    def lane_copy(turn, lane_shift):
        slot = turn % 2
        return remote(
            lane_send.at[slot, lane_shift - 1],
            lane_land.at[slot, lane_shift - 1],
            lane_sem.at[slot, lane_shift - 1],
            lane_land_sem.at[slot, lane_shift - 1],
            "expert",
            place.expert_of(0, lane_shift),
        )

    def block_copy(step, lane_shift):
        slot = step % 2
        turn_slot = (step // lanes) % 2
        return remote(
            sum_buf.at[slot, :, core, :, second],
            block_land.at[turn_slot, lane_shift - 1],
            block_sem.at[slot],
            block_land_sem.at[turn_slot, lane_shift - 1],
            "expert",
            place.expert_of(0, lane_shift),
        )

    def block_side_copy(turn, shift):
        slot = turn % 2
        return remote(
            block_send.at[slot, shift - 1],
            block_side_land.at[slot, shift - 1],
            block_side_sem.at[slot, shift - 1],
            block_side_land_sem.at[slot, shift - 1],
            "tensor",
            place.tensor_of(shift),
        )

    def layer_copy(turn):
        slot = turn % 2
        return remote(
            layer_send.at[slot],
            layer_land.at[turn],
            layer_sem.at[slot],
            layer_land_sem.at[turn],
            "expert",
            place.expert_of((turn + 1) % layers, 0),
        )

    def per_lane(lane_shift, act):
        for value in range(1, lanes):

            @pl.when(lane_shift == value)
            def _():
                act(value)

    def combine_cores(step):
        slot = step % 2
        _, lane_shift = shifts_of(step)
        copy = core_send(step)
        copy.wait_recv()
        copy.wait_send()
        for shift in range(sides):
            other = place.side_of(shift)
            sum_buf[slot, other, core] = (
                sum_buf[slot, other, core].astype(jnp.float32)
                + core_land[slot, other].astype(jnp.float32)
            ).astype(jnp.bfloat16)
            if shift > 0:
                side_copy(step, shift).start()
        per_lane(lane_shift, lambda value: block_copy(step, value).start())

    def combine_sides(step):
        slot = step % 2
        turn = step // lanes
        _, lane_shift = shifts_of(step)
        total = sum_buf[slot, side, core, :, first].astype(jnp.float32)
        for shift in range(1, sides):
            side_copy(step, shift).wait_recv()
            side_copy(step, shift).wait_send()
            total = total + side_land[slot, shift - 1].astype(jnp.float32)
        total = total.astype(jnp.bfloat16)

        def pass_on(value):
            block_copy(step, value).wait_send()

            @pl.when(turn >= 2)
            def _():
                lane_copy(turn - 2, value).wait_send()

            lane_send[turn % 2, value - 1] = total
            lane_copy(turn, value).start()

        per_lane(lane_shift, pass_on)

        @pl.when(lane_shift == 0)
        def _():
            turn_slot = turn % 2

            @pl.when(turn >= 2)
            def _():
                layer_copy(turn - 2).wait_send()
                for shift in range(1, sides):
                    block_side_copy(turn - 2, shift).wait_send()

            layer_send[turn_slot, :, first] = total
            for value in range(1, lanes):
                block_copy(step, value).wait_recv()
            for shift in range(sides):
                other = place.side_of(shift)
                block = sum_buf[slot, other, core, :, second].astype(jnp.float32)
                for value in range(1, lanes):
                    block = block + block_land[turn_slot, value - 1, other].astype(jnp.float32)
                block = block.astype(jnp.bfloat16)
                if shift == 0:
                    layer_send[turn_slot, :, second] = block
                else:
                    block_send[turn_slot, shift - 1] = block
                    block_side_copy(turn, shift).start()

    def turn_total(turn):
        slot = turn % 2
        branch = layer_send[slot, :, first].astype(jnp.float32)
        for value in range(1, lanes):
            lane_copy(turn, value).wait_recv()
            branch = branch + lane_land[slot, value - 1].astype(jnp.float32)
        block = layer_send[slot, :, second].astype(jnp.float32)
        for shift in range(1, sides):
            block_side_copy(turn, shift).wait_recv()
            block = block + block_side_land[slot, shift - 1].astype(jnp.float32)
        return branch, block

    def combine_lanes(step):
        turn = step // lanes
        _, lane_shift = shifts_of(step)

        @pl.when(lane_shift == 0)
        def _():
            slot = turn % 2
            branch, block = turn_total(turn)
            layer_send[slot, :, first] = branch.astype(jnp.bfloat16)
            layer_send[slot, :, second] = block.astype(jnp.bfloat16)
            layer_copy(turn).start()

    for copy in weight_copies[:2]:
        copy.wait()
    for copy in part_copies:
        copy.wait()
    pl.semaphore_wait(barrier, count)

    def softmax_named(logits, code):
        named = code > 0.5
        highest = jnp.max(jnp.where(named, logits, -jnp.inf), axis=1, keepdims=True)
        raised = jnp.where(named, jnp.exp(logits - highest), 0.0)
        return raised / jnp.sum(raised, axis=1, keepdims=True)

    def services(step):
        @pl.when((step >= 3) & (step < groups + 2))
        def _():
            combine_lanes(step - 3)

        @pl.when((step >= 2) & (step < groups + 2))
        def _():
            combine_sides(step - 2)

        @pl.when((step >= 1) & (step < groups + 1))
        def _():
            combine_cores(step - 1)

    def step_body(step, carry):
        slot = step % 2
        running = step < groups

        @pl.when(running)
        def _():
            for copy in load_copies(step):
                copy.wait()

            @pl.when(step > 0)
            def _():
                for copy in store_copies(step - 1):
                    copy.wait()

            def hidden_rows(block, inner):
                rows = pl.ds(pl.multiple_of(block * row_block, row_block), row_block)
                back = cotangent_buf[rows, :]
                dhid = dot_rows(back, down_w[...])
                code = codes_buf[rows, :].astype(jnp.float32)
                lane = lax.broadcasted_iota(jnp.int32, code.shape, 1)
                gates = softmax_named(logits_buf[rows, :], code)
                gates = jnp.where(code > 1.5, gates, 0.0)
                pre = acts_buf[0, rows, :].astype(jnp.float32)
                lin = acts_buf[1, rows, :].astype(jnp.float32)
                unit = lax.broadcasted_iota(jnp.int32, pre.shape, 1)
                gate = None
                for member in range(local_experts):
                    chosen = jnp.sum(
                        jnp.where(lane == me * local_experts + member, gates, 0.0),
                        axis=1,
                        keepdims=True,
                    )
                    gate = (
                        jnp.broadcast_to(chosen, pre.shape)
                        if gate is None
                        else jnp.where(unit >= member * own_width, chosen, gate)
                    )
                sigmoid = jax.nn.sigmoid(pre)
                active = pre * sigmoid
                hid = active * lin
                product = hid * dhid
                units_buf[0, rows, :] = (hid * gate).astype(jnp.bfloat16)
                dhid = dhid * gate
                units_buf[1, rows, :] = (dhid * lin * (sigmoid + active * (1.0 - sigmoid))).astype(
                    jnp.bfloat16
                )
                units_buf[2, rows, :] = (dhid * active).astype(jnp.bfloat16)
                gate_grad = jnp.zeros(code.shape, jnp.float32)
                for member in range(local_experts):
                    inside = (unit >= member * own_width) & (unit < (member + 1) * own_width)
                    gate_grad = jnp.where(
                        lane == me * local_experts + member,
                        jnp.sum(jnp.where(inside, product, 0.0), axis=1, keepdims=True),
                        gate_grad,
                    )
                gate_grad_buf[rows, :] = gate_grad
                return inner

            lax.fori_loop(0, length // row_block, hidden_rows, 0)

            def shared_rows(block, inner):
                rows = pl.ds(pl.multiple_of(block * row_block, row_block), row_block)
                dhid = dot_rows(cotangent_buf[rows, :], shared_down_w[...])
                pre = acts_buf[2, rows, :].astype(jnp.float32)
                lin = acts_buf[3, rows, :].astype(jnp.float32)
                sigmoid = jax.nn.sigmoid(pre)
                active = pre * sigmoid
                units_buf[3, rows, :] = (active * lin).astype(jnp.bfloat16)
                units_buf[4, rows, :] = (dhid * lin * (sigmoid + active * (1.0 - sigmoid))).astype(
                    jnp.bfloat16
                )
                units_buf[5, rows, :] = (dhid * active).astype(jnp.bfloat16)
                return inner

            lax.fori_loop(0, length // row_block, shared_rows, 0)

            @pl.when(step + 1 < groups)
            def _():
                for copy in load_copies(step + 1):
                    copy.start()

            @pl.when(step == 0)
            def _():
                for copy in weight_copies[2:]:
                    copy.wait()

        services(step)

        @pl.when(running)
        def _():
            def mix_columns(block, inner):
                start = pl.multiple_of(block * column_block, column_block)
                columns = pl.ds(start, column_block)
                moved = pl.ds(pl.multiple_of(width + start, column_block), column_block)
                sum_buf[slot, :, :, :, columns] = (
                    dot_plain(units_buf[0], down_w[:, columns])
                    .astype(jnp.bfloat16)
                    .reshape(sides, 2, part_rows, column_block)
                )
                total = dot_plain(units_buf[1], gate_w[:, columns]) + dot_plain(
                    units_buf[2], up_w[:, columns]
                )
                sum_buf[slot, :, :, :, moved] = total.astype(jnp.bfloat16).reshape(
                    sides, 2, part_rows, column_block
                )
                return inner

            lax.fori_loop(0, width // column_block, mix_columns, 0)

            @pl.when(step == groups - 1)
            def _():
                def mix_shared(block, inner):
                    start = pl.multiple_of(block * column_block, column_block)
                    columns = pl.ds(start, column_block)
                    moved = pl.ds(pl.multiple_of(width + start, column_block), column_block)
                    for target, total in (
                        (columns, dot_plain(units_buf[3], shared_down_w[:, columns])),
                        (
                            moved,
                            dot_plain(units_buf[4], shared_gate_w[:, columns])
                            + dot_plain(units_buf[5], shared_up_w[:, columns]),
                        ),
                    ):
                        sum_buf[slot, :, :, :, target] = (
                            sum_buf[slot, :, :, :, target].astype(jnp.float32)
                            + total.reshape(sides, 2, part_rows, column_block)
                        ).astype(jnp.bfloat16)
                    return inner

                lax.fori_loop(0, width // column_block, mix_shared, 0)

            sum_buf[slot, :, :, :, pl.ds(2 * width, LANES)] = (
                gate_grad_buf[...].astype(jnp.bfloat16).reshape(sides, 2, part_rows, LANES)
            )
            core_send(step).start()
            for copy in store_copies(step):
                copy.start()

        return carry

    lax.fori_loop(0, groups + 2, step_body, 0)

    last = layers - 1
    last_slot = last % 2
    for value in range(1, lanes):
        lane_copy(last, value).wait_recv()
    for shift in range(1, sides):
        block_side_copy(last, shift).wait_recv()
    for turn in range(last):
        layer_copy(turn).wait_recv()
    gain_grad_ref[...] = jnp.zeros_like(gain_grad_ref)
    few_rows = min(32, part_rows)

    def finish_rows(index, inner):
        rows = pl.ds(pl.multiple_of(index * few_rows, few_rows), few_rows)
        branch = layer_send[last_slot, rows, first].astype(jnp.float32)
        for value in range(1, lanes):
            branch = branch + lane_land[last_slot, value - 1, rows, :].astype(jnp.float32)
        block = layer_send[last_slot, rows, second].astype(jnp.float32)
        for shift in range(1, sides):
            block = block + block_side_land[last_slot, shift - 1, rows, :].astype(jnp.float32)
        for turn in range(last):
            branch = branch + layer_land[turn, rows, first].astype(jnp.float32)
            block = block + layer_land[turn, rows, second].astype(jnp.float32)
        residual = residual_ref[rows, :]
        result_ref[rows, :] = (residual + branch).astype(jnp.bfloat16)

        code = code_part[rows, :].astype(jnp.float32)
        gates = softmax_named(gates_part[rows, :], code)
        gate_grad = jnp.where(code > 1.5, block[:, width:], 0.0)
        logit = (
            gates * (gate_grad - jnp.sum(gates * gate_grad, axis=1, keepdims=True))
        ).astype(jnp.bfloat16)
        logit_ref[rows, :] = logit
        upstream = block[:, :width] + dot_rows(logit, router_w[...])
        factor = lax.rsqrt(jnp.mean(residual * residual, axis=1, keepdims=True) + EPS)
        unit_rows = residual * factor
        scaled = upstream * gain_ref[...]
        inner_mean = jnp.mean(scaled * unit_rows, axis=1, keepdims=True)
        gain_grad_ref[...] += jnp.sum(upstream * unit_rows, axis=0, keepdims=True)
        grad_residual = cotangent_part[rows, :].astype(jnp.float32) + factor * (
            scaled - unit_rows * inner_mean
        )
        grad_residual_ref[rows, :] = grad_residual
        part_buf[rows, :] = grad_residual.astype(jnp.bfloat16)
        return inner

    lax.fori_loop(0, part_rows // few_rows, finish_rows, 0)
    spread_over_tensor(
        place, part_buf, spread_ref, (own_sem, spread_side_sem, spread_core_sem, arrive_sem)
    )

    for copy in store_copies(groups - 1):
        copy.wait()
    for turn in range(max(layers - 2, 0), layers):
        for value in range(1, lanes):
            lane_copy(turn, value).wait_send()
        for shift in range(1, sides):
            block_side_copy(turn, shift).wait_send()
    layer_copy(last - 1).wait_send()


ANYWHERE = pl.BlockSpec(memory_space=pl.ANY)
IN_VMEM = pl.BlockSpec(memory_space=pltpu.VMEM)


def run_forward(attention, inputs, gain, weights, router_padded):
    groups = lax.axis_size("expert")
    tensors = lax.axis_size("tensor")
    sides = tensors // 2
    layers = min(LAYERS, groups)
    lanes = groups // layers
    length, width = inputs.shape
    part_rows = length // tensors
    hidden = weights[0].shape[0]
    bf16 = jnp.bfloat16
    f32 = jnp.float32
    dma = pltpu.SemaphoreType.DMA
    block = pltpu.VMEM((hidden, width), bf16)
    return pl.pallas_call(
        functools.partial(forward_kernel, groups=groups, tensors=tensors),
        out_shape=(
            jax.ShapeDtypeStruct((groups, length, width), bf16),
            jax.ShapeDtypeStruct((4, groups, length, hidden), bf16),
            jax.ShapeDtypeStruct((groups, length, LANES), f32),
            jax.ShapeDtypeStruct((part_rows, width), f32),
        ),
        in_specs=[ANYWHERE, ANYWHERE, IN_VMEM] + [ANYWHERE] * 5,
        out_specs=(ANYWHERE,) * 3 + (IN_VMEM,),
        scratch_shapes=[block] * 4
        + [
            pltpu.VMEM((width, LANES), bf16),
            pltpu.VMEM((sides, 2, part_rows, width), bf16),
            pltpu.VMEM((sides, part_rows, width), bf16),
            pltpu.VMEM((sides - 1, part_rows, width), bf16),
            pltpu.VMEM((sides - 1, part_rows, width), bf16),
            pltpu.VMEM((part_rows, width), bf16),
            pltpu.VMEM((part_rows, width), bf16),
            pltpu.VMEM((2, length, width), bf16),
            pltpu.VMEM((2, length, LANES), f32),
            pltpu.VMEM((2, 4, length, hidden), bf16),
            dma((5,)),
            dma((3,)),
            dma((2,)),
            dma((2, 2)),
            dma(()),
            dma(()),
            dma((sides - 1,)),
            dma((sides - 1,)),
            dma((layers,)),
            dma((layers,)),
            dma((layers, lanes)),
            dma((layers, lanes)),
            dma((layers, sides)),
            dma((layers, sides)),
            dma((layers, lanes, sides)),
            dma((layers, lanes, sides)),
            dma((layers, lanes, sides)),
            dma((layers, lanes, sides)),
            dma((layers, lanes, sides)),
            dma((layers, lanes, sides)),
        ],
        compiler_params=pltpu.CompilerParams(
            collective_id=1, has_side_effects=True, vmem_limit_bytes=60 * 1024 * 1024
        ),
        cost_estimate=pl.CostEstimate(
            flops=8 * groups * length * width * hidden,
            bytes_accessed=100_000_000,
            transcendentals=0,
        ),
        name="experts_forward",
    )(
        attention.reshape(sides, 2, part_rows, width),
        inputs,
        gain.reshape(1, width),
        *weights,
        router_padded,
    )


def run_backward(
    cotangent_all, acts, logits, weights, router_padded, residual, gain, local_experts
):
    groups = lax.axis_size("expert")
    tensors = lax.axis_size("tensor")
    sides = tensors // 2
    layers = min(LAYERS, groups)
    lanes = groups // layers
    part_rows, width = residual.shape
    length = part_rows * tensors
    hidden = weights[0].shape[0]
    second = width + LANES
    packed = width + second
    bf16 = jnp.bfloat16
    f32 = jnp.float32
    dma = pltpu.SemaphoreType.DMA
    block = pltpu.VMEM((hidden, width), bf16)
    units = jax.ShapeDtypeStruct((groups, length, hidden), bf16)
    return pl.pallas_call(
        functools.partial(
            backward_kernel, groups=groups, tensors=tensors, local_experts=local_experts
        ),
        out_shape=(units,) * 6
        + (
            jax.ShapeDtypeStruct((tensors, part_rows, width), bf16),
            jax.ShapeDtypeStruct((part_rows, width), bf16),
            jax.ShapeDtypeStruct((part_rows, width), f32),
            jax.ShapeDtypeStruct((part_rows, LANES), bf16),
            jax.ShapeDtypeStruct((1, width), f32),
        ),
        in_specs=[ANYWHERE] * 10 + [IN_VMEM] * 2,
        out_specs=(ANYWHERE,) * 7 + (IN_VMEM,) * 4,
        scratch_shapes=[block] * 6
        + [
            pltpu.VMEM((width, LANES), bf16),
            pltpu.VMEM((length, width), bf16),
            pltpu.VMEM((4, length, hidden), bf16),
            pltpu.VMEM((length, LANES), f32),
            pltpu.VMEM((length, LANES), bf16),
            pltpu.VMEM((6, length, hidden), bf16),
            pltpu.VMEM((length, LANES), f32),
            pltpu.VMEM((2, sides, 2, part_rows, packed), bf16),
            pltpu.VMEM((2, sides, part_rows, packed), bf16),
            pltpu.VMEM((2, sides - 1, part_rows, width), bf16),
            pltpu.VMEM((2, lanes - 1, part_rows, width), bf16),
            pltpu.VMEM((2, lanes - 1, part_rows, width), bf16),
            pltpu.VMEM((2, lanes - 1, sides, part_rows, second), bf16),
            pltpu.VMEM((2, sides - 1, part_rows, second), bf16),
            pltpu.VMEM((2, sides - 1, part_rows, second), bf16),
            pltpu.VMEM((2, part_rows, packed), bf16),
            pltpu.VMEM((layers - 1, part_rows, packed), bf16),
            pltpu.VMEM((part_rows, width), bf16),
            pltpu.VMEM((part_rows, LANES), bf16),
            pltpu.VMEM((part_rows, LANES), f32),
            pltpu.VMEM((part_rows, width), bf16),
            dma((7,)),
            dma((4,)),
            dma((6,)),
            dma((3,)),
            dma((2,)),
            dma((2,)),
            dma((2, sides - 1)),
            dma((2, sides - 1)),
            dma((2, lanes - 1)),
            dma((2, lanes - 1)),
            dma((2,)),
            dma((2, lanes - 1)),
            dma((2, sides - 1)),
            dma((2, sides - 1)),
            dma((2,)),
            dma((layers - 1,)),
            dma(()),
            dma((sides,)),
            dma((sides,)),
            dma((tensors,)),
        ],
        compiler_params=pltpu.CompilerParams(
            collective_id=2, has_side_effects=True, vmem_limit_bytes=60 * 1024 * 1024
        ),
        cost_estimate=pl.CostEstimate(
            flops=10 * groups * length * width * hidden,
            bytes_accessed=100_000_000,
            transcendentals=0,
        ),
        name="experts_backward",
    )(
        cotangent_all.reshape(groups, length, width + LANES),
        acts,
        logits,
        *weights,
        router_padded,
        residual,
        gain.reshape(1, width),
    )


def weight_kernel(
    query_ref,
    latent_ref,
    out_ref,
    rest_ref,
    first_ref,
    residual_ref,
    inputs_ref,
    gain_ref,
    units_0,
    units_1,
    units_2,
    units_3,
    units_4,
    units_5,
    rows_ref,
    cotangent_ref,
    query_sum,
    latent_sum,
    out_sum,
    rest_spread,
    first_spread,
    grad_0,
    grad_1,
    grad_2,
    grad_3,
    grad_4,
    grad_5,
    query_own,
    latent_own,
    out_own,
    rest_own,
    query_lane,
    latent_lane,
    out_lane,
    rest_lane,
    query_layer,
    latent_layer,
    out_layer,
    rest_layer,
    rest_part,
    rest_block,
    first_core_land,
    first_send,
    first_land,
    first_part,
    sum_core_land,
    sum_send,
    sum_land,
    units_buf,
    turned_buf,
    rows_buf,
    grad_buf,
    own_sem,
    lane_sem,
    lane_land_sem,
    layer_sem,
    layer_land_sem,
    units_sem,
    rows_sem,
    grad_sem,
    spread_own_sem,
    spread_side_sem,
    spread_core_sem,
    arrive_sem,
    tensor_core_sem,
    tensor_core_land_sem,
    tensor_side_sem,
    tensor_side_land_sem,
    first_own_sem,
    first_side_sem,
    first_core_sem,
    first_arrive_sem,
    *,
    groups,
    tensors,
):
    place = Place(groups, tensors)
    layers, lanes = place.layers, place.lanes
    sides = place.sides
    columns = rest_part.shape[1]
    tokens = units_buf.shape[1]
    width = rows_ref.shape[1]
    column_block = rows_buf.shape[2]
    barrier, count = place.greet(True)

    sums = (query_sum, latent_sum, out_sum, None)
    owns = (query_own, latent_own, out_own, rest_own)
    lane_lands = (query_lane, latent_lane, out_lane, rest_lane)
    layer_lands = (query_layer, latent_layer, out_layer, rest_layer)

    def share(index, expert):
        if index == 0:
            return query_ref.at[expert]
        if index == 1:
            return latent_ref.at[expert]
        part = pl.ds(pl.multiple_of(expert * columns, columns), columns)
        return (out_ref if index == 2 else rest_block).at[:, part]

    def own_copies(turn, indices=range(4)):
        return [
            pltpu.make_async_copy(
                share(index, place.expert_of((turn + 1) % layers, 0)),
                owns[index].at[turn],
                own_sem.at[turn, index],
            )
            for index in indices
        ]

    def lane_copies(turn, indices=range(4)):
        return [
            remote(
                share(index, place.expert_of((turn + 1) % layers, shift)),
                lane_lands[index].at[turn, shift - 1],
                lane_sem.at[turn, shift - 1, index],
                lane_land_sem.at[turn, shift - 1, index],
                "expert",
                place.expert_of(0, shift),
            )
            for shift in range(1, lanes)
            for index in indices
        ]

    def layer_copies(turn, indices=range(4)):
        return [
            remote(
                owns[index].at[turn],
                layer_lands[index].at[turn],
                layer_sem.at[turn, index],
                layer_land_sem.at[turn, index],
                "expert",
                place.expert_of((turn + 1) % layers, 0),
            )
            for index in indices
        ]

    def lane_total(turn, index):
        total = owns[index][turn].astype(jnp.float32)
        for shift in range(1, lanes):
            total = total + lane_lands[index][turn, shift - 1].astype(jnp.float32)
        return total

    def combine(turn, indices=range(4)):
        for copy in own_copies(turn, indices):
            copy.wait()
        for copy in lane_copies(turn, indices):
            copy.wait_recv()
        if turn < layers - 1:
            for index, copy in zip(indices, layer_copies(turn, indices)):
                owns[index][turn] = lane_total(turn, index).astype(jnp.bfloat16)
                copy.start()

    units = (units_0, units_1, units_2, units_3, units_4, units_5)
    grads = (grad_0, grad_1, grad_2, grad_3, grad_4, grad_5)
    sources = (rows_ref, rows_ref, cotangent_ref, rows_ref, rows_ref, cotangent_ref)

    def units_copy(index):
        return pltpu.make_async_copy(units[index], units_buf.at[index % 2], units_sem.at[index % 2])

    def rows_copy(index, block, slot):
        if index < 3:
            start = pl.multiple_of(block * column_block, column_block)
            part = pl.ds(start, column_block)
            target = rows_buf.at[slot]
        else:
            part = pl.ds(pl.multiple_of(place.me * columns, columns), columns)
            target = rows_buf.at[slot, :, pl.ds(0, columns)]
        return pltpu.make_async_copy(sources[index].at[:, part], target, rows_sem.at[slot])

    def grad_copy(index, block, slot):
        if index < 3:
            start = pl.multiple_of(block * column_block, column_block)
            return pltpu.make_async_copy(
                grad_buf.at[slot], grads[index].at[:, pl.ds(start, column_block)], grad_sem.at[slot]
            )
        return pltpu.make_async_copy(
            grad_buf.at[slot, :, pl.ds(0, columns)], grads[index], grad_sem.at[slot]
        )

    turn_rows = min(512, tokens)

    def turn_units(index):
        units_copy(index).wait()

        def body(block, inner):
            rows = pl.ds(pl.multiple_of(block * turn_rows, turn_rows), turn_rows)
            turned_buf[:, rows] = units_buf[index % 2, rows, :].T
            return inner

        lax.fori_loop(0, tokens // turn_rows, body, 0)
        if index + 2 < 6:
            units_copy(index + 2).start()

    blocks = width // column_block

    def routed(index):
        rows_copy(index, 0, 0).start()
        turn_units(index)

        def body(block, inner):
            slot = block % 2

            @pl.when(block + 1 < blocks)
            def _():
                rows_copy(index, block + 1, 1 - slot).start()

            rows_copy(index, block, slot).wait()

            @pl.when(block >= 2)
            def _():
                grad_copy(index, block - 2, slot).wait()

            grad_buf[slot] = dot_plain(turned_buf[...], rows_buf[slot])
            grad_copy(index, block, slot).start()
            return inner

        lax.fori_loop(0, blocks, body, 0)
        for block in range(max(blocks - 2, 0), blocks):
            grad_copy(index, block, block % 2).wait()

    def shared(index):
        slot = index % 2
        rows_copy(index, 0, slot).start()
        turn_units(index)
        rows_copy(index, 0, slot).wait()
        part = pl.ds(0, columns)
        grad_buf[slot, :, part] = dot_plain(turned_buf[...], rows_buf[slot, :, part])
        grad_copy(index, 0, slot).start()
        grad_copy(index, 0, slot).wait()

    tensor_sums = (
        (first_ref, first_core_land, first_send, first_land),
        (rest_ref, sum_core_land, sum_send, sum_land),
    )

    def core_exchange(which):
        source, land, _, _ = tensor_sums[which]
        return remote(
            source.at[:, 1 - place.core],
            land,
            tensor_core_sem.at[which],
            tensor_core_land_sem.at[which],
            "tensor",
            place.sibling,
        )

    def side_exchange(which, shift):
        _, _, send, land = tensor_sums[which]
        return remote(
            send.at[shift - 1],
            land.at[shift - 1],
            tensor_side_sem.at[which, shift - 1],
            tensor_side_land_sem.at[which, shift - 1],
            "tensor",
            place.tensor_of(shift),
        )

    def core_sum(which, other):
        source, land, _, _ = tensor_sums[which]
        return source[other, place.core].astype(jnp.float32) + land[other].astype(jnp.float32)

    def send_sides(which):
        core_exchange(which).wait_recv()
        for shift in range(1, sides):
            tensor_sums[which][2][shift - 1] = core_sum(which, place.side_of(shift)).astype(
                jnp.bfloat16
            )
            side_exchange(which, shift).start()

    def tensor_total(which):
        total = core_sum(which, place.side)
        for shift in range(1, sides):
            side_exchange(which, shift).wait_recv()
            total = total + tensor_sums[which][3][shift - 1].astype(jnp.float32)
        return total

    first_own = pltpu.make_async_copy(first_part, first_spread.at[place.mine], first_own_sem)

    def first_piece(tensor):
        return first_spread.at[tensor]

    def first_copy(view, sem, tensor, target):
        return remote(
            view, first_piece(tensor), sem, first_arrive_sem.at[tensor], "tensor", target
        )

    first_sends = [
        first_copy(first_part, first_side_sem.at[shift], place.mine, place.tensor_of(shift))
        for shift in range(1, sides)
    ]
    first_sends.append(
        first_copy(first_part, first_core_sem.at[0], place.mine, place.sibling)
    )
    first_forwards = [
        first_copy(
            first_piece(place.tensor_of(shift)),
            first_core_sem.at[shift],
            place.tensor_of(shift),
            place.sibling,
        )
        for shift in range(1, sides)
    ]

    def await_first(tensor):
        view = first_piece(tensor)
        pltpu.make_async_copy(view, view, first_arrive_sem.at[tensor]).wait()

    def finish_first():
        upstream = tensor_total(0)
        rows = inputs_ref[...].astype(jnp.float32)
        factor = lax.rsqrt(jnp.mean(rows * rows, axis=1, keepdims=True) + EPS)
        unit_rows = rows * factor
        scaled = upstream * gain_ref[...]
        inner_mean = jnp.mean(scaled * unit_rows, axis=1, keepdims=True)
        first_part[...] = (
            residual_ref[...] + factor * (scaled - unit_rows * inner_mean)
        ).astype(jnp.bfloat16)
        first_own.start()
        for copy in first_sends:
            copy.start()
        gain_grad = jnp.sum(upstream * unit_rows, axis=0, keepdims=True)
        summed_rows = rest_block.shape[0] - 16
        rest_block[pl.ds(0, summed_rows), :] = tensor_total(1).astype(jnp.bfloat16)
        row = lax.broadcasted_iota(jnp.int32, (16, width), 0)
        rest_block[pl.ds(summed_rows, 16), :] = jnp.where(row == 0, gain_grad, 0.0).astype(
            jnp.bfloat16
        )
        for turn in range(layers):
            for copy in lane_copies(turn, (3,)) + own_copies(turn, (3,)):
                copy.start()

    def forward_first():
        for shift in range(1, sides):
            await_first(place.tensor_of(shift))
            first_forwards[shift - 1].start()

    units_copy(0).start()
    units_copy(1).start()
    pl.semaphore_wait(barrier, count)
    for which in range(2):
        core_exchange(which).start()
    for turn in range(layers):
        for copy in lane_copies(turn, range(3)) + own_copies(turn, range(3)):
            copy.start()
    for which in range(2):
        send_sides(which)
    routed(0)
    combine(0, range(3))
    finish_first()
    routed(1)
    if layers > 2:
        combine(1, range(3))
    forward_first()
    routed(2)
    for turn in range(2, layers - 1):
        combine(turn, range(3))
    for turn in range(layers - 1):
        combine(turn, (3,))
    for index in range(3, 6):
        shared(index)
    combine(layers - 1)

    last = layers - 1
    for turn in range(last):
        for copy in layer_copies(turn):
            copy.wait_recv()
    for index in range(4):
        total = lane_total(last, index)
        for turn in range(last):
            total = total + layer_lands[index][turn].astype(jnp.float32)
        if index < 3:
            sums[index][...] = total
        else:
            rest_part[...] = total.astype(jnp.bfloat16)
    spread_over_tensor(
        place,
        rest_part,
        rest_spread,
        (spread_own_sem, spread_side_sem, spread_core_sem, arrive_sem),
    )
    for shift in range(sides):
        await_first(place.side_of(shift) * 2 + (1 - place.core))
    first_own.wait()
    for copy in first_sends + first_forwards:
        copy.wait_send()
    for which in range(2):
        core_exchange(which).wait_send()
        for shift in range(1, sides):
            side_exchange(which, shift).wait_send()
    for turn in range(layers):
        for copy in lane_copies(turn):
            copy.wait_send()
        if turn < last:
            for copy in layer_copies(turn):
                copy.wait_send()


def run_weights(
    query, latent, out, rest, first, residual, inputs_part, gain, units, rows, cotangent
):
    groups = lax.axis_size("expert")
    tensors = lax.axis_size("tensor")
    layers = min(LAYERS, groups)
    lanes = groups // layers
    sides = tensors // 2
    part_rows = residual.shape[0]
    rest_rows = rest.shape[0] // tensors
    tokens, width = rows.shape
    hidden = units[0].shape[1]
    columns = width // groups
    column_block = min(256, width)
    bf16 = jnp.bfloat16
    f32 = jnp.float32
    dma = pltpu.SemaphoreType.DMA
    query = query.reshape(groups, query.shape[0] // groups, query.shape[1])
    latent = latent.reshape(groups, latent.shape[0] // groups, latent.shape[1])
    shapes = (
        query.shape[1:],
        latent.shape[1:],
        (out.shape[0], columns),
        (rest_rows + 16, columns),
    )
    routed = jax.ShapeDtypeStruct((hidden, width), f32)
    shared = jax.ShapeDtypeStruct((hidden, columns), f32)
    return pl.pallas_call(
        functools.partial(weight_kernel, groups=groups, tensors=tensors),
        out_shape=tuple(jax.ShapeDtypeStruct(shape, f32) for shape in shapes[:3])
        + (jax.ShapeDtypeStruct((tensors,) + shapes[3], bf16),)
        + (jax.ShapeDtypeStruct((tensors, part_rows, width), bf16),)
        + (routed,) * 3
        + (shared,) * 3,
        in_specs=[ANYWHERE] * 3 + [IN_VMEM] * 5 + [ANYWHERE] * 8,
        out_specs=(IN_VMEM,) * 3 + (ANYWHERE,) * 8,
        scratch_shapes=[pltpu.VMEM((layers,) + shape, bf16) for shape in shapes]
        + [pltpu.VMEM((layers, lanes - 1) + shape, bf16) for shape in shapes]
        + [pltpu.VMEM((layers - 1,) + shape, bf16) for shape in shapes]
        + [
            pltpu.VMEM(shapes[3], bf16),
            pltpu.VMEM((rest_rows + 16, width), bf16),
            pltpu.VMEM((sides, part_rows, width), bf16),
            pltpu.VMEM((sides - 1, part_rows, width), bf16),
            pltpu.VMEM((sides - 1, part_rows, width), bf16),
            pltpu.VMEM((part_rows, width), bf16),
            pltpu.VMEM((sides, rest_rows, width), bf16),
            pltpu.VMEM((sides - 1, rest_rows, width), bf16),
            pltpu.VMEM((sides - 1, rest_rows, width), bf16),
            pltpu.VMEM((2, tokens, hidden), bf16),
            pltpu.VMEM((hidden, tokens), bf16),
            pltpu.VMEM((2, tokens, column_block), bf16),
            pltpu.VMEM((2, hidden, column_block), f32),
            dma((layers, 4)),
            dma((layers, lanes - 1, 4)),
            dma((layers, lanes - 1, 4)),
            dma((layers - 1, 4)),
            dma((layers - 1, 4)),
            dma((2,)),
            dma((2,)),
            dma((2,)),
            dma(()),
            dma((sides,)),
            dma((sides,)),
            dma((tensors,)),
            dma((2,)),
            dma((2,)),
            dma((2, sides - 1)),
            dma((2, sides - 1)),
            dma(()),
            dma((sides,)),
            dma((sides,)),
            dma((tensors,)),
        ],
        compiler_params=pltpu.CompilerParams(
            collective_id=4, has_side_effects=True, vmem_limit_bytes=60 * 1024 * 1024
        ),
        cost_estimate=pl.CostEstimate(
            flops=7 * tokens * width * hidden, bytes_accessed=100_000_000, transcendentals=0
        ),
        name="weights",
    )(
        query,
        latent,
        out,
        rest.reshape(sides, 2, rest_rows, width),
        first.reshape(sides, 2, part_rows, width),
        residual,
        inputs_part,
        gain.reshape(1, width),
        *units,
        rows,
        cotangent,
    )


def on_device(
    inputs,
    cotangent,
    positions,
    routes,
    slot_index,
    attention_gain,
    feedforward_gain,
    latent_gain,
    query_weight,
    latent_down,
    latent_up,
    out_weight,
    router_weight,
    shared_gate,
    shared_up,
    shared_down,
    expert_gate,
    expert_up,
    expert_down,
):
    length, model_width = inputs.shape
    tensor_count = lax.axis_size("tensor")
    group_count = lax.axis_size("expert")
    tensor_index = lax.axis_index("tensor")
    group_index = lax.axis_index("expert")
    head_width = NOPE + ROPE
    local_heads = query_weight.shape[1] // head_width
    local_experts, _, expert_hidden_width = expert_gate.shape
    shared_width = shared_gate.shape[1]
    experts_all = local_experts * group_count
    capacity = max(
        tensor_count, length * TOP * 4 // (3 * experts_all) // tensor_count * tensor_count
    )
    score_scale = 1.0 / math.sqrt(head_width)
    part_rows = length // tensor_count
    part_start = tensor_index * part_rows
    shard_columns = model_width // group_count

    def own_part(rows):
        return lax.dynamic_slice_in_dim(rows, part_start, part_rows, 0)

    def own_sequence(rows):
        return lax.dynamic_slice_in_dim(rows, group_index * length, length, 0)

    def own_columns(rows):
        return lax.dynamic_slice_in_dim(rows, group_index * shard_columns, shard_columns, 1)

    marks = expert_table(routes, jnp.where(slot_index < capacity, 2.0, 1.0), LANES)
    cotangent_all = gather_rows(
        jnp.concatenate([own_part(cotangent), own_part(marks).astype(jnp.bfloat16)], axis=1)
    )

    rows_in = inputs.astype(jnp.float32)
    normed_one, unit_one, factor_one = normalize(rows_in, attention_gain)
    first_norm = normed_one.astype(jnp.bfloat16)
    cosine, sine_table = rope_tables(positions)
    query_raw = plain_dot(first_norm, query_weight).reshape(length, local_heads, head_width)
    queries = jnp.concatenate(
        [
            query_raw[..., :NOPE],
            rotate(query_raw[..., NOPE:], cosine[:, None], sine_table[:, None]),
        ],
        axis=-1,
    ).astype(jnp.bfloat16)
    latent_raw = plain_dot(first_norm, latent_down)
    latent_normed, unit_latent, factor_latent = normalize(latent_raw[:, :KVR], latent_gain)
    latent = latent_normed.astype(jnp.bfloat16)
    key_rope = rotate(latent_raw[:, KVR:], cosine, sine_table).astype(jnp.bfloat16)
    key_value = (
        plain_dot(latent, latent_up).astype(jnp.bfloat16).reshape(length, local_heads, NOPE + VD)
    )
    key_rows = jnp.concatenate(
        [
            key_value[..., :NOPE],
            jnp.broadcast_to(key_rope[:, None, :], (length, local_heads, ROPE)),
        ],
        axis=-1,
    )
    values = key_value[..., NOPE:]
    visible = visible_mask(positions, length)
    scores = jnp.where(
        visible[None],
        jnp.einsum("qhd,khd->hqk", queries, key_rows, preferred_element_type=jnp.float32)
        * score_scale,
        -jnp.inf,
    )
    weights = jax.nn.softmax(scores, axis=-1)
    weights_low = weights.astype(jnp.bfloat16)
    head_out = (
        jnp.einsum("hqk,khd->qhd", weights_low, values, preferred_element_type=jnp.float32)
        .astype(jnp.bfloat16)
        .reshape(length, local_heads * VD)
    )
    gate_stored = expert_gate.swapaxes(1, 2).reshape(shared_width, model_width)
    up_stored = expert_up.swapaxes(1, 2).reshape(shared_width, model_width)
    down_stored = expert_down.reshape(shared_width, model_width)
    router_padded = jnp.pad(router_weight, ((0, 0), (0, LANES - experts_all)))
    second_all, acts, logits_all, residual = run_forward(
        plain_dot(head_out, out_weight).astype(jnp.bfloat16),
        inputs,
        feedforward_gain,
        (gate_stored, up_stored, shared_gate.T, shared_up.T),
        router_padded,
    )
    (
        expert_hidden,
        expert_dpre,
        expert_dlin,
        shared_hidden,
        shared_dpre,
        shared_dlin,
        attention_grad,
        result_part,
        grad_residual,
        logit_low,
        grad_feedforward_gain,
    ) = run_backward(
        cotangent_all,
        acts,
        logits_all,
        (gate_stored, up_stored, down_stored, shared_gate.T, shared_up.T, shared_down),
        router_padded,
        residual,
        feedforward_gain,
        local_experts,
    )
    result = lax.all_gather(result_part, "tensor", axis=0, tiled=True)
    tokens = group_count * length
    second_all = second_all.reshape(tokens, model_width)

    attention_grad = attention_grad.reshape(length, model_width)
    second_part = lax.dynamic_slice_in_dim(
        second_all, group_index * length + part_start, part_rows, 0
    )
    grad_out_weight = lead_dot(head_out, attention_grad)
    head_grad = (
        tail_dot(attention_grad, out_weight).astype(jnp.bfloat16).reshape(length, local_heads, VD)
    )
    weight_grad = jnp.einsum("qhd,khd->hqk", head_grad, values, preferred_element_type=jnp.float32)
    score_grad = (
        weights * (weight_grad - jnp.sum(weights * weight_grad, axis=-1, keepdims=True))
    ).astype(jnp.bfloat16)
    query_grad = (
        jnp.einsum("hqk,khd->qhd", score_grad, key_rows, preferred_element_type=jnp.float32)
        * score_scale
    )
    key_grad = (
        jnp.einsum("hqk,qhd->khd", score_grad, queries, preferred_element_type=jnp.float32)
        * score_scale
    )
    value_grad = jnp.einsum(
        "hqk,qhd->khd", weights_low, head_grad, preferred_element_type=jnp.float32
    )
    query_low = (
        jnp.concatenate(
            [
                query_grad[..., :NOPE],
                rotate_back(query_grad[..., NOPE:], cosine[:, None], sine_table[:, None]),
            ],
            axis=-1,
        )
        .astype(jnp.bfloat16)
        .reshape(length, local_heads * head_width)
    )
    grad_query = lead_dot(first_norm, query_low)
    keyvalue_low = (
        jnp.concatenate([key_grad[..., :NOPE], value_grad], axis=-1)
        .astype(jnp.bfloat16)
        .reshape(length, local_heads * (NOPE + VD))
    )
    grad_latent_up = lead_dot(latent, keyvalue_low)
    latent_grad = tail_dot(keyvalue_low, latent_up)
    latent_back, grad_latent_gain = norm_back(latent_grad, unit_latent, factor_latent, latent_gain)
    rope_back = rotate_back(jnp.sum(key_grad[..., NOPE:], axis=1), cosine, sine_table)
    down_low = jnp.concatenate([latent_back, rope_back], axis=1).astype(jnp.bfloat16)
    first_terms = (tail_dot(query_low, query_weight) + tail_dot(down_low, latent_down)).astype(
        jnp.bfloat16
    )
    latent_width = latent_down.shape[1]
    latent_gain_rows = jnp.pad(
        grad_latent_gain.reshape(group_count, -1),
        ((0, 0), (0, shard_columns - KVR // group_count)),
    ).reshape(1, model_width)
    gain_start = latent_width + -(-experts_all // 16) * 16
    rest_count = gain_start + 16
    rest_rows = -(-rest_count // (16 * tensor_count)) * 16 * tensor_count

    def at_row(start, rows):
        return jnp.pad(rows, ((start, rest_rows - start - rows.shape[0]), (0, 0)))

    rest = (
        lead_dot(jnp.pad(down_low, ((0, 0), (0, rest_rows - latent_width))), first_norm)
        + at_row(latent_width, lead_dot(logit_low[:, :experts_all], second_part))
        + at_row(gain_start, grad_feedforward_gain)
        + at_row(gain_start + 1, latent_gain_rows)
    ).astype(jnp.bfloat16)
    (
        grad_query,
        grad_latent_up,
        grad_out_weight,
        rest,
        grad_input,
        grad_expert_gate,
        grad_expert_up,
        grad_expert_down,
        grad_shared_gate,
        grad_shared_up,
        grad_shared_down,
    ) = run_weights(
        grad_query.astype(jnp.bfloat16),
        grad_latent_up.astype(jnp.bfloat16),
        grad_out_weight.astype(jnp.bfloat16),
        rest,
        first_terms,
        grad_residual,
        own_part(inputs),
        attention_gain,
        [
            units.reshape(tokens, shared_width)
            for units in (
                expert_dpre,
                expert_dlin,
                expert_hidden,
                shared_dpre,
                shared_dlin,
                shared_hidden,
            )
        ],
        second_all,
        cotangent_all,
    )
    grad_input = grad_input.reshape(length, model_width).astype(jnp.float32)
    rest = rest.astype(jnp.float32)
    grad_attention_gain = jnp.sum(rest[:, -16], axis=0)
    rest = rest[:, :-16].reshape(-1, shard_columns)
    gain_rows = rest[gain_start:rest_count]

    def stored_experts(rows):
        return rows.reshape(local_experts, expert_hidden_width, model_width)

    return (
        result,
        grad_input,
        grad_attention_gain,
        gain_rows[0],
        gain_rows[1, : KVR // group_count],
        grad_query,
        rest[:latent_width].T,
        grad_latent_up,
        grad_out_weight,
        rest[latent_width : latent_width + experts_all].T,
        grad_shared_gate.T,
        grad_shared_up.T,
        grad_shared_down,
        stored_experts(grad_expert_gate).swapaxes(1, 2),
        stored_experts(grad_expert_up).swapaxes(1, 2),
        stored_experts(grad_expert_down),
    )


def solution(mesh):
    placed = (
        P("expert", None),
        P("expert", None),
        P("expert"),
        P("expert", None),
        P("expert", None),
        P(),
        P(),
        P(),
        P(None, "tensor"),
        P(),
        P(None, "tensor"),
        P("tensor", None),
        P(),
        P(None, "tensor"),
        P(None, "tensor"),
        P("tensor", None),
        P("expert", None, "tensor"),
        P("expert", None, "tensor"),
        P("expert", "tensor", None),
    )
    return jax.shard_map(
        on_device,
        mesh=mesh,
        in_specs=placed,
        out_specs=(
            P("expert", None),
            P("expert", None),
            P("expert"),
            P("expert"),
            P("expert"),
            P("expert", "tensor"),
            P("expert", None),
            P("expert", "tensor"),
            P("tensor", "expert"),
            P("expert", None),
            P("expert", "tensor"),
            P("expert", "tensor"),
            P("tensor", "expert"),
            P("expert", None, "tensor"),
            P("expert", None, "tensor"),
            P("expert", "tensor", None),
        ),
        check_vma=False,
    )
```

time: 1350 us -> 631 us (0.47)
  waiting for transfers between devices: 860 us -> 0.06 us
  Pallas kernels: 0 us -> 509 us
  matrix products: 337 us -> 41 us
  blocking collectives: 37.7 us -> 0 us
  other arithmetic: 52.7 us -> 16.2 us
    reduce_scatter x9 -> x0, waiting for transfers between devices: 665 us -> none  [the longest x4 529 us: scatter_rows(): return lax.psum_scatter(rows, BOTH, scatter_dimension=0, tiled=True)]
    pallas_call x0 -> x3, Pallas kernels: none -> 509 us  [the longest x1 216 us: run_backward(): pl.pallas_call(functools.partial(backward_kernel, groups=groups, tensors=...]
    dot_general x13 -> x4, matrix products: 146 us -> 11.3 us  [plain_dot(): return jnp.dot(left_side, right_side, preferred_element_type=jnp.float32)]
    all_gather x2 -> x1, waiting for transfers between devices: 125 us -> 0.02 us  [gather_rows(): return lax.all_gather(rows, BOTH, axis=0, tiled=True)]
    dot_general x14 -> x5, matrix products: 97 us -> 14.2 us  [lead_dot(): lax.dot_general(left_side, right_side, (((0,), (0,)), ((), ())), preferre...]
    dot_general x9 -> x4, matrix products: 90.4 us -> 9.88 us  [tail_dot(): lax.dot_general(left_side, right_side, (((1,), (1,)), ((), ())), preferre...]
    all_gather x2 -> x0, waiting for transfers between devices: 48.1 us -> none  [the longest x1 24.8 us: on_device(): lax.all_gather((grad_residual + input_back).astype(jnp.bfloat16), 'tensor...]
    all_gather x2 -> x0, blocking collectives: 37.7 us -> none  [the longest x1 31.3 us: on_device(): marked_all = lax.all_gather(marked, 'expert', axis=0, tiled=True)]
  transfers between devices with their start and end apart: 14 -> 2, of which waited for: 12 -> 0; matrix products, arithmetic and copies ran while one was open for 23% -> 7% of each run, Pallas kernels for 0% -> 47%
where the time goes in v3:
time: 631 us; the launch traced here: 626 us
  Pallas kernels  509 us (81%)
  local copies, waits for them, and re-layouts  45.3 us (7%)
  matrix products  41 us (6%)
  other arithmetic  16.2 us (3%)
  between operations  14.9 us (2%)
    pallas_call x1, Pallas kernels, run_backward(): pl.pallas_call(functools.partial(backward_kernel, groups=groups, tensors=...  216 us
    pallas_call x1, Pallas kernels, run_forward(): pl.pallas_call(functools.partial(forward_kernel, groups=groups, tensors=t...  168 us
    pallas_call x1, Pallas kernels, run_weights(): pl.pallas_call(functools.partial(weight_kernel, groups=groups, tensors=te...  124 us
    unnamed x103, local copies, waits for them, and re-layouts  29.5 us
    dot_general x5, matrix products, lead_dot(): lax.dot_general(left_side, right_side, (((0,), (0,)), ((), ())), preferre...  14.2 us
  transfers between devices with their start and end apart: 2, of which 0 were waited for; matrix products, arithmetic and copies ran while one was open for 7% of the time, Pallas kernels for 47%

profile of v3, /device:TPU:0, one launch (start us, length us, event | category | flops | bytes accessed | tf_op | source)
XLA Modules:
  0.0 626.1 jit_solution(7924797576496482088)
XLA Ops:
  7.2 0.9 compare_select_fusion
  8.6 1.0 fusion.50
  9.8 1.1 constant_dynamic-slice_fusion.1
  11.4 0.8 pad_maximum_fusion.7
  12.3 2.2 fusion.1
  14.6 3.4 fusion.47
  18.1 0.9 copy-done.1
  19.0 1.8 convolution_convert_fusion.4
  20.8 2.5 copy.64
  23.3 1.9 slice.162
  25.2 3.5 fusion.45
  28.8 1.1 copy-done.15
  29.9 0.9 slice.222
  30.7 1.0 copy.51
  31.7 1.9 pad.24.router_ref
  33.7 1.2 multiply_cosine_fusion
  35.0 1.1 subtract_convert_fusion.1
  36.1 2.1 fusion.13
  38.4 1.9 constant_dynamic-slice_fusion.inputs_ref
  40.3 2.1 fusion.51
  42.5 0.5 convolution_convert_fusion.7
  42.9 1.7 copy-done.5
  44.6 1.1 copy-done.32
  45.7 2.6 convolution_convert_fusion.2
  48.3 168.3 %experts_forward.1 = (bf16[8,512,2048]{2,1,0:T(8,128)(2,1)}, bf16[4,8,512,704]{3,2,1,0:T(8,128)(2,1)}, f32[8,512,128]{2,1,0:T(8,128)}, f32[128,2048]{1,0:T(8,128)}) custom-call(bf16[2,2,128,2048]{3,2,1,0:T(8,128)(2,1)} %bitcast.158, bf16[512,2048]{1,0:T(8,128)(2,1)} %inputs_ref.1, f32[1,2048]{1,0:T(1,128)} %bitcast.144, bf16[704,2048]{1,0:T(8,128)(2,1)} %bitcast.135, ...), custom_call_target="tpu_custom_call" | custom-call | flops 47244640256 | bytes 100000000 | tf_op jit(solution)/shard_map/experts_forward/pallas_call | solution.py:1168
  216.6 216.2 %experts_backward.1 = (bf16[8,512,704]{2,1,0:T(8,128)(2,1)}, bf16[8,512,704]{2,1,0:T(8,128)(2,1)}, bf16[8,512,704]{2,1,0:T(8,128)(2,1)}, bf16[8,512,704]{2,1,0:T...) custom-call(bf16[8,512,2176]{2,1,0:T(8,128)(2,1)} %bitcast.134, ...), custom_call_target="tpu_custom_call" | custom-call | flops 59055800320 | bytes 100000000 | tf_op jit(solution)/shard_map/experts_backward/pallas_call | solution.py:1247
  432.8 3.7 convolution_convert_fusion.5
  436.6 0.8 multiply_reduce_fusion
  437.3 0.8 fusion.8
  438.2 1.2 multiply_convert_fusion
  439.4 0.8 multiply_bitcast_fusion
  440.5 0.6 multiply_bitcast_fusion.1
  441.3 1.0 copy-done.2
  442.6 0.9 multiply_reduce_fusion.2
  443.5 1.8 convolution_convert_fusion.3
  445.3 2.6 convolution_convert_fusion.1.out_ref
  447.9 1.8 fusion.52
  449.8 3.7 convolution_convert_fusion
  453.6 0.3 fusion.32
  454.1 0.9 pad_maximum_fusion.6
  455.0 0.5 copy-done.31
  455.4 3.5 add_convert_fusion.1
  459.1 1.3 fusion.14
  460.3 4.9 add_convert_fusion
  465.3 124.1 %weights.1 = (f32[256,768]{1,0:T(8,128)}, f32[64,1024]{1,0:T(8,128)}, f32[512,256]{1,0:T(8,128)}, bf16[4,176,256]{2,1,0:T(8,128)(2,1)}, bf16[4,128,2048]{2,1,0:T...) custom-call(bf16[8,256,768]{2,1,0:T(8,128)(2,1)} %bitcast.153, ...), custom_call_target="tpu_custom_call" | custom-call | flops 41339060224 | bytes 100000000 | tf_op jit(solution)/shard_map/weights/pallas_call | solution.py:1749
  589.4 1.2 slice.173
  590.5 1.0 convert_element_type.110
  591.6 0.6 slice.174
  592.1 0.6 slice_reduce_fusion.1
  592.7 0.5 slice_bitcast_fusion.2
  593.2 0.6 slice_bitcast_fusion.1
  593.8 0.9 slice_bitcast_fusion
  594.7 2.7 bitcast_convert_fusion
  597.4 3.3 copy.76
  600.7 2.2 copy.77
  602.9 0.7 copy.78
  603.6 2.3 copy.79
  605.9 2.0 copy.80
  607.9 0.9 copy.81
  608.7 0.9 copy.82
  609.6 2.9 copy.83
  612.5 2.9 copy.84
  615.4 1.1 slice-done.1
  616.5 2.5 copy.85
  (123 shorter events, 3.0 us)
Async XLA Ops:
  7.2 18.0 %copy-start = (bf16[2048,768]{1,0:T(8,128)(2,1)S(1)}, bf16[2048,768]{1,0:T(8,128)(2,1)}, u32[]{:S(2)}) copy-start(bf16[2048,768]{1,0:T(8,128)(2,1)} %param.27) | copy-start | bytes 9437188
  7.2 209.4 %all-gather.3.cloned.1.call-start = ((), (), s32[]{:S(2)}) async-start(), calls=%async_computation | async-start | bytes 18382848 | tf_op jit(solution)/shard_map/all_gather | solution.py:92
  10.9 3.6 copy-start.35
  12.3 585.1 %all-gather.5.cloned.1.call-start = ((), (), s32[]{:S(2)}) async-start(), calls=%async_computation.1 | async-start | bytes 2621440 | tf_op jit(solution)/shard_map/all_gather | solution.py:1945
  12.3 2.3 copy-start.7
  14.6 10.6 %copy-start.29 = (f32[512]{0:T(512)}, f32[512]{0:T(512)S(1)}, u32[]{:S(2)}) copy-start(f32[512]{0:T(512)S(1)} %add_rsqrt_fusion.1) | copy-start | bytes 6148
  14.6 4.4 copy-start.25
  14.6 4.4 copy-start.33
  18.0 1.0 copy-start.1
  25.2 5.6 copy-start.21
  28.7 1.1 copy-start.15
  28.7 5.0 copy-start.28
  33.7 4.5 copy-start.26
  33.7 1.2 copy-start.23
  36.1 2.1 copy-start.16
  36.1 2.1 copy-start.18
  40.3 2.2 copy-start.9
  42.4 2.2 copy-start.5
  42.5 3.2 copy-start.32
  44.6 3.7 copy-start.38
  432.8 3.7 copy-start.6
  432.8 3.7 copy-start.10
  438.2 1.2 copy-start.12
  438.2 1.2 copy-start.17
  438.2 1.2 copy-start.19
  439.4 1.0 copy-start.4
  441.0 1.3 copy-start.2
  441.0 1.6 copy-start.34
  443.5 1.8 copy-start.37
  443.5 1.8 copy-start.39
  447.9 1.9 copy-start.8
  447.9 1.9 copy-start.30
  447.9 1.9 copy-start.36
  449.8 3.7 copy-start.24
  449.8 3.7 copy-start.27
  453.5 1.9 copy-start.31
  455.4 3.6 copy-start.22
  455.4 4.9 copy-start.40
  589.3 5.4 copy-start.11
  594.7 8.2 %copy-start.20 = (f32[64,1024]{1,0:T(8,128)S(1)}, f32[64,1024]{1,0:T(8,128)}, u32[]{:S(2)}) copy-start(f32[64,1024]{1,0:T(8,128)} %get-tuple-element.126) | copy-start | bytes 786436
  597.4 15.1 %slice-start.2 = ((s8[5767168]{0:T(1024)(128)(4,1)}), s8[4194304]{0:T(1024)(128)(4,1)S(1)}, s32[]{:S(2)}) async-start(s8[5767168]{0:T(1024)(128)(4,1)} %bitcast.98), calls=%async_computation.4 | async-start | bytes 8388608
  600.7 7.2 %copy-start.14 = (f32[704,256]{1,0:T(8,128)S(1)}, f32[704,256]{1,0:T(8,128)}, u32[]{:S(2)}) copy-start(f32[704,256]{1,0:T(8,128)} %get-tuple-element.63) | copy-start | bytes 2162692
  600.7 8.0 %copy-start.13 = (f32[704,256]{1,0:T(8,128)S(1)}, f32[704,256]{1,0:T(8,128)}, u32[]{:S(2)}) copy-start(f32[704,256]{1,0:T(8,128)} %get-tuple-element.131) | copy-start | bytes 2162692
  602.9 6.7 %copy-start.3 = (f32[704,2048]{1,0:T(8,128)S(1)}, f32[704,2048]{1,0:T(8,128)}, u32[]{:S(2)}) copy-start(f32[704,2048]{1,0:T(8,128)} %get-tuple-element.65) | copy-start | bytes 17301508
  608.7 3.8 slice-start.3
  609.6 5.9 slice-start
  612.5 4.0 slice-start.1
Sparse Core Ops, SparseCore 0:
  12.4 175.1 all-gather.2
  459.2 23.5 all-gather.4

commit v4 on v3

--- a/solution.py
+++ b/solution.py
@@ -949,6 +949,7 @@
     def step_body(step, carry):
         slot = step % 2
         running = step < groups
+        services(step)
 
         @pl.when(running)
         def _():
@@ -1031,8 +1032,6 @@
             def _():
                 for copy in weight_copies[2:]:
                     copy.wait()
-
-        services(step)
 
         @pl.when(running)
         def _():

time: 631 us -> 635 us (level)
  transfers between devices with their start and end apart: 2 -> 2, of which waited for: 0 -> 0; matrix products, arithmetic and copies ran while one was open for 7% -> 7% of each run, Pallas kernels for 47% -> 46%
where the time goes in v4:
time: 635 us; the launch traced here: 631 us
  Pallas kernels  513 us (81%)
  local copies, waits for them, and re-layouts  45.3 us (7%)
  matrix products  41 us (6%)
  other arithmetic  16.2 us (3%)
  between operations  14.9 us (2%)
    pallas_call x1, Pallas kernels, run_backward(): pl.pallas_call(functools.partial(backward_kernel, groups=groups, tensors=...  221 us
    pallas_call x1, Pallas kernels, run_forward(): pl.pallas_call(functools.partial(forward_kernel, groups=groups, tensors=t...  168 us
    pallas_call x1, Pallas kernels, run_weights(): pl.pallas_call(functools.partial(weight_kernel, groups=groups, tensors=te...  124 us
    unnamed x103, local copies, waits for them, and re-layouts  29.5 us
    dot_general x5, matrix products, lead_dot(): lax.dot_general(left_side, right_side, (((0,), (0,)), ((), ())), preferre...  14.2 us
  transfers between devices with their start and end apart: 2, of which 0 were waited for; matrix products, arithmetic and copies ran while one was open for 7% of the time, Pallas kernels for 46%

profile of v4, /device:TPU:0, one launch (start us, length us, event | category | flops | bytes accessed | tf_op | source)
XLA Modules:
  0.0 630.7 jit_solution(7285652023556596538)
XLA Ops:
  7.2 0.9 compare_select_fusion
  8.6 1.0 fusion.50
  9.8 1.1 constant_dynamic-slice_fusion.1
  11.4 0.8 pad_maximum_fusion.7
  12.3 2.2 fusion.1
  14.6 3.4 fusion.47
  18.1 0.9 copy-done.1
  19.0 1.8 convolution_convert_fusion.4
  20.8 2.5 copy.64
  23.3 1.9 slice.162
  25.2 3.5 fusion.45
  28.8 1.1 copy-done.15
  29.9 0.9 slice.222
  30.7 1.0 copy.51
  31.7 1.9 pad.24.router_ref
  33.7 1.2 multiply_cosine_fusion
  35.0 1.1 subtract_convert_fusion.1
  36.1 2.1 fusion.13
  38.4 1.9 constant_dynamic-slice_fusion.inputs_ref
  40.3 2.1 fusion.51
  42.5 0.5 convolution_convert_fusion.7
  42.9 1.7 copy-done.5
  44.6 1.1 copy-done.32
  45.7 2.6 convolution_convert_fusion.2
  48.3 168.3 %experts_forward.1 = (bf16[8,512,2048]{2,1,0:T(8,128)(2,1)}, bf16[4,8,512,704]{3,2,1,0:T(8,128)(2,1)}, f32[8,512,128]{2,1,0:T(8,128)}, f32[128,2048]{1,0:T(8,128)}) custom-call(bf16[2,2,128,2048]{3,2,1,0:T(8,128)(2,1)} %bitcast.158, bf16[512,2048]{1,0:T(8,128)(2,1)} %inputs_ref.1, f32[1,2048]{1,0:T(1,128)} %bitcast.144, bf16[704,2048]{1,0:T(8,128)(2,1)} %bitcast.135, ...), custom_call_target="tpu_custom_call" | custom-call | flops 47244640256 | bytes 100000000 | tf_op jit(solution)/shard_map/experts_forward/pallas_call | solution.py:1167
  216.6 220.6 %experts_backward.1 = (bf16[8,512,704]{2,1,0:T(8,128)(2,1)}, bf16[8,512,704]{2,1,0:T(8,128)(2,1)}, bf16[8,512,704]{2,1,0:T(8,128)(2,1)}, bf16[8,512,704]{2,1,0:T...) custom-call(bf16[8,512,2176]{2,1,0:T(8,128)(2,1)} %bitcast.134, ...), custom_call_target="tpu_custom_call" | custom-call | flops 59055800320 | bytes 100000000 | tf_op jit(solution)/shard_map/experts_backward/pallas_call | solution.py:1246
  437.2 3.7 convolution_convert_fusion.5
  440.9 0.8 multiply_reduce_fusion
  441.7 0.8 fusion.8
  442.5 1.2 multiply_convert_fusion
  443.8 0.8 multiply_bitcast_fusion
  444.8 0.6 multiply_bitcast_fusion.1
  445.6 1.0 copy-done.2
  447.0 0.9 multiply_reduce_fusion.2
  447.8 1.8 convolution_convert_fusion.3
  449.6 2.6 convolution_convert_fusion.1.out_ref
  452.3 1.8 fusion.52
  454.2 3.7 convolution_convert_fusion
  457.9 0.3 fusion.32
  458.4 0.9 pad_maximum_fusion.6
  459.3 0.5 copy-done.31
  459.8 3.5 add_convert_fusion.1
  463.4 1.3 fusion.14
  464.7 4.9 add_convert_fusion
  469.6 124.3 %weights.1 = (f32[256,768]{1,0:T(8,128)}, f32[64,1024]{1,0:T(8,128)}, f32[512,256]{1,0:T(8,128)}, bf16[4,176,256]{2,1,0:T(8,128)(2,1)}, bf16[4,128,2048]{2,1,0:T...) custom-call(bf16[8,256,768]{2,1,0:T(8,128)(2,1)} %bitcast.153, ...), custom_call_target="tpu_custom_call" | custom-call | flops 41339060224 | bytes 100000000 | tf_op jit(solution)/shard_map/weights/pallas_call | solution.py:1748
  594.0 1.2 slice.173
  595.1 1.0 convert_element_type.110
  596.2 0.6 slice.174
  596.7 0.6 slice_reduce_fusion.1
  597.3 0.5 slice_bitcast_fusion.2
  597.8 0.6 slice_bitcast_fusion.1
  598.4 0.9 slice_bitcast_fusion
  599.3 2.7 bitcast_convert_fusion
  602.0 3.3 copy.76
  605.3 2.2 copy.77
  607.5 0.7 copy.78
  608.2 2.3 copy.79
  610.5 2.0 copy.80
  612.5 0.9 copy.81
  613.3 0.9 copy.82
  614.2 2.9 copy.83
  617.1 2.9 copy.84
  620.0 1.1 slice-done.1
  621.1 2.5 copy.85
  (123 shorter events, 3.0 us)
Async XLA Ops:
  7.2 18.0 %copy-start = (bf16[2048,768]{1,0:T(8,128)(2,1)S(1)}, bf16[2048,768]{1,0:T(8,128)(2,1)}, u32[]{:S(2)}) copy-start(bf16[2048,768]{1,0:T(8,128)(2,1)} %param.27) | copy-start | bytes 9437188
  7.2 209.4 %all-gather.3.cloned.1.call-start = ((), (), s32[]{:S(2)}) async-start(), calls=%async_computation | async-start | bytes 18382848 | tf_op jit(solution)/shard_map/all_gather | solution.py:92
  10.9 3.6 copy-start.35
  12.3 589.7 %all-gather.5.cloned.1.call-start = ((), (), s32[]{:S(2)}) async-start(), calls=%async_computation.1 | async-start | bytes 2621440 | tf_op jit(solution)/shard_map/all_gather | solution.py:1944
  12.3 2.3 copy-start.7
  14.6 10.6 %copy-start.29 = (f32[512]{0:T(512)}, f32[512]{0:T(512)S(1)}, u32[]{:S(2)}) copy-start(f32[512]{0:T(512)S(1)} %add_rsqrt_fusion.1) | copy-start | bytes 6148
  14.6 4.4 copy-start.25
  14.6 4.4 copy-start.33
  18.0 1.0 copy-start.1
  25.2 5.6 copy-start.21
  28.7 1.1 copy-start.15
  28.7 5.0 copy-start.28
  33.7 4.5 copy-start.26
  33.7 1.2 copy-start.23
  36.1 2.1 copy-start.16
  36.1 2.1 copy-start.18
  40.3 2.2 copy-start.9
  42.4 2.2 copy-start.5
  42.5 3.2 copy-start.32
  44.6 3.7 copy-start.38
  437.2 3.7 copy-start.6
  437.2 3.7 copy-start.10
  442.5 1.2 copy-start.12
  442.5 1.2 copy-start.17
  442.5 1.2 copy-start.19
  443.8 1.0 copy-start.4
  445.4 1.3 copy-start.2
  445.4 1.6 copy-start.34
  447.8 1.8 copy-start.37
  447.8 1.8 copy-start.39
  452.2 1.9 copy-start.8
  452.3 1.9 copy-start.30
  452.3 1.9 copy-start.36
  454.2 3.7 copy-start.24
  454.2 3.7 copy-start.27
  457.9 1.9 copy-start.31
  459.8 3.6 copy-start.22
  459.8 4.9 copy-start.40
  593.9 5.4 copy-start.11
  599.3 8.2 %copy-start.20 = (f32[64,1024]{1,0:T(8,128)S(1)}, f32[64,1024]{1,0:T(8,128)}, u32[]{:S(2)}) copy-start(f32[64,1024]{1,0:T(8,128)} %get-tuple-element.126) | copy-start | bytes 786436
  602.0 15.1 %slice-start.2 = ((s8[5767168]{0:T(1024)(128)(4,1)}), s8[4194304]{0:T(1024)(128)(4,1)S(1)}, s32[]{:S(2)}) async-start(s8[5767168]{0:T(1024)(128)(4,1)} %bitcast.98), calls=%async_computation.4 | async-start | bytes 8388608
  605.3 7.2 %copy-start.14 = (f32[704,256]{1,0:T(8,128)S(1)}, f32[704,256]{1,0:T(8,128)}, u32[]{:S(2)}) copy-start(f32[704,256]{1,0:T(8,128)} %get-tuple-element.63) | copy-start | bytes 2162692
  605.3 8.0 %copy-start.13 = (f32[704,256]{1,0:T(8,128)S(1)}, f32[704,256]{1,0:T(8,128)}, u32[]{:S(2)}) copy-start(f32[704,256]{1,0:T(8,128)} %get-tuple-element.131) | copy-start | bytes 2162692
  607.5 6.7 %copy-start.3 = (f32[704,2048]{1,0:T(8,128)S(1)}, f32[704,2048]{1,0:T(8,128)}, u32[]{:S(2)}) copy-start(f32[704,2048]{1,0:T(8,128)} %get-tuple-element.65) | copy-start | bytes 17301508
  613.3 3.8 slice-start.3
  614.2 5.9 slice-start
  617.1 4.0 slice-start.1
Sparse Core Ops, SparseCore 0:
  12.4 175.1 all-gather.2
  463.5 23.8 all-gather.4

commit v5 on v3

--- a/solution.py
+++ b/solution.py
@@ -330,7 +330,7 @@
     me, mine, core = place.me, place.mine, place.core
     length = rows_buf.shape[1]
     width = rows_buf.shape[2]
-    half = width // 2
+    half = width * 3 // 4
     part_rows = length // tensors
     row_block = min(256, length)
 
@@ -383,7 +383,9 @@
         sequence = place.expert_of(layer_shift, lane_shift)
         if columns is None:
             return rows_ref.at[sequence, rows, :]
-        return rows_ref.at[sequence, rows, pl.ds(columns * half, half)]
+        return rows_ref.at[
+            sequence, rows, pl.ds(0, half) if columns == 0 else pl.ds(half, width - half)
+        ]
 
     def await_bytes(view, sem):
         pltpu.make_async_copy(view, view, sem).wait()

time: 631 us -> 632 us (level)
  no operation moved by 1% of the time
where the time goes in v5:
time: 632 us; the launch traced here: 627 us
  Pallas kernels  509 us (81%)
  local copies, waits for them, and re-layouts  45.3 us (7%)
  matrix products  41 us (6%)
  other arithmetic  16.2 us (3%)
  between operations  14.9 us (2%)
    pallas_call x1, Pallas kernels, run_backward(): pl.pallas_call(functools.partial(backward_kernel, groups=groups, tensors=...  214 us
    pallas_call x1, Pallas kernels, run_forward(): pl.pallas_call(functools.partial(forward_kernel, groups=groups, tensors=t...  169 us
    pallas_call x1, Pallas kernels, run_weights(): pl.pallas_call(functools.partial(weight_kernel, groups=groups, tensors=te...  126 us
    unnamed x103, local copies, waits for them, and re-layouts  29.5 us
    dot_general x5, matrix products, lead_dot(): lax.dot_general(left_side, right_side, (((0,), (0,)), ((), ())), preferre...  14.2 us
  transfers between devices with their start and end apart: 2, of which 0 were waited for; matrix products, arithmetic and copies ran while one was open for 7% of the time, Pallas kernels for 47%

profile of v5, /device:TPU:0, one launch (start us, length us, event | category | flops | bytes accessed | tf_op | source)
XLA Modules:
  0.0 627.0 jit_solution(105932020377026993)
XLA Ops:
  7.2 0.9 compare_select_fusion
  8.6 1.0 fusion.50
  9.8 1.1 constant_dynamic-slice_fusion.1
  11.4 0.8 pad_maximum_fusion.7
  12.3 2.2 fusion.1
  14.6 3.4 fusion.47
  18.1 0.9 copy-done.1
  19.0 1.8 convolution_convert_fusion.4
  20.8 2.5 copy.64
  23.3 1.9 slice.162
  25.2 3.5 fusion.45
  28.8 1.1 copy-done.15
  29.9 0.9 slice.222
  30.7 1.0 copy.51
  31.7 1.9 pad.24.router_ref
  33.7 1.2 multiply_cosine_fusion
  35.0 1.1 subtract_convert_fusion.1
  36.1 2.1 fusion.13
  38.4 1.9 constant_dynamic-slice_fusion.inputs_ref
  40.3 2.1 fusion.51
  42.5 0.5 convolution_convert_fusion.7
  42.9 1.7 copy-done.5
  44.6 1.1 copy-done.32
  45.7 2.6 convolution_convert_fusion.2
  48.3 169.2 %experts_forward.1 = (bf16[8,512,2048]{2,1,0:T(8,128)(2,1)}, bf16[4,8,512,704]{3,2,1,0:T(8,128)(2,1)}, f32[8,512,128]{2,1,0:T(8,128)}, f32[128,2048]{1,0:T(8,128)}) custom-call(bf16[2,2,128,2048]{3,2,1,0:T(8,128)(2,1)} %bitcast.158, bf16[512,2048]{1,0:T(8,128)(2,1)} %inputs_ref.1, f32[1,2048]{1,0:T(1,128)} %bitcast.144, bf16[704,2048]{1,0:T(8,128)(2,1)} %bitcast.135, ...), custom_call_target="tpu_custom_call" | custom-call | flops 47244640256 | bytes 100000000 | tf_op jit(solution)/shard_map/experts_forward/pallas_call | solution.py:1170
  217.5 214.3 %experts_backward.1 = (bf16[8,512,704]{2,1,0:T(8,128)(2,1)}, bf16[8,512,704]{2,1,0:T(8,128)(2,1)}, bf16[8,512,704]{2,1,0:T(8,128)(2,1)}, bf16[8,512,704]{2,1,0:T...) custom-call(bf16[8,512,2176]{2,1,0:T(8,128)(2,1)} %bitcast.134, ...), custom_call_target="tpu_custom_call" | custom-call | flops 59055800320 | bytes 100000000 | tf_op jit(solution)/shard_map/experts_backward/pallas_call | solution.py:1249
  431.9 3.7 convolution_convert_fusion.5
  435.6 0.8 multiply_reduce_fusion
  436.4 0.8 fusion.8
  437.2 1.2 multiply_convert_fusion
  438.5 0.8 multiply_bitcast_fusion
  439.5 0.6 multiply_bitcast_fusion.1
  440.3 1.0 copy-done.2
  441.7 0.9 multiply_reduce_fusion.2
  442.5 1.8 convolution_convert_fusion.3
  444.3 2.6 convolution_convert_fusion.1.out_ref
  447.0 1.8 fusion.52
  448.9 3.7 convolution_convert_fusion
  452.6 0.3 fusion.32
  453.1 0.9 pad_maximum_fusion.6
  454.0 0.5 copy-done.31
  454.5 3.5 add_convert_fusion.1
  458.1 1.3 fusion.14
  459.4 4.9 add_convert_fusion
  464.3 125.9 %weights.1 = (f32[256,768]{1,0:T(8,128)}, f32[64,1024]{1,0:T(8,128)}, f32[512,256]{1,0:T(8,128)}, bf16[4,176,256]{2,1,0:T(8,128)(2,1)}, bf16[4,128,2048]{2,1,0:T...) custom-call(bf16[8,256,768]{2,1,0:T(8,128)(2,1)} %bitcast.153, ...), custom_call_target="tpu_custom_call" | custom-call | flops 41339060224 | bytes 100000000 | tf_op jit(solution)/shard_map/weights/pallas_call | solution.py:1751
  590.3 1.2 slice.173
  591.4 1.0 convert_element_type.110
  592.5 0.6 slice.174
  593.0 0.6 slice_reduce_fusion.1
  593.6 0.5 slice_bitcast_fusion.2
  594.1 0.6 slice_bitcast_fusion.1
  594.7 0.9 slice_bitcast_fusion
  595.6 2.7 bitcast_convert_fusion
  598.3 3.3 copy.76
  601.6 2.2 copy.77
  603.8 0.7 copy.78
  604.5 2.3 copy.79
  606.7 2.0 copy.80
  608.8 0.9 copy.81
  609.6 0.9 copy.82
  610.5 2.9 copy.83
  613.4 2.9 copy.84
  616.3 1.1 slice-done.1
  617.4 2.5 copy.85
  (123 shorter events, 3.0 us)
Async XLA Ops:
  7.2 18.0 %copy-start = (bf16[2048,768]{1,0:T(8,128)(2,1)S(1)}, bf16[2048,768]{1,0:T(8,128)(2,1)}, u32[]{:S(2)}) copy-start(bf16[2048,768]{1,0:T(8,128)(2,1)} %param.27) | copy-start | bytes 9437188
  7.2 210.3 %all-gather.3.cloned.1.call-start = ((), (), s32[]{:S(2)}) async-start(), calls=%async_computation | async-start | bytes 18382848 | tf_op jit(solution)/shard_map/all_gather | solution.py:92
  10.9 3.6 copy-start.35
  12.3 586.0 %all-gather.5.cloned.1.call-start = ((), (), s32[]{:S(2)}) async-start(), calls=%async_computation.1 | async-start | bytes 2621440 | tf_op jit(solution)/shard_map/all_gather | solution.py:1947
  12.3 2.3 copy-start.7
  14.6 10.6 %copy-start.29 = (f32[512]{0:T(512)}, f32[512]{0:T(512)S(1)}, u32[]{:S(2)}) copy-start(f32[512]{0:T(512)S(1)} %add_rsqrt_fusion.1) | copy-start | bytes 6148
  14.6 4.4 copy-start.25
  14.6 4.4 copy-start.33
  18.0 1.0 copy-start.1
  25.2 5.6 copy-start.21
  28.7 1.1 copy-start.15
  28.7 5.0 copy-start.28
  33.7 4.5 copy-start.26
  33.7 1.2 copy-start.23
  36.1 2.1 copy-start.16
  36.1 2.1 copy-start.18
  40.3 2.2 copy-start.9
  42.4 2.2 copy-start.5
  42.5 3.2 copy-start.32
  44.6 3.7 copy-start.38
  431.9 3.7 copy-start.6
  431.9 3.7 copy-start.10
  437.2 1.2 copy-start.12
  437.2 1.2 copy-start.17
  437.2 1.2 copy-start.19
  438.4 1.0 copy-start.4
  440.1 1.3 copy-start.2
  440.1 1.6 copy-start.34
  442.5 1.8 copy-start.37
  442.5 1.8 copy-start.39
  446.9 1.9 copy-start.8
  446.9 1.9 copy-start.30
  447.0 1.9 copy-start.36
  448.9 3.7 copy-start.24
  448.9 3.7 copy-start.27
  452.6 1.9 copy-start.31
  454.5 3.6 copy-start.22
  454.5 4.9 copy-start.40
  590.2 5.4 copy-start.11
  595.6 8.2 %copy-start.20 = (f32[64,1024]{1,0:T(8,128)S(1)}, f32[64,1024]{1,0:T(8,128)}, u32[]{:S(2)}) copy-start(f32[64,1024]{1,0:T(8,128)} %get-tuple-element.126) | copy-start | bytes 786436
  598.3 15.1 %slice-start.2 = ((s8[5767168]{0:T(1024)(128)(4,1)}), s8[4194304]{0:T(1024)(128)(4,1)S(1)}, s32[]{:S(2)}) async-start(s8[5767168]{0:T(1024)(128)(4,1)} %bitcast.98), calls=%async_computation.4 | async-start | bytes 8388608
  601.6 7.2 %copy-start.14 = (f32[704,256]{1,0:T(8,128)S(1)}, f32[704,256]{1,0:T(8,128)}, u32[]{:S(2)}) copy-start(f32[704,256]{1,0:T(8,128)} %get-tuple-element.63) | copy-start | bytes 2162692
  601.6 8.0 %copy-start.13 = (f32[704,256]{1,0:T(8,128)S(1)}, f32[704,256]{1,0:T(8,128)}, u32[]{:S(2)}) copy-start(f32[704,256]{1,0:T(8,128)} %get-tuple-element.131) | copy-start | bytes 2162692
  603.8 6.7 %copy-start.3 = (f32[704,2048]{1,0:T(8,128)S(1)}, f32[704,2048]{1,0:T(8,128)}, u32[]{:S(2)}) copy-start(f32[704,2048]{1,0:T(8,128)} %get-tuple-element.65) | copy-start | bytes 17301508
  609.6 3.8 slice-start.3
  610.5 5.9 slice-start
  613.4 4.0 slice-start.1
Sparse Core Ops, SparseCore 0:
  12.4 178.4 all-gather.2
  458.2 25.4 all-gather.4
